TPU v7x, 768 devices: a whole 4x8x12 slice. The times are simulated.
768 devices in a mesh: wave: 48 (over z, x_lo, core), lev: 16 (over x_hi, y).
Axes of the slice: x: 4 (x_hi: 2, x_lo: 2; x = x_hi * 2 + x_lo), y: 8, z: 12, core: 2. Of those that a mesh axis runs over, the one named last changes fastest.
Arguments:
- spectral: bfloat16 [1536, 2, 32, 1536], P('wave', None, 'lev'), may hold values from -6 to 6
- wave_ids: int32 [1536], replicated, may hold values from 0 to 1535, as said below
- lat_rows: int32 [384], replicated, may hold values from 1 to 1152, as said below
- shift_rows: int32 [2, 96, 80], P(None, 'wave', 'lev'), may hold values from -4 to 4, as said below
- shift_cols: int32 [2, 96, 80], P(None, 'wave', 'lev'), may hold values from -4 to 4, as said below
- frac_rows: float32 [2, 96, 80], P(None, 'wave', 'lev'), may hold values from 0 to 1
- frac_cols: float32 [2, 96, 80], P(None, 'wave', 'lev'), may hold values from 0 to 1
- phys_weight: bfloat16 [32, 32], replicated, may hold values from -1 to 1
- phys_bias: float32 [32], replicated, may hold values from -4 to 4
Outputs:
- advected: bfloat16 [32, 384, 10240], P(None, 'wave', 'lev')
Inputs may be any that keep to these rules, and one draw needn't show every extreme that they name: wave_ids: a permutation of the wavenumbers; slot r lies on the wave device of index r // 32. lat_rows: strictly increasing; row j lies at colatitude pi * lat_rows[j] / 1536, so the window covers colatitudes up to some 135 degrees. shift_rows: both the smallest and the largest value occur in every draw. shift_cols: both the smallest and the largest value occur in every draw.
All inputs are finite; a program needn't handle non-finite values.
Results may differ from a plain program's by a relative error of at most 0.005.
Values may be sent and summed in bfloat16 or wider, within the bound.
No kernel may reach another device: no remote copies, remote signals or barrier semaphores. Data moves between devices by JAX's collectives and lax.ppermute only.
A program may use at most 32 MiB of HBM per device.

v0:
```python
import math

import jax
import jax.numpy as jnp
from jax import lax
from jax.sharding import PartitionSpec as P

BLOCK_ROWS = 4
BLOCK_COLS = 128
RIM_WIDTH = 6


def with_halo(array, sides, width, wrap):
    for axis, dim in sides:
        size, length = (lax.axis_size(axis), array.shape[dim])
        up = [(i, (i + 1) % size) for i in range(size if wrap else size - 1)]
        down = [(j, i) for i, j in up]
        last = lax.slice_in_dim(array, length - width, length, axis=dim)
        first = lax.slice_in_dim(array, 0, width, axis=dim)
        before = lax.ppermute(last, axis, up)
        after = lax.ppermute(first, axis, down)
        array = jnp.concatenate([before, array, after], axis=dim)
    return array


def angle_pair(first_ints, second_ints, period):
    product = first_ints[:, None] * second_ints[None, :] % period
    angles = product.astype(jnp.float32) * (2.0 * math.pi / period)
    return (jnp.cos(angles), jnp.sin(angles))


def meridional(k_values, lat_rows, period):
    cos_k, sin_k = angle_pair(k_values, lat_rows, period)
    return jnp.concatenate([cos_k, sin_k], axis=1).astype(jnp.bfloat16)


def cubic_weights(fraction):
    coord = 1.0 - fraction
    return (
        -coord * (coord - 1.0) * (coord - 2.0) / 6.0,
        (coord + 1.0) * (coord - 1.0) * (coord - 2.0) / 2.0,
        -(coord + 1.0) * coord * (coord - 2.0) / 2.0,
        (coord + 1.0) * coord * (coord - 1.0) / 6.0,
    )


def interpolate(window, row_frac, col_frac):
    window = window.astype(jnp.float32)
    row_weights = cubic_weights(row_frac)
    col_weights = cubic_weights(col_frac)
    along = row_weights[0] * window[:, 0:BLOCK_ROWS]
    along = along + row_weights[1] * window[:, 1 : BLOCK_ROWS + 1]
    along = along + row_weights[2] * window[:, 2 : BLOCK_ROWS + 2]
    along = along + row_weights[3] * window[:, 3 : BLOCK_ROWS + 3]
    result = col_weights[0] * along[:, :, 0:BLOCK_COLS]
    result = result + col_weights[1] * along[:, :, 1 : BLOCK_COLS + 1]
    result = result + col_weights[2] * along[:, :, 2 : BLOCK_COLS + 2]
    result = result + col_weights[3] * along[:, :, 3 : BLOCK_COLS + 3]
    return result


def column_physics(departed, phys_weight, phys_bias):
    flat = departed.reshape(departed.shape[0], -1)
    forcing = (
        jnp.dot(phys_weight, flat.astype(jnp.bfloat16), preferred_element_type=jnp.float32)
        + phys_bias[:, None]
    )
    return (flat + jnp.tanh(forcing)).astype(jnp.bfloat16).reshape(departed.shape)


def block_update(
    padded, row_start, col_start, row_move, col_move, row_part, col_part, phys_weight, phys_bias
):
    lead_rows = RIM_WIDTH - 2
    window = lax.dynamic_slice(
        padded,
        (jnp.int32(0), row_start + lead_rows - row_move, col_start + lead_rows - col_move),
        (padded.shape[0], BLOCK_ROWS + 3, BLOCK_COLS + 3),
    )
    return column_physics(interpolate(window, row_part, col_part), phys_weight, phys_bias)


def advance(padded, row_shift, col_shift, row_frac, col_frac, phys_weight, phys_bias):
    row_starts = jnp.arange(row_shift.shape[0], dtype=jnp.int32) * BLOCK_ROWS
    col_starts = jnp.arange(row_shift.shape[1], dtype=jnp.int32) * BLOCK_COLS

    def one_block(row_start, col_start, row_move, col_move, row_part, col_part):
        return block_update(
            padded,
            row_start,
            col_start,
            row_move,
            col_move,
            row_part,
            col_part,
            phys_weight,
            phys_bias,
        )

    inner = jax.vmap(one_block, in_axes=(None, 0, 0, 0, 0, 0))
    outer = jax.vmap(inner, in_axes=(0, None, 0, 0, 0, 0))
    blocks = outer(row_starts, col_starts, row_shift, col_shift, row_frac, col_frac)
    return blocks.transpose(2, 0, 3, 1, 4).reshape(
        padded.shape[0], row_shift.shape[0] * BLOCK_ROWS, row_shift.shape[1] * BLOCK_COLS
    )


def shards(
    spectral,
    wave_ids,
    lat_rows,
    shift_rows,
    shift_cols,
    frac_rows,
    frac_cols,
    phys_weight,
    phys_bias,
):
    slot_count, part_count, fields, wave_count = spectral.shape
    lat_count = lat_rows.shape[0]
    wave_devices = lax.axis_size("wave")
    band_rows = lat_count // wave_devices
    period = 8 * lat_count
    scale_factor = 1.0 / math.sqrt(wave_count)
    first_slot = lax.axis_index("wave") * slot_count
    own_ids = lax.dynamic_slice_in_dim(wave_ids, first_slot, slot_count)
    k_index = jnp.arange(wave_count, dtype=jnp.int32)
    keep_mask = k_index[None, :] < (wave_count - own_ids)[:, None]
    masked = jnp.where(keep_mask[:, None, None, :], spectral, jnp.zeros_like(spectral))
    masked = masked.reshape(slot_count * part_count * fields, wave_count)
    basis_table = meridional(k_index, lat_rows, period)
    projected = jnp.dot(masked, basis_table, preferred_element_type=jnp.float32)
    projected = projected.reshape(slot_count, part_count, fields, 2, lat_count)
    cos_wave, sin_wave = angle_pair(own_ids, lat_rows, period)
    legendre = (
        cos_wave[:, None, None, :] * projected[:, :, :, 0]
        - sin_wave[:, None, None, :] * projected[:, :, :, 1]
    ) * scale_factor
    legendre = legendre.astype(jnp.bfloat16).reshape(
        slot_count, part_count, fields, wave_devices, band_rows
    )
    outgoing = legendre.transpose(3, 0, 1, 2, 4).reshape(wave_devices, -1)
    arrived = lax.all_to_all(outgoing, "wave", split_axis=0, concat_axis=0, tiled=True)
    band_values = arrived.reshape(wave_devices * slot_count, part_count, fields, band_rows)
    lon_count = shift_rows.shape[2] * BLOCK_COLS
    nlon = lon_count * lax.axis_size("lev")
    lon_index = lax.axis_index("lev") * lon_count + jnp.arange(lon_count, dtype=jnp.int32)
    cos_lon, sin_lon = angle_pair(wave_ids, lon_index, nlon)
    own_table = jnp.stack([cos_lon, -sin_lon], axis=1).astype(jnp.bfloat16)
    summed = lax.dot_general(
        lax.all_gather(band_values, "lev", axis=2, tiled=True),
        own_table,
        (((0, 1), (0, 1)), ((), ())),
        preferred_element_type=jnp.float32,
    )
    field_state = (summed * scale_factor).astype(jnp.bfloat16)
    for substep_index in range(shift_rows.shape[0]):
        padded = with_halo(field_state, (("wave", 1),), RIM_WIDTH, False)
        padded = with_halo(padded, (("lev", 2),), RIM_WIDTH, True)
        field_state = advance(
            padded,
            shift_rows[substep_index],
            shift_cols[substep_index],
            frac_rows[substep_index],
            frac_cols[substep_index],
            phys_weight,
            phys_bias,
        )
    return field_state


def solution(mesh):
    return jax.shard_map(
        shards,
        mesh=mesh,
        in_specs=(
            P("wave", None, "lev", None),
            P(),
            P(),
            P(None, "wave", "lev"),
            P(None, "wave", "lev"),
            P(None, "wave", "lev"),
            P(None, "wave", "lev"),
            P(),
            P(),
        ),
        out_specs=P(None, "wave", "lev"),
        check_vma=False,
    )
```

profile of v0, /device:TPU:1, one launch (start us, length us, event | category | flops | bytes accessed | tf_op | source)
XLA Modules:
  0.0 258.4 jit_solution(17506977966589242058)
XLA Ops:
  6.6 11.2 %cosine_convert_fusion.1 = (bf16[1536,384]{0,1:T(8,128)(2,1)S(1)}, bf16[1536,384]{0,1:T(8,128)(2,1)S(1)}) fusion(s32[384]{0:T(512)} %param.11), kind=kLoop, calls=%fused_computation.22 | loop fusion | flops 6488064 | bytes 2360832 | tf_op jit(solution)/shard_map/convert.2
  23.3 29.8 %all_to_all.9 = bf16[48,2,512]{2,1,0:T(2,128)(2,1)S(1)} all-to-all(bf16[48,2,512]{2,1,0:T(2,128)(2,1)S(1)} %reshape.676), channel_id=1, replica_groups=mesh['wave'=48,'lev'=16] {'wave'}, dimensions={0} | all-to-all | bytes 196608 | tf_op jit(solution)/shard_map/all_to_all | solution.py:143
  53.7 1.8 reshape.615
  55.6 3.1 %copy.26 = bf16[1536,2,2,8]{0,3,1,2:T(8,128)(2,1)} copy(bf16[1536,2,2,8]{3,2,1,0:T(2,128)(2,1)S(1)} %reshape.615) | data formatting | bytes 196608 | tf_op jit(solution)/shard_map/reshape | solution.py:144
  58.8 18.1 %cosine_convert_fusion = (bf16[1536,1,640]{2,0,1:T(8,128)(2,1)S(1)}, bf16[1536,1,640]{2,0,1:T(8,128)(2,1)}) fusion(s32[640]{0:T(1024)S(1)} %iota_add_fusion, s32[1536]{0:T(1024)S(1)} %copy-done.2), kind=kLoop, calls=%fused_computation.12 | loop fusion | flops 11796480 | bytes 3940864 | tf_op jit(solution)/shard_map/convert
  76.8 65.4 %all-gather.2.cloned.1.call-done = bf16[1536,2,32,8]{0,3,1,2:T(8,128)(2,1)} async-done(((bf16[1536,2,2,8]{0,3,1,2:T(8,128)(2,1)}), bf16[1536,2,32,8]{0,3,1,2:T(8,128)(2,1)}) %all-gather.2.cloned.1.call-update) | async-done | bytes 1572880 | tf_op jit(solution)/shard_map/all_gather | solution.py:151
  142.2 3.5 %fusion.27 = bf16[32,8,640]{2,1,0:T(8,128)(2,1)S(1)} fusion(bf16[1536,2,32,8]{0,3,1,2:T(8,128)(2,1)} %all-gather.2.cloned.1.call-done, bf16[1536,1,640]{2,0,1:T(8,128)(2,1)} %get-tuple-element.56, bf16[1536,1,640]{2,0,1:T(8,128)(2,1)S(1)} %get-tuple-element.55), kind=kOutput, calls=%fused_computation.51 | convolution fusion | flops 1008926720 | bytes 5832704 | tf_op jit(solution)/shard_map/dot_general | solution.py:150
  145.8 6.1 %collective-permute-start = (bf16[32,6,640]{2,1,0:T(8,128)(2,1)S(1)}, bf16[32,6,640]{2,1,0:T(8,128)(2,1)S(1)}, u32[]{:S(2)}, u32[]{:S(2)}) collective-permute-start(bf16[32,6,640]{2,1,0:T(8,128)(2,1)S(1)} %get-tuple-element.51), channel_id=1, source_target_pairs={{0,16},{16,32},{32,48},{48,64},{64,80},{80,96},{96,112},{112,128},... | collective-permute-start | bytes 737288 | tf_op jit(solution)/shard_map/ppermute | solution.py:20
  151.9 1.9 collective-permute-start.1
  153.9 2.0 collective-permute-done
  155.9 4.4 %collective-permute-done.1 = bf16[32,6,640]{2,1,0:T(8,128)(2,1)S(1)} collective-permute-done((bf16[32,6,640]{2,1,0:T(8,128)(2,1)S(1)}, bf16[32,6,640]{2,1,0:T(8,128)(2,1)S(1)}, u32[]{:S(2)}, u32[]{:S(2)}) %collective-permute-start.1) | collective-permute-done | bytes 245792 | tf_op jit(solution)/shard_map/ppermute | solution.py:21
  160.5 2.9 %collective-permute-start.2 = (bf16[32,20,6]{2,1,0:T(8,128)(2,1)S(1)}, bf16[32,20,6]{2,1,0:T(8,128)(2,1)S(1)}, u32[]{:S(2)}, u32[]{:S(2)}) collective-permute-start(bf16[32,20,6]{2,1,0:T(8,128)(2,1)S(1)} %get-tuple-element.45), channel_id=1, source_target_pairs={{0,1},{1,2},{2,3},{3,4},{4,5},{5,6},{6,7},{7,8},{8,9},{9,10},{10,1... | collective-permute-start | bytes 23048 | tf_op jit(solution)/shard_map/ppermute | solution.py:20
  163.4 6.2 %collective-permute-start.3 = (bf16[32,20,6]{2,1,0:T(8,128)(2,1)S(1)}, bf16[32,20,6]{2,1,0:T(8,128)(2,1)S(1)}, u32[]{:S(2)}, u32[]{:S(2)}) collective-permute-start(bf16[32,20,6]{2,1,0:T(8,128)(2,1)S(1)} %get-tuple-element.46), channel_id=1, source_target_pairs={{1,0},{2,1},{3,2},{4,3},{5,4},{6,5},{7,6},{8,7},{9,8},{10,9},{11,1... | collective-permute-start | bytes 23048 | tf_op jit(solution)/shard_map/ppermute | solution.py:21
  173.4 20.9 %while.2 = (s32[]{:T(128)}, bf16[32,20,652]{2,1,0:T(8,128)(2,1)S(1)}, s32[10,3]{0,1:T(4,128)S(1)}, bf16[10,32,7,131]{3,2,1,0:T(8,128)(2,1)S(1)}, s32[]{:T(128)}) while((s32[]{:T(128)}, bf16[32,20,652]{2,1,0:T(8,128)(2,1)S(1)}, s32[10,3]{0,1:T(4,128)S(1)}, bf16[10,32,7,131]{3,2,1,0:T(8,128)(2,1)S(1)}, s32[]{:T(128)}) %tuple.61), condition=%wide.while_cond, body=%wide.while_body.sunk | while | flops 2 | bytes 262261 | solution.py:75
  198.5 2.9 %collective-permute-start.4 = (bf16[32,6,640]{2,1,0:T(8,128)(2,1)S(1)}, bf16[32,6,640]{2,1,0:T(8,128)(2,1)S(1)}, u32[]{:S(2)}, u32[]{:S(2)}) collective-permute-start(bf16[32,6,640]{2,1,0:T(8,128)(2,1)S(1)} %get-tuple-element.49), channel_id=1, source_target_pairs={{0,16},{16,32},{32,48},{48,64},{64,80},{80,96},{96,112},{112,128},... | collective-permute-start | bytes 737288 | tf_op jit(solution)/shard_map/ppermute | solution.py:20
  201.4 1.9 collective-permute-start.5
  203.3 2.1 collective-permute-done.4
  205.4 5.2 %collective-permute-done.5 = bf16[32,6,640]{2,1,0:T(8,128)(2,1)S(1)} collective-permute-done((bf16[32,6,640]{2,1,0:T(8,128)(2,1)S(1)}, bf16[32,6,640]{2,1,0:T(8,128)(2,1)S(1)}, u32[]{:S(2)}, u32[]{:S(2)}) %collective-permute-start.5) | collective-permute-done | bytes 245792 | tf_op jit(solution)/shard_map/ppermute | solution.py:21
  210.8 1.9 collective-permute-start.6
  212.7 8.3 %collective-permute-start.7 = (bf16[32,20,6]{2,1,0:T(8,128)(2,1)S(1)}, bf16[32,20,6]{2,1,0:T(8,128)(2,1)S(1)}, u32[]{:S(2)}, u32[]{:S(2)}) collective-permute-start(bf16[32,20,6]{2,1,0:T(8,128)(2,1)S(1)} %get-tuple-element.44), channel_id=1, source_target_pairs={{1,0},{2,1},{3,2},{4,3},{5,4},{6,5},{7,6},{8,7},{9,8},{10,9},{11,1... | collective-permute-start | bytes 23048 | tf_op jit(solution)/shard_map/ppermute | solution.py:21
  225.1 21.8 %while.3 = (s32[]{:T(128)}, bf16[32,20,652]{2,1,0:T(8,128)(2,1)S(1)}, s32[10,3]{0,1:T(4,128)S(1)}, bf16[10,32,7,131]{3,2,1,0:T(8,128)(2,1)S(1)}, s32[]{:T(128)}) while((s32[]{:T(128)}, bf16[32,20,652]{2,1,0:T(8,128)(2,1)S(1)}, s32[10,3]{0,1:T(4,128)S(1)}, bf16[10,32,7,131]{3,2,1,0:T(8,128)(2,1)S(1)}, s32[]{:T(128)}) %tuple.64), condition=%wide.while_cond.1, body=%wide.while_body.1.sunk | while | flops 2 | bytes 262261 | solution.py:75
  225.8 1.5 bitcast_dynamic-update-slice_fusion.5
  227.9 1.5 bitcast_dynamic-update-slice_fusion.5
  230.1 1.5 bitcast_dynamic-update-slice_fusion.5
  (133 shorter events, 61.0 us)
Async XLA Ops:
  6.5 190.7 %copy-start = (bf16[32,32]{1,0:T(8,128)(2,1)S(1)}, bf16[32,32]{1,0:T(8,128)(2,1)}, u32[]{:S(2)}) copy-start(bf16[32,32]{1,0:T(8,128)(2,1)} %param.16) | copy-start | bytes 6148
  6.5 11.2 %copy-start.3 = (s32[384]{0:T(512)S(1)}, s32[384]{0:T(512)}, u32[]{:S(2)}) copy-start(s32[384]{0:T(512)} %param.11) | copy-start | bytes 4612
  6.5 11.3 %copy-start.2 = (s32[1536]{0:T(1024)S(1)}, s32[1536]{0:T(1024)}, u32[]{:S(2)}) copy-start(s32[1536]{0:T(1024)} %param.10) | copy-start | bytes 18436
  6.5 11.5 %copy-start.1 = (bf16[32,2,2,1536]{3,2,1,0:T(2,128)(2,1)S(1)}, bf16[32,2,2,1536]{3,2,1,0:T(2,128)(2,1)}, u32[]{:S(2)}) copy-start(bf16[32,2,2,1536]{3,2,1,0:T(2,128)(2,1)} %param.9) | copy-start | bytes 1179652
  6.5 135.7 %all-gather.2.cloned.1.call-start = ((), (), s32[]{:S(2)}) async-start(), calls=%async_computation.1 | async-start | bytes 1671168 | tf_op jit(solution)/shard_map/all_gather | solution.py:151
  53.7 5.0 %copy-start.5 = (f32[2,2,5]{2,1,0:T(2,128)S(1)}, f32[2,2,5]{2,1,0:T(2,128)}, u32[]{:S(2)}) copy-start(f32[2,2,5]{2,1,0:T(2,128)} %param.14) | copy-start | bytes 244
  142.2 11.6 %copy-start.7 = (s32[2,2,5]{2,1,0:T(2,128)S(1)}, s32[2,2,5]{2,1,0:T(2,128)}, u32[]{:S(2)}) copy-start(s32[2,2,5]{2,1,0:T(2,128)} %param.13) | copy-start | bytes 244
  142.2 11.6 %copy-start.8 = (s32[2,2,5]{2,1,0:T(2,128)S(1)}, s32[2,2,5]{2,1,0:T(2,128)}, u32[]{:S(2)}) copy-start(s32[2,2,5]{2,1,0:T(2,128)} %param.12) | copy-start | bytes 244
  142.2 11.7 %copy-start.6 = (f32[2,2,5]{2,1,0:T(2,128)S(1)}, f32[2,2,5]{2,1,0:T(2,128)}, u32[]{:S(2)}) copy-start(f32[2,2,5]{2,1,0:T(2,128)} %param.15) | copy-start | bytes 244
  145.8 10.1 %collective-permute-start = (bf16[32,6,640]{2,1,0:T(8,128)(2,1)S(1)}, bf16[32,6,640]{2,1,0:T(8,128)(2,1)S(1)}, u32[]{:S(2)}, u32[]{:S(2)}) collective-permute-start(bf16[32,6,640]{2,1,0:T(8,128)(2,1)S(1)} %get-tuple-element.51), channel_id=1, source_target_pairs={{0,16},{16,32},{32,48},{48,64},{64,80},{80,96},{96,112},{112,128},... | collective-permute-start | bytes 737288 | tf_op jit(solution)/shard_map/ppermute | solution.py:20
  151.9 8.4 %collective-permute-start.1 = (bf16[32,6,640]{2,1,0:T(8,128)(2,1)S(1)}, bf16[32,6,640]{2,1,0:T(8,128)(2,1)S(1)}, u32[]{:S(2)}, u32[]{:S(2)}) collective-permute-start(bf16[32,6,640]{2,1,0:T(8,128)(2,1)S(1)} %get-tuple-element.52), channel_id=1, source_target_pairs={{16,0},{32,16},{48,32},{64,48},{80,64},{96,80},{112,96},{128,112},... | collective-permute-start | bytes 737288 | tf_op jit(solution)/shard_map/ppermute | solution.py:21
  160.5 10.0 %collective-permute-start.2 = (bf16[32,20,6]{2,1,0:T(8,128)(2,1)S(1)}, bf16[32,20,6]{2,1,0:T(8,128)(2,1)S(1)}, u32[]{:S(2)}, u32[]{:S(2)}) collective-permute-start(bf16[32,20,6]{2,1,0:T(8,128)(2,1)S(1)} %get-tuple-element.45), channel_id=1, source_target_pairs={{0,1},{1,2},{2,3},{3,4},{4,5},{5,6},{6,7},{7,8},{8,9},{9,10},{10,1... | collective-permute-start | bytes 23048 | tf_op jit(solution)/shard_map/ppermute | solution.py:20
  163.4 8.6 %collective-permute-start.3 = (bf16[32,20,6]{2,1,0:T(8,128)(2,1)S(1)}, bf16[32,20,6]{2,1,0:T(8,128)(2,1)S(1)}, u32[]{:S(2)}, u32[]{:S(2)}) collective-permute-start(bf16[32,20,6]{2,1,0:T(8,128)(2,1)S(1)} %get-tuple-element.46), channel_id=1, source_target_pairs={{1,0},{2,1},{3,2},{4,3},{5,4},{6,5},{7,6},{8,7},{9,8},{10,9},{11,1... | collective-permute-start | bytes 23048 | tf_op jit(solution)/shard_map/ppermute | solution.py:21
  195.8 1.4 copy-start.4
  198.5 6.9 %collective-permute-start.4 = (bf16[32,6,640]{2,1,0:T(8,128)(2,1)S(1)}, bf16[32,6,640]{2,1,0:T(8,128)(2,1)S(1)}, u32[]{:S(2)}, u32[]{:S(2)}) collective-permute-start(bf16[32,6,640]{2,1,0:T(8,128)(2,1)S(1)} %get-tuple-element.49), channel_id=1, source_target_pairs={{0,16},{16,32},{32,48},{48,64},{64,80},{80,96},{96,112},{112,128},... | collective-permute-start | bytes 737288 | tf_op jit(solution)/shard_map/ppermute | solution.py:20
  201.4 9.2 %collective-permute-start.5 = (bf16[32,6,640]{2,1,0:T(8,128)(2,1)S(1)}, bf16[32,6,640]{2,1,0:T(8,128)(2,1)S(1)}, u32[]{:S(2)}, u32[]{:S(2)}) collective-permute-start(bf16[32,6,640]{2,1,0:T(8,128)(2,1)S(1)} %get-tuple-element.50), channel_id=1, source_target_pairs={{16,0},{32,16},{48,32},{64,48},{80,64},{96,80},{112,96},{128,112},... | collective-permute-start | bytes 737288 | tf_op jit(solution)/shard_map/ppermute | solution.py:21
  210.8 11.4 %collective-permute-start.6 = (bf16[32,20,6]{2,1,0:T(8,128)(2,1)S(1)}, bf16[32,20,6]{2,1,0:T(8,128)(2,1)S(1)}, u32[]{:S(2)}, u32[]{:S(2)}) collective-permute-start(bf16[32,20,6]{2,1,0:T(8,128)(2,1)S(1)} %get-tuple-element.43), channel_id=1, source_target_pairs={{0,1},{1,2},{2,3},{3,4},{4,5},{5,6},{6,7},{7,8},{8,9},{9,10},{10,1... | collective-permute-start | bytes 23048 | tf_op jit(solution)/shard_map/ppermute | solution.py:20
  212.7 10.9 %collective-permute-start.7 = (bf16[32,20,6]{2,1,0:T(8,128)(2,1)S(1)}, bf16[32,20,6]{2,1,0:T(8,128)(2,1)S(1)}, u32[]{:S(2)}, u32[]{:S(2)}) collective-permute-start(bf16[32,20,6]{2,1,0:T(8,128)(2,1)S(1)} %get-tuple-element.44), channel_id=1, source_target_pairs={{1,0},{2,1},{3,2},{4,3},{5,4},{6,5},{7,6},{8,7},{9,8},{10,9},{11,1... | collective-permute-start | bytes 23048 | tf_op jit(solution)/shard_map/ppermute | solution.py:21
Sparse Core Ops, SparseCore 0:
  58.8 83.3 all-gather.1
where the time goes:
time: 263 us; the launch traced here: 258 us
  waiting for transfers between devices  83.9 us (32%)
  local copies, waits for them, and re-layouts  52.8 us (20%)
  other arithmetic  40.7 us (15%)
  starting transfers between devices  32.2 us (12%)
  blocking collectives  29.8 us (11%)
  between operations  13.9 us (5%)
  matrix products  4.79 us (2%)
    all_gather x1, waiting for transfers between devices, shards(): lax.all_gather(band_values, 'lev', axis=2, tiled=True)  65.4 us
    gather x60, local copies, waits for them, and re-layouts  42.3 us
    all_to_all x1, blocking collectives, shards(): lax.all_to_all(outgoing, 'wave', split_axis=0, concat_axis=0, tiled=True)  29.8 us
    another operation x2, other arithmetic  29.2 us
    ppermute x4, starting transfers between devices, with_halo(): after = lax.ppermute(first, axis, down)  18.4 us
    ppermute x4, starting transfers between devices, with_halo(): before = lax.ppermute(last, axis, up)  13.8 us
    ppermute x4, waiting for transfers between devices, with_halo(): after = lax.ppermute(first, axis, down)  12.6 us
    ppermute x4, waiting for transfers between devices, with_halo(): before = lax.ppermute(last, axis, up)  5.89 us
  transfers between devices with their start and end apart: 9, of which 9 were waited for; matrix products, arithmetic and copies ran while one was open for 7% of the time, Pallas kernels for 0%

commit v1 on v0

v1 whole, which is shorter than its diff:
```python
import functools
import math

import jax
import jax.numpy as jnp
from jax import lax
from jax.experimental import pallas as pl
from jax.experimental.pallas import tpu as pltpu
from jax.sharding import PartitionSpec as P

BLOCK_ROWS = 4
BLOCK_COLS = 128
LANES = 128
ABOVE = 6
BELOW = 5
STAMP_LANE = 32
F32 = jnp.float32
BF16 = jnp.bfloat16
NT = (((1,), (1,)), ((), ()))


def sincos(x, period):
    quarter = period // 4
    turns = jnp.floor(x * (1.0 / quarter) + 0.5)
    t = (x - turns * float(quarter)) * (2.0 * math.pi / period)
    t2 = t * t
    s = t * (1.0 + t2 * (-1.0 / 6.0 + t2 * (1.0 / 120.0 + t2 * (-1.0 / 5040.0))))
    c = 1.0 + t2 * (-0.5 + t2 * (1.0 / 24.0 + t2 * (-1.0 / 720.0 + t2 * (1.0 / 40320.0))))
    k = turns.astype(jnp.int32)
    swap = (k & 1) == 1
    cos, sin = jnp.where(swap, s, c), jnp.where(swap, c, s)
    cos = jnp.where(((k + 1) & 2) != 0, -cos, cos)
    sin = jnp.where((k & 2) != 0, -sin, sin)
    return cos, sin


def rotate(c, s, rc, rs):
    return c * rc - s * rs, s * rc + c * rs


def legendre_kernel(period, scale, x_ref, m_col_ref, m_row_ref, lat_ref, out_ref, cos_ref, sin_ref, cw_ref, sw_ref):
    rows, waves = x_ref.shape
    lats = lat_ref.shape[0]
    step = 32
    lane = lax.broadcasted_iota(jnp.int32, (step, LANES), 1).astype(F32)
    m_row = jnp.broadcast_to(m_row_ref[...], (step, LANES))

    def fill(i, carry):
        at = pl.ds(pl.multiple_of(i * step, step), step)
        lat = jnp.broadcast_to(lat_ref[at, :], (step, LANES))
        cw, sw = sincos(lat * m_row, period)
        cw_ref[at, :] = cw
        sw_ref[at, :] = sw
        c, s = sincos(lat * lane, period)
        rc, rs = sincos(lat * float(LANES), period)
        for a in range(waves // LANES):
            cols = pl.ds(a * LANES, LANES)
            cos_ref[at, cols] = c.astype(BF16)
            sin_ref[at, cols] = s.astype(BF16)
            if a + 1 < waves // LANES:
                c, s = rotate(c, s, rc, rs)
        return carry

    lax.fori_loop(0, lats // step, fill, 0)
    k = lax.broadcasted_iota(jnp.int32, (rows, waves), 1)
    x = jnp.where(k < waves - m_col_ref[...], x_ref[...].astype(F32), 0.0).astype(BF16)
    p0 = lax.dot_general(cos_ref[...], x, NT, preferred_element_type=F32)
    p1 = lax.dot_general(sin_ref[...], x, NT, preferred_element_type=F32)
    leg = ((cw_ref[...] * p0 - sw_ref[...] * p1) * scale).astype(BF16)
    src = lax.broadcasted_iota(jnp.int32, (rows, rows), 0)
    dst = lax.broadcasted_iota(jnp.int32, (rows, rows), 1)
    slots = rows // 4
    order = jnp.where((src % 4) * slots + src // 4 == dst, 1.0, 0.0).astype(BF16)
    out_ref[...] = jnp.dot(leg, order, preferred_element_type=F32).astype(BF16)


def legendre(x, own_ids, lat_rows, period, scale):
    rows, waves = x.shape
    lats = lat_rows.shape[0]
    ids = jnp.repeat(own_ids, 4)
    return pl.pallas_call(
        functools.partial(legendre_kernel, period, scale),
        out_shape=jax.ShapeDtypeStruct((lats, rows), BF16),
        scratch_shapes=[
            pltpu.VMEM((lats, waves), BF16),
            pltpu.VMEM((lats, waves), BF16),
            pltpu.VMEM((lats, LANES), F32),
            pltpu.VMEM((lats, LANES), F32),
        ],
        compiler_params=pltpu.CompilerParams(vmem_limit_bytes=24 << 20),
        name="legendre",
    )(x, ids[:, None], ids[None, :].astype(F32), lat_rows.astype(F32)[:, None])


def times_i(z, power):
    re, im = z
    return ((re, im), (-im, re), (-re, -im), (im, -re))[power % 4]


def add(*terms):
    re, im = terms[0]
    for r, i in terms[1:]:
        re, im = re + r, im + i
    return re, im


def four(z):
    a, b = add(z[0], z[2]), add(z[0], times_i(z[2], 2))
    c, d = add(z[1], z[3]), add(z[1], times_i(z[3], 2))
    return add(a, c), add(b, times_i(d, 1)), add(a, times_i(c, 2)), add(b, times_i(d, 3))


def sixteen_real(y):
    inner = [four([y[4 * q1 + q0] for q1 in range(4)]) for q0 in range(4)]
    out = [None] * 16
    for a0 in range(4):
        v = []
        for q0 in range(4):
            re, im = inner[q0][a0]
            if q0 * a0:
                angle = 2.0 * math.pi * q0 * a0 / 16.0
                cos, sin = math.cos(angle), math.sin(angle)
                re, im = re * cos - im * sin, re * sin + im * cos
            v.append((re, im))
        even, odd = v[0][0] + v[2][0], v[0][0] - v[2][0]
        plus, minus = v[1][0] + v[3][0], v[3][1] - v[1][1]
        out[a0], out[a0 + 8] = even + plus, even - plus
        out[a0 + 4], out[a0 + 12] = odd + minus, odd - minus
    return out


def fourier_kernel(nlon, scale, z_ref, m_ref, stamp_ref, out_ref, e_ref, l_ref, d_ref):
    waves = m_ref.shape[1]
    chunks = waves // LANES
    spans = e_ref.shape[0] // 64
    sub = lax.broadcasted_iota(jnp.int32, (8, LANES), 0).astype(F32)

    def table(i, carry):
        at = pl.ds(pl.multiple_of(i * LANES, LANES), LANES)
        at_sin = pl.ds(pl.multiple_of(waves + i * LANES, LANES), LANES)
        m = jnp.broadcast_to(m_ref[:, at], (8, LANES))
        c, s = sincos(m * sub, nlon)
        c8, s8 = sincos(m * 8.0, nlon)
        c64, s64 = sincos(m * 64.0, nlon)
        z = [(c, s)]
        for _ in range(7):
            z.append(rotate(*z[-1], c8, s8))
        start = z
        for t in range(spans):
            if t == spans - 1:
                z = [rotate(a, b, c64, -s64) for a, b in start]
            for h in range(4):
                (c0, s0), (c1, s1) = z[2 * h], z[2 * h + 1]
                rows = pl.ds(t * 64 + h * 16, 16)
                e_ref[rows, at] = jnp.concatenate([c0, c1], axis=0).astype(BF16)
                e_ref[rows, at_sin] = jnp.concatenate([s0, s1], axis=0).astype(BF16)
            if t < spans - 2:
                z = [rotate(a, b, c64, s64) for a, b in z]
        return carry

    lax.fori_loop(0, chunks, table, 0)
    group = lax.broadcasted_iota(jnp.int32, (8, LANES), 1) // 32

    def spread(i, carry):
        at = pl.ds(pl.multiple_of(i * LANES, LANES), LANES)
        at_sin = pl.ds(pl.multiple_of(waves + i * LANES, LANES), LANES)
        block = [z_ref[4 * i + u].astype(F32) for u in range(4)]
        parts = []
        for cf in range(4):
            whole = None
            for u in range(4):
                turn = (32 * (u - cf)) % LANES
                moved = pltpu.roll(block[u], turn, 1) if turn else block[u]
                whole = moved if whole is None else jnp.where(group == u, moved, whole)
            parts.append(whole)
        real = jnp.concatenate(parts[0:2], axis=0)
        imag = jnp.concatenate(parts[2:4], axis=0)
        m = jnp.broadcast_to(m_ref[:, at], (16, LANES))
        residue = m - 16.0 * jnp.floor(m * 0.0625)
        for q in range(16):
            keep = residue == float(q)
            re = jnp.where(keep, real, 0.0)
            im = jnp.where(keep, imag, 0.0)
            top, low = pl.ds(q * 32, 16), pl.ds(q * 32 + 16, 16)
            re16, im16 = re.astype(BF16), im.astype(BF16)
            l_ref[top, at] = re16
            l_ref[low, at] = im16
            l_ref[top, at_sin] = (-im).astype(BF16)
            l_ref[low, at_sin] = re16
        return carry

    lax.fori_loop(0, chunks, spread, 0)
    lane = lax.broadcasted_iota(jnp.int32, (16, LANES), 1)
    unused = (lane >= STAMP_LANE) & (lane < LANES - STAMP_LANE)
    stamp = jnp.broadcast_to(stamp_ref[...], (16, LANES))
    tiles = e_ref.shape[0] // LANES
    for pair in range(tiles // 2):
        d_ref[...] = lax.dot_general(
            l_ref[...], e_ref[pl.ds(pair * 256, 256), :], NT, preferred_element_type=F32
        )
        for h in range(2):
            t = 2 * pair + h
            cols = pl.ds(h * LANES, LANES)
            y = [(d_ref[pl.ds(q * 32, 16), cols], d_ref[pl.ds(q * 32 + 16, 16), cols]) for q in range(16)]
            g = sixteen_real(y)
            for a in range(16):
                value = g[a] * scale
                if t == tiles - 1:
                    value = jnp.where(unused, stamp, value)
                out_ref[a, pl.ds(t * 16, 16), :] = value.astype(BF16)


def fourier(z, wave_ids, stamp, nlon, scale):
    waves = wave_ids.shape[0]
    tiles = 6
    return pl.pallas_call(
        functools.partial(fourier_kernel, nlon, scale),
        out_shape=jax.ShapeDtypeStruct((16, tiles * 16, LANES), BF16),
        scratch_shapes=[
            pltpu.VMEM((tiles * LANES, 2 * waves), BF16),
            pltpu.VMEM((512, 2 * waves), BF16),
            pltpu.VMEM((512, 256), F32),
        ],
        compiler_params=pltpu.CompilerParams(vmem_limit_bytes=24 << 20),
        name="fourier",
    )(z, wave_ids.astype(F32)[None, :], stamp)


def regroup_kernel(x_ref, out_ref, wide_ref):
    rows, tiles = out_ref.shape[:2]
    sources = x_ref.shape[0]
    span = x_ref.shape[1]
    for v in range(sources):
        wide_ref[pl.ds(v * span, span), :] = x_ref[v].astype(F32)
    for j in range(rows):
        for t in range(tiles):
            for f in range(2):
                got = wide_ref[pl.ds(t * 16 + f * 8 + j, sources, stride=span), :]
                out_ref[j, t, pl.ds(f * sources, sources), :] = got.astype(BF16)


def regroup(x):
    return pl.pallas_call(
        regroup_kernel,
        out_shape=jax.ShapeDtypeStruct((8, x.shape[1] // 16, 32, LANES), BF16),
        scratch_shapes=[pltpu.VMEM((x.shape[0] * x.shape[1], LANES), F32)],
        compiler_params=pltpu.CompilerParams(vmem_limit_bytes=8 << 20),
        name="regroup",
    )(x)


def advance_kernel(last, move_ref, weight_ref, before_ref, now_ref, after_ref, phys_ref, bias_ref, out_ref, s_ref, *rest):
    rows, tiles, fields = now_ref.shape[:3]
    s_ref[pl.ds(0, ABOVE)] = before_ref[...]
    s_ref[pl.ds(ABOVE, rows)] = now_ref[...]
    s_ref[pl.ds(ABOVE + rows, BELOW)] = after_ref[...]
    lane = lax.broadcasted_iota(jnp.int32, (fields, LANES), 1)
    left_half = lane < LANES // 2
    phys = phys_ref[...]
    bias = jnp.broadcast_to(bias_ref[...], (fields, LANES))

    def departed(band, block, tile):
        where = band * 7 + block
        base = ABOVE - 2 + band * BLOCK_ROWS - move_ref[2 * where]
        first = -move_ref[2 * where + 1] - 2
        wr = [weight_ref[8 * where + a] for a in range(4)]
        wc = [weight_ref[8 * where + 4 + a] for a in range(4)]
        centre, edge = [], []
        for k in range(BLOCK_ROWS + 3):
            before = s_ref[base + k, (tile + tiles - 1) % tiles].astype(F32)
            after = s_ref[base + k, (tile + 1) % tiles].astype(F32)
            centre.append(s_ref[base + k, tile].astype(F32))
            edge.append(jnp.where(left_half, after, before))
        taps = []
        for b in range(4):
            shift = first + b
            outside = (lane < shift) | (lane >= LANES + shift)
            taps.append((outside, (LANES - shift) & (LANES - 1)))
        result = []
        for i in range(BLOCK_ROWS):
            c = sum(wr[a] * centre[i + a] for a in range(4))
            e = sum(wr[a] * edge[i + a] for a in range(4))
            total = None
            for b in range(4):
                outside, turn = taps[b]
                term = wc[b] * pltpu.roll(jnp.where(outside, e, c), turn, 1)
                total = term if total is None else total + term
            result.append(total)
        return result

    def one_band(band, carry):
        for tile in range(5 if last else 6):
            if tile < 5:
                dep = departed(band, tile + 1, tile)
            else:
                right = departed(band, 6, tile)
                left = departed(band, 0, tile)
                dep = [jnp.where(left_half, r, l) for r, l in zip(right, left)]
            low = jnp.concatenate(dep, axis=1).astype(BF16)
            forcing = jnp.dot(phys, low, preferred_element_type=F32)
            for i in range(BLOCK_ROWS):
                push = forcing[:, i * LANES : (i + 1) * LANES] + bias
                value = dep[i] + jnp.tanh(push)
                row = band * BLOCK_ROWS + i
                if last:
                    at = pl.ds(pl.multiple_of((row * 5 + tile) * fields, fields), fields)
                    rest[0][at, :] = value
                else:
                    out_ref[row, tile] = value.astype(BF16)
        return carry

    lax.fori_loop(0, rows // BLOCK_ROWS, one_band, 0)
    if last:
        for f in range(fields):
            kept = (f % 2) * (fields // 2) + f // 2
            for t in range(5):
                got = rest[0][pl.ds(t * fields + kept, rows, stride=5 * fields), :]
                out_ref[f, :, pl.ds(t * LANES, LANES)] = got.astype(BF16)


def advance(last, moves, weights, before, now, after, phys, bias):
    rows, tiles, fields = now.shape[:3]
    smem, vmem = pl.BlockSpec(memory_space=pltpu.SMEM), pl.BlockSpec(memory_space=pltpu.VMEM)
    scratch = [pltpu.VMEM((ABOVE + rows + BELOW, tiles, fields, LANES), BF16)]
    if last:
        shape = (fields, rows, 5 * LANES)
        scratch.append(pltpu.VMEM((rows * 5 * fields, LANES), F32))
    else:
        shape = (rows, tiles, fields, LANES)
    return pl.pallas_call(
        functools.partial(advance_kernel, last),
        out_shape=jax.ShapeDtypeStruct(shape, BF16),
        in_specs=[smem, smem] + [vmem] * 5,
        scratch_shapes=scratch,
        compiler_params=pltpu.CompilerParams(vmem_limit_bytes=16 << 20),
        name="advance_last" if last else "advance_first",
    )(moves, weights, before, now, after, phys, bias)


def cubic_weights(fraction):
    coord = 1.0 - fraction
    return (
        -coord * (coord - 1.0) * (coord - 2.0) / 6.0,
        (coord + 1.0) * (coord - 1.0) * (coord - 2.0) / 2.0,
        -(coord + 1.0) * coord * (coord - 2.0) / 2.0,
        (coord + 1.0) * coord * (coord - 1.0) / 6.0,
    )


def three_parts(value):
    high = lax.reduce_precision(value, 8, 7)
    mid = lax.reduce_precision(value - high, 8, 7)
    return high, mid, value - high - mid


def edge_stamp(shift_rows, shift_cols, frac_rows, frac_cols):
    pieces = [shift_rows.astype(F32), shift_cols.astype(F32), *three_parts(frac_rows), *three_parts(frac_cols)]
    table = jnp.stack(pieces, axis=0)
    edges = jnp.concatenate([table[:, :, :1], table[:, :, -1:]], axis=2)
    flat = edges.reshape(1, -1)
    return jnp.pad(flat, ((0, 0), (STAMP_LANE, LANES - STAMP_LANE - flat.shape[1])))


def read_stamp(lanes, side):
    table = lanes.astype(F32).reshape(8, 2, 2)[:, :, side : side + 1]
    return table[0], table[1], table[2] + table[3] + table[4], table[5] + table[6] + table[7]


def block_tables(shift_rows, shift_cols, frac_rows, frac_cols):
    moves = jnp.stack([shift_rows, shift_cols], axis=-1).astype(jnp.int32).reshape(-1)
    weights = jnp.stack(cubic_weights(frac_rows) + cubic_weights(frac_cols), axis=-1).reshape(-1)
    return moves, weights


def row_halos(state):
    size = lax.axis_size("wave")
    rows = state.shape[0]
    before = lax.ppermute(state[rows - ABOVE :], "wave", [(i, i + 1) for i in range(size - 1)])
    after = lax.ppermute(state[:BELOW], "wave", [(i + 1, i) for i in range(size - 1)])
    return before, after


def shards(spectral, wave_ids, lat_rows, shift_rows, shift_cols, frac_rows, frac_cols, phys_weight, phys_bias):
    slots, parts, fields, waves = spectral.shape
    lats = lat_rows.shape[0]
    bands, owners = lax.axis_size("wave"), lax.axis_size("lev")
    nlon = shift_rows.shape[2] * BLOCK_COLS * owners
    scale = 1.0 / math.sqrt(waves)
    own_ids = lax.dynamic_slice_in_dim(wave_ids, lax.axis_index("wave") * slots, slots)
    outgoing = legendre(spectral.reshape(slots * parts * fields, waves), own_ids, lat_rows, 8 * lats, scale)
    outgoing = outgoing.reshape(bands, lats // bands, slots * parts * fields)
    arrived = lax.all_to_all(outgoing, "wave", split_axis=0, concat_axis=0, tiled=True)
    stamp = edge_stamp(shift_rows[0], shift_cols[0], frac_rows[0], frac_cols[0])
    columns = fourier(arrived, wave_ids, stamp, nlon, scale)
    columns = lax.all_to_all(columns, "lev", split_axis=0, concat_axis=0, tiled=True)
    state = regroup(columns)
    before, after = row_halos(state)

    me = lax.axis_index("lev")
    stamp_row = columns.shape[1] - 16
    size = (1, 1, 32)
    west = lax.dynamic_slice(columns, ((me + owners - 1) % owners, stamp_row, STAMP_LANE), size)
    east = lax.dynamic_slice(columns, ((me + 1) % owners, stamp_row, STAMP_LANE), size)
    west, east = read_stamp(west, 1), read_stamp(east, 0)
    own = (shift_rows.astype(F32), shift_cols.astype(F32), frac_rows, frac_cols)
    first = [jnp.concatenate([w, o[0], e], axis=1) for w, o, e in zip(west, own, east)]
    second = [jnp.pad(o[1], ((0, 0), (1, 1))) for o in own]

    split = (owners, fields)
    phys = phys_weight.reshape(split + split).transpose(1, 0, 3, 2).reshape(phys_weight.shape)
    bias = phys_bias.reshape(split).T.reshape(-1, 1)
    state = advance(False, *block_tables(*first), before, state, after, phys, bias)
    before, after = row_halos(state)
    return advance(True, *block_tables(*second), before, state, after, phys, bias)


def solution(mesh):
    blocks = P(None, "wave", "lev")
    return jax.shard_map(
        shards,
        mesh=mesh,
        in_specs=(P("wave", None, "lev", None), P(), P(), blocks, blocks, blocks, blocks, P(), P()),
        out_specs=P(None, "wave", "lev"),
        check_vma=False,
    )
```

time: 263 us -> 92.7 us (0.35); the launches traced: 258 us -> 92.2 us
  waiting for transfers between devices: 83.9 us -> 26.1 us
  local copies, waits for them, and re-layouts: 52.8 us -> 8.28 us
  other arithmetic: 40.7 us -> 1.42 us
  blocking collectives: 29.8 us -> 0 us
  Pallas kernels: 0 us -> 16.4 us
  between operations: 13.9 us -> 0.25 us
  starting transfers between devices: 32.2 us -> 39.7 us
  matrix products: 4.79 us -> 0 us
    all_gather x1 -> x0, waiting for transfers between devices: 65.4 us -> none  [shards(): lax.all_gather(band_values, 'lev', axis=2, tiled=True)]
    gather x60 -> x0, local copies, waits for them, and re-layouts: 42.3 us -> none
    all_to_all x1 -> x0, blocking collectives: 29.8 us -> none  [shards(): lax.all_to_all(outgoing, 'wave', split_axis=0, concat_axis=0, tiled=True)]
    another operation x2 -> x5, other arithmetic: 29.2 us -> 0.26 us  [the longest x2 0.15 us: block_tables(): jnp.stack([shift_rows, shift_cols], axis=-1).astype(jnp.int32).reshape(-1)]
    all_to_all x0 -> x2, starting transfers between devices: none -> 27 us  [the longest x1 17.9 us: shards(): lax.all_to_all(outgoing, 'wave', split_axis=0, concat_axis=0, tiled=True)]
    ppermute x8 -> x4, starting transfers between devices: 32.2 us -> 12.7 us  [the longest x2 6.39 us: row_halos(): lax.ppermute(state[:BELOW], 'wave', [(i + 1, i) for i in range(size - 1)])]
    all_to_all x0 -> x2, waiting for transfers between devices: none -> 19.2 us  [the longest x1 12.4 us: shards(): lax.all_to_all(columns, 'lev', split_axis=0, concat_axis=0, tiled=True)]
    pallas_call x0 -> x5, Pallas kernels: none -> 16.4 us  [the longest x1 7.03 us: fourier(): pl.pallas_call(functools.partial(fourier_kernel, nlon, scale), out_shape=...]
  transfers between devices with their start and end apart: 9 -> 6, of which waited for: 9 -> 6; matrix products, arithmetic and copies ran while one was open for 7% -> 3% of each run, Pallas kernels for 0% -> 0%
where the time goes in v1:
time: 92.7 us; the launch traced here: 92.2 us
  starting transfers between devices  39.7 us (43%)
  waiting for transfers between devices  26.1 us (28%)
  Pallas kernels  16.4 us (18%)
  local copies, waits for them, and re-layouts  8.28 us (9%)
  other arithmetic  1.42 us (2%)
    all_to_all x1, starting transfers between devices, shards(): lax.all_to_all(outgoing, 'wave', split_axis=0, concat_axis=0, tiled=True)  17.9 us
    all_to_all x1, waiting for transfers between devices, shards(): lax.all_to_all(columns, 'lev', split_axis=0, concat_axis=0, tiled=True)  12.4 us
    all_to_all x1, starting transfers between devices, shards(): lax.all_to_all(columns, 'lev', split_axis=0, concat_axis=0, tiled=True)  9.09 us
    pallas_call x1, Pallas kernels, fourier(): pl.pallas_call(functools.partial(fourier_kernel, nlon, scale), out_shape=...  7.03 us
    all_to_all x1, waiting for transfers between devices, shards(): lax.all_to_all(outgoing, 'wave', split_axis=0, concat_axis=0, tiled=True)  6.82 us
    ppermute x2, starting transfers between devices, row_halos(): lax.ppermute(state[:BELOW], 'wave', [(i + 1, i) for i in range(size - 1)])  6.39 us
    ppermute x2, starting transfers between devices, row_halos(): lax.ppermute(state[rows - ABOVE:], 'wave', [(i, i + 1) for i in range(siz...  6.31 us
    pallas_call x2, Pallas kernels, advance(): pl.pallas_call(functools.partial(advance_kernel, last), out_shape=jax.Sha...  5.05 us
  transfers between devices with their start and end apart: 6, of which 6 were waited for; matrix products, arithmetic and copies ran while one was open for 3% of the time, Pallas kernels for 0%

profile of v1, /device:TPU:1, one launch (start us, length us, event | category | flops | bytes accessed | tf_op | source)
XLA Modules:
  0.0 92.2 jit_solution(258844823490541304)
XLA Ops:
  0.0 0.7 copy-done.6
  1.2 1.1 %reshape.903.x_ref = bf16[128,1536]{1,0:T(8,128)(2,1)S(1)} reshape(bf16[32,2,2,1536]{3,2,1,0:T(2,128)(2,1)} %param.9) | data formatting | bytes 786432 | tf_op jit(solution)/shard_map/reshape | solution.py:390
  2.4 3.8 %legendre.1 = bf16[384,128]{1,0:T(8,128)(2,1)} custom-call(bf16[128,1536]{1,0:T(8,128)(2,1)S(1)} %reshape.903.x_ref, s32[128,1]{1,0:T(8,128)S(1)} %broadcast_in_dim_reshape.5.m_col_ref, f32[1,128]{1,0:T(1,128)S(1)} %convert_element_type.53.m_row_ref, f32[384,1]{1,0:T(8,128)S(1)} %broadcast_in_dim.15.lat_ref), custom_call_target="tpu_custom_call" | custom-call | tf_op jit(solution)/shard_map/legendre/pallas_call | solution.py:81
  6.2 17.9 %all-to-all-start = ((bf16[48,8,128]{2,1,0:T(8,128)(2,1)}), bf16[48,8,128]{2,1,0:T(8,128)(2,1)S(1)}, u32[]{:S(2)}, u32[]{:S(2)}) async-start(bf16[48,8,128]{2,1,0:T(8,128)(2,1)} %bitcast.14), calls=%async_computation | async-start | bytes 196608 | tf_op jit(solution)/shard_map/all_to_all | solution.py:392
  24.2 0.7 copy-done.4
  24.9 0.7 copy-done.5
  25.6 0.7 copy-done.7
  26.4 0.7 copy-done.2
  27.1 0.7 copy-done.3
  28.2 0.6 copy-done.1
  29.4 6.8 %all-to-all-done.z_ref = bf16[48,8,128]{2,1,0:T(8,128)(2,1)S(1)} async-done(((bf16[48,8,128]{2,1,0:T(8,128)(2,1)}), bf16[48,8,128]{2,1,0:T(8,128)(2,1)S(1)}, u32[]{:S(2)}, u32[]{:S(2)}) %all-to-all-start) | async-done | bytes 98336 | tf_op jit(solution)/shard_map/all_to_all | solution.py:392
  36.2 7.0 %fourier.1 = bf16[16,96,128]{2,1,0:T(8,128)(2,1)} custom-call(bf16[48,8,128]{2,1,0:T(8,128)(2,1)S(1)} %all-to-all-done.z_ref, f32[1,1536]{1,0:T(1,128)S(1)} %broadcast_in_dim.14.m_ref, f32[1,128]{1,0:T(1,128)S(1)} %pad.21.stamp_ref), custom_call_target="tpu_custom_call" | custom-call | tf_op jit(solution)/shard_map/fourier/pallas_call | solution.py:216
  43.2 9.1 %all-to-all-start.1 = ((bf16[16,96,128]{2,1,0:T(8,128)(2,1)}), bf16[16,96,128]{2,1,0:T(8,128)(2,1)S(1)}, u32[]{:S(2)}, u32[]{:S(2)}) async-start(bf16[16,96,128]{2,1,0:T(8,128)(2,1)} %fourier.1), calls=%async_computation.1 | async-start | bytes 786432 | tf_op jit(solution)/shard_map/all_to_all | solution.py:395
  52.6 12.4 %all-to-all-done.1.x_ref = bf16[16,96,128]{2,1,0:T(8,128)(2,1)S(1)} async-done(((bf16[16,96,128]{2,1,0:T(8,128)(2,1)}), bf16[16,96,128]{2,1,0:T(8,128)(2,1)S(1)}, u32[]{:S(2)}, u32[]{:S(2)}) %all-to-all-start.1) | async-done | bytes 393248 | tf_op jit(solution)/shard_map/all_to_all | solution.py:395
  66.1 4.5 %collective-permute-start.1 = (bf16[5,6,32,128]{3,2,1,0:T(8,128)(2,1)S(1)}, bf16[5,6,32,128]{3,2,1,0:T(8,128)(2,1)S(1)}, u32[]{:S(2)}, u32[]{:S(2)}) collective-permute-start(bf16[5,6,32,128]{3,2,1,0:T(8,128)(2,1)S(1)} %slice.171), channel_id=1, source_target_pairs={{16,0},{32,16},{48,32},{64,48},{80,64},{96,80},{112,96},{128,112},... | collective-permute-start | bytes 737288 | tf_op jit(solution)/shard_map/ppermute | solution.py:379
  70.6 1.9 %collective-permute-start = (bf16[6,6,32,128]{3,2,1,0:T(8,128)(2,1)S(1)}, bf16[6,6,32,128]{3,2,1,0:T(8,128)(2,1)S(1)}, u32[]{:S(2)}, u32[]{:S(2)}) collective-permute-start(bf16[6,6,32,128]{3,2,1,0:T(8,128)(2,1)S(1)} %slice.170), channel_id=1, source_target_pairs={{0,16},{16,32},{32,48},{48,64},{64,80},{80,96},{96,112},{112,128},... | collective-permute-start | bytes 884744 | tf_op jit(solution)/shard_map/ppermute | solution.py:378
  73.2 0.9 collective-permute-done.1.after_ref
  74.1 2.1 %collective-permute-done.before_ref = bf16[6,6,32,128]{3,2,1,0:T(8,128)(2,1)S(1)} collective-permute-done((bf16[6,6,32,128]{3,2,1,0:T(8,128)(2,1)S(1)}, bf16[6,6,32,128]{3,2,1,0:T(8,128)(2,1)S(1)}, u32[]{:S(2)}, u32[]{:S(2)}) %collective-permute-start) | collective-permute-done | bytes 294944 | tf_op jit(solution)/shard_map/ppermute | solution.py:378
  76.2 2.1 %advance_first.1.now_ref = bf16[8,6,32,128]{3,2,1,0:T(8,128)(2,1)S(1)} custom-call(s32[28]{0:T(128)S(1)} %convert_element_type.59.move_ref, f32[112]{0:T(128)S(1)} %reshape.910.weight_ref, bf16[6,6,32,128]{3,2,1,0:T(8,128)(2,1)S(1)} %collective-permute-done.before_ref, bf16[8,6,32,128]{3,2,1,0:T(8,128)(2,1)S(1)} %regroup.1.now_ref, ...), custom_call_target="tpu_custom_call" | custom-call | tf_op jit(solution)/shard_map/advance_first/pallas_call | solution.py:330
  78.4 1.9 %collective-permute-start.3 = (bf16[5,6,32,128]{3,2,1,0:T(8,128)(2,1)S(1)}, bf16[5,6,32,128]{3,2,1,0:T(8,128)(2,1)S(1)}, u32[]{:S(2)}, u32[]{:S(2)}) collective-permute-start(bf16[5,6,32,128]{3,2,1,0:T(8,128)(2,1)S(1)} %slice.173), channel_id=1, source_target_pairs={{16,0},{32,16},{48,32},{64,48},{80,64},{96,80},{112,96},{128,112},... | collective-permute-start | bytes 737288 | tf_op jit(solution)/shard_map/ppermute | solution.py:379
  80.3 4.4 %collective-permute-start.2 = (bf16[6,6,32,128]{3,2,1,0:T(8,128)(2,1)S(1)}, bf16[6,6,32,128]{3,2,1,0:T(8,128)(2,1)S(1)}, u32[]{:S(2)}, u32[]{:S(2)}) collective-permute-start(bf16[6,6,32,128]{3,2,1,0:T(8,128)(2,1)S(1)} %slice.172), channel_id=1, source_target_pairs={{0,16},{16,32},{32,48},{48,64},{64,80},{80,96},{96,112},{112,128},... | collective-permute-start | bytes 884744 | tf_op jit(solution)/shard_map/ppermute | solution.py:378
  85.3 1.3 %collective-permute-done.3.after_ref = bf16[5,6,32,128]{3,2,1,0:T(8,128)(2,1)S(1)} collective-permute-done((bf16[5,6,32,128]{3,2,1,0:T(8,128)(2,1)S(1)}, bf16[5,6,32,128]{3,2,1,0:T(8,128)(2,1)S(1)}, u32[]{:S(2)}, u32[]{:S(2)}) %collective-permute-start.3) | collective-permute-done | bytes 245792 | tf_op jit(solution)/shard_map/ppermute | solution.py:379
  86.6 2.6 %collective-permute-done.2.before_ref = bf16[6,6,32,128]{3,2,1,0:T(8,128)(2,1)S(1)} collective-permute-done((bf16[6,6,32,128]{3,2,1,0:T(8,128)(2,1)S(1)}, bf16[6,6,32,128]{3,2,1,0:T(8,128)(2,1)S(1)}, u32[]{:S(2)}, u32[]{:S(2)}) %collective-permute-start.2) | collective-permute-done | bytes 294944 | tf_op jit(solution)/shard_map/ppermute | solution.py:378
  89.2 2.9 %advance_last.1 = bf16[32,8,640]{2,1,0:T(8,128)(2,1)} custom-call(s32[28]{0:T(128)S(1)} %convert_element_type.51.move_ref, f32[112]{0:T(128)S(1)} %reshape.902.weight_ref, bf16[6,6,32,128]{3,2,1,0:T(8,128)(2,1)S(1)} %collective-permute-done.2.before_ref, bf16[8,6,32,128]{3,2,1,0:T(8,128)(2,1)S(1)} %advance_first.1.now_ref, ...), custom_call_target="tpu_custom_call" | custom-call | tf_op jit(solution)/shard_map/advance_last/pallas_call | solution.py:330
  (77 shorter events, 4.4 us)
Async XLA Ops:
  0.0 0.7 copy-start.6
  0.0 0.7 copy-start
  6.2 30.0 %all-to-all-start = ((bf16[48,8,128]{2,1,0:T(8,128)(2,1)}), bf16[48,8,128]{2,1,0:T(8,128)(2,1)S(1)}, u32[]{:S(2)}, u32[]{:S(2)}) async-start(bf16[48,8,128]{2,1,0:T(8,128)(2,1)} %bitcast.14), calls=%async_computation | async-start | bytes 196608 | tf_op jit(solution)/shard_map/all_to_all | solution.py:392
  24.2 0.7 copy-start.4
  24.9 0.7 copy-start.5
  25.6 0.7 copy-start.7
  26.4 0.7 copy-start.2
  27.1 0.7 copy-start.3
  28.1 0.7 copy-start.1
  43.2 21.7 %all-to-all-start.1 = ((bf16[16,96,128]{2,1,0:T(8,128)(2,1)}), bf16[16,96,128]{2,1,0:T(8,128)(2,1)S(1)}, u32[]{:S(2)}, u32[]{:S(2)}) async-start(bf16[16,96,128]{2,1,0:T(8,128)(2,1)} %fourier.1), calls=%async_computation.1 | async-start | bytes 786432 | tf_op jit(solution)/shard_map/all_to_all | solution.py:395
  66.1 7.9 %collective-permute-start.1 = (bf16[5,6,32,128]{3,2,1,0:T(8,128)(2,1)S(1)}, bf16[5,6,32,128]{3,2,1,0:T(8,128)(2,1)S(1)}, u32[]{:S(2)}, u32[]{:S(2)}) collective-permute-start(bf16[5,6,32,128]{3,2,1,0:T(8,128)(2,1)S(1)} %slice.171), channel_id=1, source_target_pairs={{16,0},{32,16},{48,32},{64,48},{80,64},{96,80},{112,96},{128,112},... | collective-permute-start | bytes 737288 | tf_op jit(solution)/shard_map/ppermute | solution.py:379
  70.6 5.6 %collective-permute-start = (bf16[6,6,32,128]{3,2,1,0:T(8,128)(2,1)S(1)}, bf16[6,6,32,128]{3,2,1,0:T(8,128)(2,1)S(1)}, u32[]{:S(2)}, u32[]{:S(2)}) collective-permute-start(bf16[6,6,32,128]{3,2,1,0:T(8,128)(2,1)S(1)} %slice.170), channel_id=1, source_target_pairs={{0,16},{16,32},{32,48},{48,64},{64,80},{80,96},{96,112},{112,128},... | collective-permute-start | bytes 884744 | tf_op jit(solution)/shard_map/ppermute | solution.py:378
  78.4 8.3 %collective-permute-start.3 = (bf16[5,6,32,128]{3,2,1,0:T(8,128)(2,1)S(1)}, bf16[5,6,32,128]{3,2,1,0:T(8,128)(2,1)S(1)}, u32[]{:S(2)}, u32[]{:S(2)}) collective-permute-start(bf16[5,6,32,128]{3,2,1,0:T(8,128)(2,1)S(1)} %slice.173), channel_id=1, source_target_pairs={{16,0},{32,16},{48,32},{64,48},{80,64},{96,80},{112,96},{128,112},... | collective-permute-start | bytes 737288 | tf_op jit(solution)/shard_map/ppermute | solution.py:379
  80.3 8.9 %collective-permute-start.2 = (bf16[6,6,32,128]{3,2,1,0:T(8,128)(2,1)S(1)}, bf16[6,6,32,128]{3,2,1,0:T(8,128)(2,1)S(1)}, u32[]{:S(2)}, u32[]{:S(2)}) collective-permute-start(bf16[6,6,32,128]{3,2,1,0:T(8,128)(2,1)S(1)} %slice.172), channel_id=1, source_target_pairs={{0,16},{16,32},{32,48},{48,64},{64,80},{80,96},{96,112},{112,128},... | collective-permute-start | bytes 884744 | tf_op jit(solution)/shard_map/ppermute | solution.py:378

commit v2 on v1

--- a/solution.py
+++ b/solution.py
@@ -38,7 +38,7 @@
     return c * rc - s * rs, s * rc + c * rs
 
 
-def legendre_kernel(period, scale, x_ref, m_col_ref, m_row_ref, lat_ref, out_ref, cos_ref, sin_ref, cw_ref, sw_ref):
+def legendre_kernel(period, middle, turn, scale, x_ref, m_col_ref, m_row_ref, lat_ref, out_ref, cos_ref, sin_ref, cw_ref, sw_ref):
     rows, waves = x_ref.shape
     lats = lat_ref.shape[0]
     step = 32
@@ -66,7 +66,11 @@
     x = jnp.where(k < waves - m_col_ref[...], x_ref[...].astype(F32), 0.0).astype(BF16)
     p0 = lax.dot_general(cos_ref[...], x, NT, preferred_element_type=F32)
     p1 = lax.dot_general(sin_ref[...], x, NT, preferred_element_type=F32)
-    leg = ((cw_ref[...] * p0 - sw_ref[...] * p1) * scale).astype(BF16)
+    leg = (cw_ref[...] * p0 - sw_ref[...] * p1) * scale
+    cos, sin = sincos(m_row_ref[...] * float(middle), turn)
+    real = lax.broadcasted_iota(jnp.int32, (1, LANES), 1) % 4 < 2
+    other = jnp.where(real, pltpu.roll(leg, LANES - 2, 1), pltpu.roll(leg, 2, 1))
+    leg = (leg * cos + other * jnp.where(real, -sin, sin)).astype(BF16)
     src = lax.broadcasted_iota(jnp.int32, (rows, rows), 0)
     dst = lax.broadcasted_iota(jnp.int32, (rows, rows), 1)
     slots = rows // 4
@@ -74,12 +78,12 @@
     out_ref[...] = jnp.dot(leg, order, preferred_element_type=F32).astype(BF16)
 
 
-def legendre(x, own_ids, lat_rows, period, scale):
+def legendre(x, own_ids, lat_rows, period, middle, turn, scale):
     rows, waves = x.shape
     lats = lat_rows.shape[0]
     ids = jnp.repeat(own_ids, 4)
     return pl.pallas_call(
-        functools.partial(legendre_kernel, period, scale),
+        functools.partial(legendre_kernel, period, middle, turn, scale),
         out_shape=jax.ShapeDtypeStruct((lats, rows), BF16),
         scratch_shapes=[
             pltpu.VMEM((lats, waves), BF16),
@@ -129,41 +133,51 @@
     return out
 
 
-def fourier_kernel(nlon, scale, z_ref, m_ref, stamp_ref, out_ref, e_ref, l_ref, d_ref):
+def table_kernel(period, m_ref, e_ref):
     waves = m_ref.shape[1]
-    chunks = waves // LANES
-    spans = e_ref.shape[0] // 64
-    sub = lax.broadcasted_iota(jnp.int32, (8, LANES), 0).astype(F32)
-
-    def table(i, carry):
+    spans = e_ref.shape[0] // LANES
+    odd = 2.0 * lax.broadcasted_iota(jnp.int32, (8, LANES), 0).astype(F32) + 1.0
+
+    def fill(i, carry):
         at = pl.ds(pl.multiple_of(i * LANES, LANES), LANES)
-        at_sin = pl.ds(pl.multiple_of(waves + i * LANES, LANES), LANES)
         m = jnp.broadcast_to(m_ref[:, at], (8, LANES))
-        c, s = sincos(m * sub, nlon)
-        c8, s8 = sincos(m * 8.0, nlon)
-        c64, s64 = sincos(m * 64.0, nlon)
-        z = [(c, s)]
+        c8, s8 = sincos(m * 16.0, period)
+        c64, s64 = sincos(m * 128.0, period)
+        z = [sincos(m * odd, period)]
         for _ in range(7):
             z.append(rotate(*z[-1], c8, s8))
-        start = z
         for t in range(spans):
-            if t == spans - 1:
-                z = [rotate(a, b, c64, -s64) for a, b in start]
+            base = 256 * (t // 2) + 64 * (t % 2)
             for h in range(4):
                 (c0, s0), (c1, s1) = z[2 * h], z[2 * h + 1]
-                rows = pl.ds(t * 64 + h * 16, 16)
-                e_ref[rows, at] = jnp.concatenate([c0, c1], axis=0).astype(BF16)
-                e_ref[rows, at_sin] = jnp.concatenate([s0, s1], axis=0).astype(BF16)
-            if t < spans - 2:
+                e_ref[pl.ds(base + h * 16, 16), at] = jnp.concatenate([c0, c1], axis=0).astype(BF16)
+                e_ref[pl.ds(base + 128 + h * 16, 16), at] = jnp.concatenate([s0, s1], axis=0).astype(BF16)
+            if t + 1 < spans:
                 z = [rotate(a, b, c64, s64) for a, b in z]
         return carry
 
-    lax.fori_loop(0, chunks, table, 0)
+    lax.fori_loop(0, waves // LANES, fill, 0)
+
+
+def fourier_table(m, period, tiles):
+    waves = m.shape[1]
+    return pl.pallas_call(
+        functools.partial(table_kernel, period),
+        out_shape=jax.ShapeDtypeStruct((tiles * LANES, waves), BF16),
+        in_specs=[pl.BlockSpec(memory_space=pltpu.VMEM)],
+        out_specs=pl.BlockSpec(memory_space=pltpu.VMEM),
+        compiler_params=pltpu.CompilerParams(vmem_limit_bytes=8 << 20),
+        cost_estimate=pl.CostEstimate(flops=20000000, bytes_accessed=2500000, transcendentals=0),
+        name="fourier_table",
+    )(m)
+
+
+def fourier_kernel(scale, z_ref, m_ref, stamp_ref, e_ref, out_ref, l_ref, d_ref, g_ref):
+    waves = m_ref.shape[1]
     group = lax.broadcasted_iota(jnp.int32, (8, LANES), 1) // 32
 
     def spread(i, carry):
         at = pl.ds(pl.multiple_of(i * LANES, LANES), LANES)
-        at_sin = pl.ds(pl.multiple_of(waves + i * LANES, LANES), LANES)
         block = [z_ref[4 * i + u].astype(F32) for u in range(4)]
         parts = []
         for cf in range(4):
@@ -173,60 +187,84 @@
                 moved = pltpu.roll(block[u], turn, 1) if turn else block[u]
                 whole = moved if whole is None else jnp.where(group == u, moved, whole)
             parts.append(whole)
-        real = jnp.concatenate(parts[0:2], axis=0)
-        imag = jnp.concatenate(parts[2:4], axis=0)
-        m = jnp.broadcast_to(m_ref[:, at], (16, LANES))
+        both = jnp.concatenate(parts, axis=0)
+        m = jnp.broadcast_to(m_ref[:, at], both.shape)
         residue = m - 16.0 * jnp.floor(m * 0.0625)
         for q in range(16):
-            keep = residue == float(q)
-            re = jnp.where(keep, real, 0.0)
-            im = jnp.where(keep, imag, 0.0)
-            top, low = pl.ds(q * 32, 16), pl.ds(q * 32 + 16, 16)
-            re16, im16 = re.astype(BF16), im.astype(BF16)
-            l_ref[top, at] = re16
-            l_ref[low, at] = im16
-            l_ref[top, at_sin] = (-im).astype(BF16)
-            l_ref[low, at_sin] = re16
+            l_ref[pl.ds(q * 32, 32), at] = jnp.where(residue == float(q), both, 0.0).astype(BF16)
         return carry
 
-    lax.fori_loop(0, chunks, spread, 0)
+    lax.fori_loop(0, waves // LANES, spread, 0)
+    halves = e_ref.shape[0] // 256
+    low, high = pl.ds(0, LANES), pl.ds(LANES, LANES)
+    for p in range(halves):
+        d_ref[...] = lax.dot_general(l_ref[...], e_ref[pl.ds(p * 256, 256), :], NT, preferred_element_type=F32)
+        right, left = [], []
+        for q in range(16):
+            re, im = pl.ds(q * 32, 16), pl.ds(q * 32 + 16, 16)
+            c0, c1, s0, s1 = d_ref[re, low], d_ref[im, low], d_ref[re, high], d_ref[im, high]
+            right.append((c0 - s1, c1 + s0))
+            left.append((c0 + s1, c1 - s0))
+        for side, y in ((halves + p, right), (halves - 1 - p, left)):
+            for a, value in enumerate(sixteen_real(y)):
+                g_ref[side, pl.ds(a * 16, 16), :] = (value * scale).astype(BF16)
+
+    src = lax.broadcasted_iota(jnp.int32, (LANES, LANES), 0)
+    dst = lax.broadcasted_iota(jnp.int32, (LANES, LANES), 1)
+    half = LANES // 2
+
+    def pick(mirrored, upper):
+        want = (half - 1 + LANES * upper - dst) if mirrored else (dst + half - LANES * upper)
+        inside = (dst >= half) if upper else (dst < half)
+        return jnp.where(inside & (src == want), 1.0, 0.0).astype(BF16)
+
     lane = lax.broadcasted_iota(jnp.int32, (16, LANES), 1)
     unused = (lane >= STAMP_LANE) & (lane < LANES - STAMP_LANE)
     stamp = jnp.broadcast_to(stamp_ref[...], (16, LANES))
-    tiles = e_ref.shape[0] // LANES
-    for pair in range(tiles // 2):
-        d_ref[...] = lax.dot_general(
-            l_ref[...], e_ref[pl.ds(pair * 256, 256), :], NT, preferred_element_type=F32
+    tiles = 2 * halves
+    for t in range(tiles):
+        first, second = t, (t + 1) % tiles
+        value = jnp.dot(g_ref[first], pick(first < halves, 0), preferred_element_type=F32) + jnp.dot(
+            g_ref[second], pick(second < halves, 1), preferred_element_type=F32
         )
-        for h in range(2):
-            t = 2 * pair + h
-            cols = pl.ds(h * LANES, LANES)
-            y = [(d_ref[pl.ds(q * 32, 16), cols], d_ref[pl.ds(q * 32 + 16, 16), cols]) for q in range(16)]
-            g = sixteen_real(y)
-            for a in range(16):
-                value = g[a] * scale
-                if t == tiles - 1:
-                    value = jnp.where(unused, stamp, value)
-                out_ref[a, pl.ds(t * 16, 16), :] = value.astype(BF16)
-
-
-def fourier(z, wave_ids, stamp, nlon, scale):
-    waves = wave_ids.shape[0]
-    tiles = 6
+        for a in range(16):
+            got = value[a * 16 : (a + 1) * 16]
+            if t == tiles - 1:
+                got = jnp.where(unused, stamp, got)
+            out_ref[a, pl.ds(t * 16, 16), :] = got.astype(BF16)
+
+
+def fourier(z, m, stamp, table, scale):
+    tiles = table.shape[0] // LANES
+    vmem = pl.BlockSpec(memory_space=pltpu.VMEM)
     return pl.pallas_call(
-        functools.partial(fourier_kernel, nlon, scale),
+        functools.partial(fourier_kernel, scale),
         out_shape=jax.ShapeDtypeStruct((16, tiles * 16, LANES), BF16),
+        in_specs=[vmem] * 4,
+        out_specs=vmem,
         scratch_shapes=[
-            pltpu.VMEM((tiles * LANES, 2 * waves), BF16),
-            pltpu.VMEM((512, 2 * waves), BF16),
+            pltpu.VMEM((512, table.shape[1]), BF16),
             pltpu.VMEM((512, 256), F32),
+            pltpu.VMEM((tiles, 256, LANES), BF16),
         ],
         compiler_params=pltpu.CompilerParams(vmem_limit_bytes=24 << 20),
         name="fourier",
-    )(z, wave_ids.astype(F32)[None, :], stamp)
-
-
-def regroup_kernel(x_ref, out_ref, wide_ref):
+    )(z, m, stamp, table)
+
+
+def put_row(row, rows, at, value, out_ref, last_ref, first_ref):
+    out_ref[(row, *at)] = value
+    if row >= rows - ABOVE:
+        last_ref[(row - rows + ABOVE, *at)] = value
+    if row < BELOW:
+        first_ref[(row, *at)] = value
+
+
+def state_shapes(rows, tiles, fields):
+    return [jax.ShapeDtypeStruct((n, tiles, fields, LANES), BF16) for n in (rows, ABOVE, BELOW)]
+
+
+def regroup_kernel(x_ref, out_ref, last_ref, first_ref, wide_ref):
     rows, tiles = out_ref.shape[:2]
     sources = x_ref.shape[0]
     span = x_ref.shape[1]
@@ -236,21 +274,22 @@
         for t in range(tiles):
             for f in range(2):
                 got = wide_ref[pl.ds(t * 16 + f * 8 + j, sources, stride=span), :]
-                out_ref[j, t, pl.ds(f * sources, sources), :] = got.astype(BF16)
+                put_row(j, rows, (t, pl.ds(f * sources, sources)), got.astype(BF16), out_ref, last_ref, first_ref)
 
 
 def regroup(x):
     return pl.pallas_call(
         regroup_kernel,
-        out_shape=jax.ShapeDtypeStruct((8, x.shape[1] // 16, 32, LANES), BF16),
+        out_shape=state_shapes(8, x.shape[1] // 16, 32),
         scratch_shapes=[pltpu.VMEM((x.shape[0] * x.shape[1], LANES), F32)],
         compiler_params=pltpu.CompilerParams(vmem_limit_bytes=8 << 20),
         name="regroup",
     )(x)
 
 
-def advance_kernel(last, move_ref, weight_ref, before_ref, now_ref, after_ref, phys_ref, bias_ref, out_ref, s_ref, *rest):
+def advance_kernel(last, move_ref, weight_ref, before_ref, now_ref, after_ref, phys_ref, bias_ref, *refs):
     rows, tiles, fields = now_ref.shape[:3]
+    s_ref = refs[-1]
     s_ref[pl.ds(0, ABOVE)] = before_ref[...]
     s_ref[pl.ds(ABOVE, rows)] = now_ref[...]
     s_ref[pl.ds(ABOVE + rows, BELOW)] = after_ref[...]
@@ -288,7 +327,7 @@
             result.append(total)
         return result
 
-    def one_band(band, carry):
+    for band in range(rows // BLOCK_ROWS):
         for tile in range(5 if last else 6):
             if tile < 5:
                 dep = departed(band, tile + 1, tile)
@@ -303,19 +342,15 @@
                 value = dep[i] + jnp.tanh(push)
                 row = band * BLOCK_ROWS + i
                 if last:
-                    at = pl.ds(pl.multiple_of((row * 5 + tile) * fields, fields), fields)
-                    rest[0][at, :] = value
+                    refs[1][pl.ds((row * 5 + tile) * fields, fields), :] = value
                 else:
-                    out_ref[row, tile] = value.astype(BF16)
-        return carry
-
-    lax.fori_loop(0, rows // BLOCK_ROWS, one_band, 0)
+                    put_row(row, rows, (tile,), value.astype(BF16), *refs[:3])
     if last:
         for f in range(fields):
             kept = (f % 2) * (fields // 2) + f // 2
             for t in range(5):
-                got = rest[0][pl.ds(t * fields + kept, rows, stride=5 * fields), :]
-                out_ref[f, :, pl.ds(t * LANES, LANES)] = got.astype(BF16)
+                got = refs[1][pl.ds(t * fields + kept, rows, stride=5 * fields), :]
+                refs[0][f, :, pl.ds(t * LANES, LANES)] = got.astype(BF16)
 
 
 def advance(last, moves, weights, before, now, after, phys, bias):
@@ -323,13 +358,13 @@
     smem, vmem = pl.BlockSpec(memory_space=pltpu.SMEM), pl.BlockSpec(memory_space=pltpu.VMEM)
     scratch = [pltpu.VMEM((ABOVE + rows + BELOW, tiles, fields, LANES), BF16)]
     if last:
-        shape = (fields, rows, 5 * LANES)
-        scratch.append(pltpu.VMEM((rows * 5 * fields, LANES), F32))
+        shape = jax.ShapeDtypeStruct((fields, rows, 5 * LANES), BF16)
+        scratch.insert(0, pltpu.VMEM((rows * 5 * fields, LANES), F32))
     else:
-        shape = (rows, tiles, fields, LANES)
+        shape = state_shapes(rows, tiles, fields)
     return pl.pallas_call(
         functools.partial(advance_kernel, last),
-        out_shape=jax.ShapeDtypeStruct(shape, BF16),
+        out_shape=shape,
         in_specs=[smem, smem] + [vmem] * 5,
         scratch_shapes=scratch,
         compiler_params=pltpu.CompilerParams(vmem_limit_bytes=16 << 20),
@@ -372,11 +407,10 @@
     return moves, weights
 
 
-def row_halos(state):
+def row_halos(last, first):
     size = lax.axis_size("wave")
-    rows = state.shape[0]
-    before = lax.ppermute(state[rows - ABOVE :], "wave", [(i, i + 1) for i in range(size - 1)])
-    after = lax.ppermute(state[:BELOW], "wave", [(i + 1, i) for i in range(size - 1)])
+    before = lax.ppermute(last, "wave", [(i, i + 1) for i in range(size - 1)])
+    after = lax.ppermute(first, "wave", [(i + 1, i) for i in range(size - 1)])
     return before, after
 
 
@@ -387,14 +421,22 @@
     nlon = shift_rows.shape[2] * BLOCK_COLS * owners
     scale = 1.0 / math.sqrt(waves)
     own_ids = lax.dynamic_slice_in_dim(wave_ids, lax.axis_index("wave") * slots, slots)
-    outgoing = legendre(spectral.reshape(slots * parts * fields, waves), own_ids, lat_rows, 8 * lats, scale)
+    outgoing = legendre(spectral.reshape(slots * parts * fields, waves), own_ids, lat_rows, 8 * lats, nlon // owners - 1, 2 * nlon, scale)
     outgoing = outgoing.reshape(bands, lats // bands, slots * parts * fields)
     arrived = lax.all_to_all(outgoing, "wave", split_axis=0, concat_axis=0, tiled=True)
+    m = wave_ids.astype(F32)[None, :]
+    table = fourier_table(m, 2 * nlon, 6)
     stamp = edge_stamp(shift_rows[0], shift_cols[0], frac_rows[0], frac_cols[0])
-    columns = fourier(arrived, wave_ids, stamp, nlon, scale)
+    own = (shift_rows.astype(F32), shift_cols.astype(F32), frac_rows, frac_cols)
+    second = block_tables(*[jnp.pad(o[1], ((0, 0), (1, 1))) for o in own])
+    split = (owners, fields)
+    phys = phys_weight.reshape(split + split).transpose(1, 0, 3, 2).reshape(phys_weight.shape)
+    bias = phys_bias.reshape(split).T.reshape(-1, 1)
+    arrived, second, phys, bias = lax.optimization_barrier((arrived, second, phys, bias))
+    columns = fourier(arrived, m, stamp, table, scale)
     columns = lax.all_to_all(columns, "lev", split_axis=0, concat_axis=0, tiled=True)
-    state = regroup(columns)
-    before, after = row_halos(state)
+    state, *edges = regroup(columns)
+    before, after = row_halos(*edges)
 
     me = lax.axis_index("lev")
     stamp_row = columns.shape[1] - 16
@@ -402,16 +444,10 @@
     west = lax.dynamic_slice(columns, ((me + owners - 1) % owners, stamp_row, STAMP_LANE), size)
     east = lax.dynamic_slice(columns, ((me + 1) % owners, stamp_row, STAMP_LANE), size)
     west, east = read_stamp(west, 1), read_stamp(east, 0)
-    own = (shift_rows.astype(F32), shift_cols.astype(F32), frac_rows, frac_cols)
     first = [jnp.concatenate([w, o[0], e], axis=1) for w, o, e in zip(west, own, east)]
-    second = [jnp.pad(o[1], ((0, 0), (1, 1))) for o in own]
-
-    split = (owners, fields)
-    phys = phys_weight.reshape(split + split).transpose(1, 0, 3, 2).reshape(phys_weight.shape)
-    bias = phys_bias.reshape(split).T.reshape(-1, 1)
-    state = advance(False, *block_tables(*first), before, state, after, phys, bias)
-    before, after = row_halos(state)
-    return advance(True, *block_tables(*second), before, state, after, phys, bias)
+    state, *edges = advance(False, *block_tables(*first), before, state, after, phys, bias)
+    before, after = row_halos(*edges)
+    return advance(True, *second, before, state, after, phys, bias)
 
 
 def solution(mesh):

time: 92.7 us -> 92.4 us (level); the launches traced: 92.2 us -> 90.6 us
  other arithmetic: 1.42 us -> 9.72 us
  local copies, waits for them, and re-layouts: 8.28 us -> 4.45 us
  Pallas kernels: 16.4 us -> 13.9 us
  starting transfers between devices: 39.7 us -> 37.4 us
  waiting for transfers between devices: 26.1 us -> 24.9 us
    all_to_all x1, waiting for transfers between devices: 6.82 us -> 1.22 us  [shards(): lax.all_to_all(outgoing, 'wave', split_axis=0, concat_axis=0, tiled=True)]
    unnamed x16 -> x4, local copies, waits for them, and re-layouts: 4.65 us -> 0.01 us
    ppermute x4, waiting for transfers between devices: 6.92 us -> 11.2 us  [the longest x2 11.2 us: row_halos(): after = lax.ppermute(first, 'wave', [(i + 1, i) for i in range(size - 1)])]
    unnamed x18 -> x19, other arithmetic: 0.78 us -> 4.25 us
    pallas_call x5 -> x6, Pallas kernels: 16.4 us -> 13.9 us  [the longest x2 4.47 us: advance(): pl.pallas_call(functools.partial(advance_kernel, last), out_shape=shape,...]
    ppermute x4, starting transfers between devices: 12.7 us -> 10.4 us  [the longest x2 6.07 us: row_halos(): before = lax.ppermute(last, 'wave', [(i, i + 1) for i in range(size - 1)])]
    concatenate x4, other arithmetic: 0.1 us -> 1.49 us  [shards(): jnp.concatenate([w, o[0], e], axis=1)]
    convert_element_type x2, other arithmetic: 0.01 us -> 1.37 us  [shards(): own = (shift_rows.astype(F32), shift_cols.astype(F32), frac_rows, frac_cols)]
  transfers between devices with their start and end apart: 6 -> 6, of which waited for: 6 -> 4; matrix products, arithmetic and copies ran while one was open for 3% -> 12% of each run, Pallas kernels for 0% -> 1%
where the time goes in v2:
time: 92.4 us; the launch traced here: 90.6 us
  starting transfers between devices  37.4 us (40%)
  waiting for transfers between devices  24.9 us (27%)
  Pallas kernels  13.9 us (15%)
  other arithmetic  9.72 us (11%)
  local copies, waits for them, and re-layouts  4.45 us (5%)
    all_to_all x1, starting transfers between devices, shards(): lax.all_to_all(outgoing, 'wave', split_axis=0, concat_axis=0, tiled=True)  17.9 us
    all_to_all x1, waiting for transfers between devices, shards(): lax.all_to_all(columns, 'lev', split_axis=0, concat_axis=0, tiled=True)  12.5 us
    ppermute x2, waiting for transfers between devices, row_halos(): after = lax.ppermute(first, 'wave', [(i + 1, i) for i in range(size - 1)])  11.2 us
    all_to_all x1, starting transfers between devices, shards(): lax.all_to_all(columns, 'lev', split_axis=0, concat_axis=0, tiled=True)  9.09 us
    ppermute x2, starting transfers between devices, row_halos(): before = lax.ppermute(last, 'wave', [(i, i + 1) for i in range(size - 1)])  6.07 us
    pallas_call x2, Pallas kernels, advance(): pl.pallas_call(functools.partial(advance_kernel, last), out_shape=shape,...  4.47 us
    ppermute x2, starting transfers between devices, row_halos(): after = lax.ppermute(first, 'wave', [(i + 1, i) for i in range(size - 1)])  4.34 us
    unnamed x19, other arithmetic  4.25 us
  transfers between devices with their start and end apart: 6, of which 4 were waited for; matrix products, arithmetic and copies ran while one was open for 12% of the time, Pallas kernels for 1%

profile of v2, /device:TPU:1, one launch (start us, length us, event | category | flops | bytes accessed | tf_op | source)
XLA Modules:
  0.0 90.6 jit_solution(8374109532262305623)
XLA Ops:
  0.0 1.2 %reshape.902.x_ref = bf16[128,1536]{1,0:T(8,128)(2,1)S(1)} reshape(bf16[32,2,2,1536]{3,2,1,0:T(2,128)(2,1)} %param.9) | data formatting | bytes 786432 | tf_op jit(solution)/shard_map/reshape | solution.py:424
  1.2 0.8 fusion.8
  2.3 0.7 convert_element_type.50
  3.1 3.9 %legendre.1 = bf16[384,128]{1,0:T(8,128)(2,1)} custom-call(bf16[128,1536]{1,0:T(8,128)(2,1)S(1)} %reshape.902.x_ref, s32[128,1]{1,0:T(8,128)S(1)} %broadcast_in_dim_reshape.5.m_col_ref, f32[1,128]{1,0:T(1,128)S(1)} %convert_element_type.49.m_row_ref, f32[384,1]{1,0:T(8,128)S(1)} %broadcast_in_dim.15.lat_ref), custom_call_target="tpu_custom_call" | custom-call | tf_op jit(solution)/shard_map/legendre/pallas_call | solution.py:85
  7.0 17.9 %all-to-all-start = ((bf16[48,8,128]{2,1,0:T(8,128)(2,1)}), bf16[48,8,128]{2,1,0:T(8,128)(2,1)S(1)}, u32[]{:S(2)}, u32[]{:S(2)}) async-start(bf16[48,8,128]{2,1,0:T(8,128)(2,1)} %bitcast), calls=%async_computation | async-start | bytes 196608 | tf_op jit(solution)/shard_map/all_to_all | solution.py:426
  26.3 0.7 convert_element_type.55
  28.0 0.7 constant_dynamic-update-slice_fusion.14
  29.3 0.7 slice_bitcast_fusion.11
  30.4 0.7 constant_dynamic-update-slice_fusion.11
  31.7 0.7 slice_bitcast_fusion.10
  33.0 0.9 reshape.905
  34.8 0.9 fourier_table.1.e_ref
  35.8 1.2 %all-to-all-done.z_ref = bf16[48,8,128]{2,1,0:T(8,128)(2,1)S(1)} async-done(((bf16[48,8,128]{2,1,0:T(8,128)(2,1)}), bf16[48,8,128]{2,1,0:T(8,128)(2,1)S(1)}, u32[]{:S(2)}, u32[]{:S(2)}) %all-to-all-start) | async-done | bytes 98336 | tf_op jit(solution)/shard_map/all_to_all | solution.py:426
  37.0 4.1 %fourier.1 = bf16[16,96,128]{2,1,0:T(8,128)(2,1)} custom-call(bf16[48,8,128]{2,1,0:T(8,128)(2,1)S(1)} %all-to-all-done.z_ref, f32[1,1536]{1,0:T(1,128)S(1)} %broadcast_in_dim.14.m_ref, f32[1,128]{1,0:T(1,128)S(1)} %pad.21.stamp_ref, bf16[768,1536]{1,0:T(8,128)(2,1)S(1)} %fourier_table.1.e_ref), custom_call_target="tpu_custom_call" | custom-call | tf_op jit(solution)/shard_map/fourier/pallas_call | solution.py:240
  41.1 9.1 %all-to-all-start.1 = ((bf16[16,96,128]{2,1,0:T(8,128)(2,1)}), bf16[16,96,128]{2,1,0:T(8,128)(2,1)S(1)}, u32[]{:S(2)}, u32[]{:S(2)}) async-start(bf16[16,96,128]{2,1,0:T(8,128)(2,1)} %fourier.1), calls=%async_computation.1 | async-start | bytes 786432 | tf_op jit(solution)/shard_map/all_to_all | solution.py:437
  50.3 12.5 %all-to-all-done.1.x_ref = bf16[16,96,128]{2,1,0:T(8,128)(2,1)S(1)} async-done(((bf16[16,96,128]{2,1,0:T(8,128)(2,1)}), bf16[16,96,128]{2,1,0:T(8,128)(2,1)S(1)}, u32[]{:S(2)}, u32[]{:S(2)}) %all-to-all-start.1) | async-done | bytes 393248 | tf_op jit(solution)/shard_map/all_to_all | solution.py:437
  63.9 4.1 %collective-permute-start = (bf16[6,6,32,128]{3,2,1,0:T(8,128)(2,1)S(1)}, bf16[6,6,32,128]{3,2,1,0:T(8,128)(2,1)S(1)}, u32[]{:S(2)}, u32[]{:S(2)}) collective-permute-start(bf16[6,6,32,128]{3,2,1,0:T(8,128)(2,1)S(1)} %get-tuple-element.19), channel_id=1, source_target_pairs={{0,16},{16,32},{32,48},{48,64},{64,80},{80,96},{96,112},{112,128},... | collective-permute-start | bytes 884744 | tf_op jit(solution)/shard_map/ppermute | solution.py:412
  68.1 1.9 %collective-permute-start.1 = (bf16[5,6,32,128]{3,2,1,0:T(8,128)(2,1)S(1)}, bf16[5,6,32,128]{3,2,1,0:T(8,128)(2,1)S(1)}, u32[]{:S(2)}, u32[]{:S(2)}) collective-permute-start(bf16[5,6,32,128]{3,2,1,0:T(8,128)(2,1)S(1)} %get-tuple-element.21), channel_id=1, source_target_pairs={{16,0},{32,16},{48,32},{64,48},{80,64},{96,80},{112,96},{128,112},... | collective-permute-start | bytes 737288 | tf_op jit(solution)/shard_map/ppermute | solution.py:413
  70.5 5.0 %collective-permute-done.1.after_ref = bf16[5,6,32,128]{3,2,1,0:T(8,128)(2,1)S(1)} collective-permute-done((bf16[5,6,32,128]{3,2,1,0:T(8,128)(2,1)S(1)}, bf16[5,6,32,128]{3,2,1,0:T(8,128)(2,1)S(1)}, u32[]{:S(2)}, u32[]{:S(2)}) %collective-permute-start.1) | collective-permute-done | bytes 245792 | tf_op jit(solution)/shard_map/ppermute | solution.py:413
  75.6 1.9 %advance_first.1 = (bf16[8,6,32,128]{3,2,1,0:T(8,128)(2,1)S(1)}, bf16[6,6,32,128]{3,2,1,0:T(8,128)(2,1)S(1)}, bf16[5,6,32,128]{3,2,1,0:T(8,128)(2,1)S(1)}) custom-call(s32[28]{0:T(128)S(1)} %convert_element_type.59.move_ref, f32[112]{0:T(128)S(1)} %reshape.914.weight_ref, bf16[6,6,32,128]{3,2,1,0:T(8,128)(2,1)S(1)} %collective-permute-done.before_ref, ...), custom_call_target="tpu_custom_call" | custom-call | tf_op jit(solution)/shard_map/advance_first/pallas_call | solution.py:365
  77.5 1.9 %collective-permute-start.2 = (bf16[6,6,32,128]{3,2,1,0:T(8,128)(2,1)S(1)}, bf16[6,6,32,128]{3,2,1,0:T(8,128)(2,1)S(1)}, u32[]{:S(2)}, u32[]{:S(2)}) collective-permute-start(bf16[6,6,32,128]{3,2,1,0:T(8,128)(2,1)S(1)} %get-tuple-element.24), channel_id=1, source_target_pairs={{0,16},{16,32},{32,48},{48,64},{64,80},{80,96},{96,112},{112,128},... | collective-permute-start | bytes 884744 | tf_op jit(solution)/shard_map/ppermute | solution.py:412
  79.4 2.4 %collective-permute-start.3 = (bf16[5,6,32,128]{3,2,1,0:T(8,128)(2,1)S(1)}, bf16[5,6,32,128]{3,2,1,0:T(8,128)(2,1)S(1)}, u32[]{:S(2)}, u32[]{:S(2)}) collective-permute-start(bf16[5,6,32,128]{3,2,1,0:T(8,128)(2,1)S(1)} %get-tuple-element.26), channel_id=1, source_target_pairs={{16,0},{32,16},{48,32},{64,48},{80,64},{96,80},{112,96},{128,112},... | collective-permute-start | bytes 737288 | tf_op jit(solution)/shard_map/ppermute | solution.py:413
  81.9 6.2 %collective-permute-done.3.after_ref = bf16[5,6,32,128]{3,2,1,0:T(8,128)(2,1)S(1)} collective-permute-done((bf16[5,6,32,128]{3,2,1,0:T(8,128)(2,1)S(1)}, bf16[5,6,32,128]{3,2,1,0:T(8,128)(2,1)S(1)}, u32[]{:S(2)}, u32[]{:S(2)}) %collective-permute-start.3) | collective-permute-done | bytes 245792 | tf_op jit(solution)/shard_map/ppermute | solution.py:413
  88.1 2.5 %advance_last.1 = bf16[32,8,640]{2,1,0:T(8,128)(2,1)} custom-call(s32[28]{0:T(128)S(1)} %convert_element_type.54.move_ref, f32[112]{0:T(128)S(1)} %reshape.904.weight_ref, bf16[6,6,32,128]{3,2,1,0:T(8,128)(2,1)S(1)} %collective-permute-done.2.before_ref, bf16[8,6,32,128]{3,2,1,0:T(8,128)(2,1)S(1)} %get-tuple-element.25.now_ref, ...), custom_call_target="tpu_custom_call" | custom-call | tf_op jit(solution)/shard_map/advance_last/pallas_call | solution.py:365
  (65 shorter events, 7.7 us)
Async XLA Ops:
  0.0 34.5 %copy-start = (f32[2,2,5]{2,1,0:T(2,128)S(1)}, f32[2,2,5]{2,1,0:T(2,128)}, u32[]{:S(2)}) copy-start(f32[2,2,5]{2,1,0:T(2,128)} %param.15) | copy-start | bytes 244
  0.0 34.2 %copy-start.1 = (f32[32]{0:T(128)S(1)}, f32[32]{0:T(128)}, u32[]{:S(2)}) copy-start(f32[32]{0:T(128)} %param.17) | copy-start | bytes 388
  7.0 30.0 %all-to-all-start = ((bf16[48,8,128]{2,1,0:T(8,128)(2,1)}), bf16[48,8,128]{2,1,0:T(8,128)(2,1)S(1)}, u32[]{:S(2)}, u32[]{:S(2)}) async-start(bf16[48,8,128]{2,1,0:T(8,128)(2,1)} %bitcast), calls=%async_computation | async-start | bytes 196608 | tf_op jit(solution)/shard_map/all_to_all | solution.py:426
  41.1 21.7 %all-to-all-start.1 = ((bf16[16,96,128]{2,1,0:T(8,128)(2,1)}), bf16[16,96,128]{2,1,0:T(8,128)(2,1)S(1)}, u32[]{:S(2)}, u32[]{:S(2)}) async-start(bf16[16,96,128]{2,1,0:T(8,128)(2,1)} %fourier.1), calls=%async_computation.1 | async-start | bytes 786432 | tf_op jit(solution)/shard_map/all_to_all | solution.py:437
  63.9 11.7 %collective-permute-start = (bf16[6,6,32,128]{3,2,1,0:T(8,128)(2,1)S(1)}, bf16[6,6,32,128]{3,2,1,0:T(8,128)(2,1)S(1)}, u32[]{:S(2)}, u32[]{:S(2)}) collective-permute-start(bf16[6,6,32,128]{3,2,1,0:T(8,128)(2,1)S(1)} %get-tuple-element.19), channel_id=1, source_target_pairs={{0,16},{16,32},{32,48},{48,64},{64,80},{80,96},{96,112},{112,128},... | collective-permute-start | bytes 884744 | tf_op jit(solution)/shard_map/ppermute | solution.py:412
  68.1 7.5 %collective-permute-start.1 = (bf16[5,6,32,128]{3,2,1,0:T(8,128)(2,1)S(1)}, bf16[5,6,32,128]{3,2,1,0:T(8,128)(2,1)S(1)}, u32[]{:S(2)}, u32[]{:S(2)}) collective-permute-start(bf16[5,6,32,128]{3,2,1,0:T(8,128)(2,1)S(1)} %get-tuple-element.21), channel_id=1, source_target_pairs={{16,0},{32,16},{48,32},{64,48},{80,64},{96,80},{112,96},{128,112},... | collective-permute-start | bytes 737288 | tf_op jit(solution)/shard_map/ppermute | solution.py:413
  77.5 10.5 %collective-permute-start.2 = (bf16[6,6,32,128]{3,2,1,0:T(8,128)(2,1)S(1)}, bf16[6,6,32,128]{3,2,1,0:T(8,128)(2,1)S(1)}, u32[]{:S(2)}, u32[]{:S(2)}) collective-permute-start(bf16[6,6,32,128]{3,2,1,0:T(8,128)(2,1)S(1)} %get-tuple-element.24), channel_id=1, source_target_pairs={{0,16},{16,32},{32,48},{48,64},{64,80},{80,96},{96,112},{112,128},... | collective-permute-start | bytes 884744 | tf_op jit(solution)/shard_map/ppermute | solution.py:412
  79.4 8.6 %collective-permute-start.3 = (bf16[5,6,32,128]{3,2,1,0:T(8,128)(2,1)S(1)}, bf16[5,6,32,128]{3,2,1,0:T(8,128)(2,1)S(1)}, u32[]{:S(2)}, u32[]{:S(2)}) collective-permute-start(bf16[5,6,32,128]{3,2,1,0:T(8,128)(2,1)S(1)} %get-tuple-element.26), channel_id=1, source_target_pairs={{16,0},{32,16},{48,32},{64,48},{80,64},{96,80},{112,96},{128,112},... | collective-permute-start | bytes 737288 | tf_op jit(solution)/shard_map/ppermute | solution.py:413

commit v3 on v2

--- a/solution.py
+++ b/solution.py
@@ -13,7 +13,9 @@
 LANES = 128
 ABOVE = 6
 BELOW = 5
-STAMP_LANE = 32
+HALO = 16
+STAMP_LANE = 4 * HALO
+PER_BLOCK = 10
 F32 = jnp.float32
 BF16 = jnp.bfloat16
 NT = (((1,), (1,)), ((), ()))
@@ -38,20 +40,36 @@
     return c * rc - s * rs, s * rc + c * rs
 
 
-def legendre_kernel(period, middle, turn, scale, x_ref, m_col_ref, m_row_ref, lat_ref, out_ref, cos_ref, sin_ref, cw_ref, sw_ref):
+def down(row):
+    return jnp.broadcast_to(row, (LANES, LANES)).T
+
+
+def legendre_kernel(
+    period, middle, turn, scale, ids_ref, lat_in_ref, band_ref, x_ref, out_ref, cos_ref, sin_ref, cw_ref, sw_ref, lat_ref
+):
     rows, waves = x_ref.shape
-    lats = lat_ref.shape[0]
+    lats = out_ref.shape[0]
+    slots = rows // 4
     step = 32
-    lane = lax.broadcasted_iota(jnp.int32, (step, LANES), 1).astype(F32)
-    m_row = jnp.broadcast_to(m_row_ref[...], (step, LANES))
+    lane = lax.broadcasted_iota(jnp.int32, (1, LANES), 1)
+    first = band_ref[0] * slots
+    m_row = jnp.zeros((1, LANES), jnp.int32)
+    for s in range(slots):
+        m_row = jnp.where(lane // 4 == s, ids_ref[first + s], m_row)
+    m_col = down(m_row.astype(F32))
+    m_row = m_row.astype(F32)
+    for i in range(lats // LANES):
+        lat_ref[pl.ds(i * LANES, LANES), :] = down(lat_in_ref[:, pl.ds(i * LANES, LANES)].astype(F32))
+    wide_lane = lax.broadcasted_iota(jnp.int32, (step, LANES), 1).astype(F32)
+    wide_m = jnp.broadcast_to(m_row, (step, LANES))
 
     def fill(i, carry):
         at = pl.ds(pl.multiple_of(i * step, step), step)
-        lat = jnp.broadcast_to(lat_ref[at, :], (step, LANES))
-        cw, sw = sincos(lat * m_row, period)
+        lat = lat_ref[at, :]
+        cw, sw = sincos(lat * wide_m, period)
         cw_ref[at, :] = cw
         sw_ref[at, :] = sw
-        c, s = sincos(lat * lane, period)
+        c, s = sincos(lat * wide_lane, period)
         rc, rs = sincos(lat * float(LANES), period)
         for a in range(waves // LANES):
             cols = pl.ds(a * LANES, LANES)
@@ -62,38 +80,44 @@
         return carry
 
     lax.fori_loop(0, lats // step, fill, 0)
-    k = lax.broadcasted_iota(jnp.int32, (rows, waves), 1)
-    x = jnp.where(k < waves - m_col_ref[...], x_ref[...].astype(F32), 0.0).astype(BF16)
+    kept = []
+    k = lax.broadcasted_iota(jnp.int32, (rows, LANES), 1).astype(F32)
+    for a in range(waves // LANES):
+        part = x_ref[:, pl.ds(a * LANES, LANES)].astype(F32)
+        kept.append(jnp.where(k < (waves - a * LANES) - m_col, part, 0.0).astype(BF16))
+    x = jnp.concatenate(kept, axis=1)
     p0 = lax.dot_general(cos_ref[...], x, NT, preferred_element_type=F32)
     p1 = lax.dot_general(sin_ref[...], x, NT, preferred_element_type=F32)
     leg = (cw_ref[...] * p0 - sw_ref[...] * p1) * scale
-    cos, sin = sincos(m_row_ref[...] * float(middle), turn)
-    real = lax.broadcasted_iota(jnp.int32, (1, LANES), 1) % 4 < 2
+    cos, sin = sincos(m_row * float(middle), turn)
+    real = lane % 4 < 2
     other = jnp.where(real, pltpu.roll(leg, LANES - 2, 1), pltpu.roll(leg, 2, 1))
     leg = (leg * cos + other * jnp.where(real, -sin, sin)).astype(BF16)
     src = lax.broadcasted_iota(jnp.int32, (rows, rows), 0)
     dst = lax.broadcasted_iota(jnp.int32, (rows, rows), 1)
-    slots = rows // 4
     order = jnp.where((src % 4) * slots + src // 4 == dst, 1.0, 0.0).astype(BF16)
     out_ref[...] = jnp.dot(leg, order, preferred_element_type=F32).astype(BF16)
 
 
-def legendre(x, own_ids, lat_rows, period, middle, turn, scale):
+def legendre(x, wave_ids, band, lat_rows, period, middle, turn, scale):
     rows, waves = x.shape
     lats = lat_rows.shape[0]
-    ids = jnp.repeat(own_ids, 4)
+    smem, vmem = pl.BlockSpec(memory_space=pltpu.SMEM), pl.BlockSpec(memory_space=pltpu.VMEM)
     return pl.pallas_call(
         functools.partial(legendre_kernel, period, middle, turn, scale),
         out_shape=jax.ShapeDtypeStruct((lats, rows), BF16),
+        in_specs=[smem, vmem, smem, vmem],
+        out_specs=vmem,
         scratch_shapes=[
             pltpu.VMEM((lats, waves), BF16),
             pltpu.VMEM((lats, waves), BF16),
             pltpu.VMEM((lats, LANES), F32),
             pltpu.VMEM((lats, LANES), F32),
+            pltpu.VMEM((lats, LANES), F32),
         ],
         compiler_params=pltpu.CompilerParams(vmem_limit_bytes=24 << 20),
         name="legendre",
-    )(x, ids[:, None], ids[None, :].astype(F32), lat_rows.astype(F32)[:, None])
+    )(wave_ids, lat_rows.reshape(1, -1), band, x)
 
 
 def times_i(z, power):
@@ -133,14 +157,25 @@
     return out
 
 
-def table_kernel(period, m_ref, e_ref):
-    waves = m_ref.shape[1]
+def cubic_weights(fraction):
+    coord = 1.0 - fraction
+    return (
+        -coord * (coord - 1.0) * (coord - 2.0) * (1.0 / 6.0),
+        (coord + 1.0) * (coord - 1.0) * (coord - 2.0) * 0.5,
+        -(coord + 1.0) * coord * (coord - 2.0) * 0.5,
+        (coord + 1.0) * coord * (coord - 1.0) * (1.0 / 6.0),
+    )
+
+
+def table_kernel(period, ids_ref, sr_ref, sc_ref, fr_ref, fc_ref, e_ref, m_ref, stamp_ref, param_ref):
+    waves = ids_ref.shape[1]
     spans = e_ref.shape[0] // LANES
     odd = 2.0 * lax.broadcasted_iota(jnp.int32, (8, LANES), 0).astype(F32) + 1.0
+    m_ref[...] = ids_ref[...].astype(F32)
 
     def fill(i, carry):
         at = pl.ds(pl.multiple_of(i * LANES, LANES), LANES)
-        m = jnp.broadcast_to(m_ref[:, at], (8, LANES))
+        m = jnp.broadcast_to(ids_ref[:, at].astype(F32), (8, LANES))
         c8, s8 = sincos(m * 16.0, period)
         c64, s64 = sincos(m * 128.0, period)
         z = [sincos(m * odd, period)]
@@ -157,19 +192,43 @@
         return carry
 
     lax.fori_loop(0, waves // LANES, fill, 0)
-
-
-def fourier_table(m, period, tiles):
-    waves = m.shape[1]
+    steps, bands, blocks = sr_ref.shape
+    lane = lax.broadcasted_iota(jnp.int32, (8, LANES), 1)
+    row = lax.broadcasted_iota(jnp.int32, (8, LANES), 0)
+    stamp = jnp.zeros((8, LANES), F32)
+    for step in range(steps):
+        for band in range(bands):
+            for block in range(blocks):
+                moves = (sr_ref[step, band, block].astype(F32), sc_ref[step, band, block].astype(F32))
+                values = moves + cubic_weights(fr_ref[step, band, block]) + cubic_weights(fc_ref[step, band, block])
+                for k, value in enumerate(values):
+                    param_ref[((step * bands + band) * blocks + block) * PER_BLOCK + k] = value
+                    side = {0: 0, blocks - 1: 1}.get(block)
+                    if step == 0 and side is not None:
+                        at = STAMP_LANE + (side * bands + band) * PER_BLOCK + k
+                        stamp = jnp.where(lane == at, value, stamp)
+    high = stamp.astype(BF16).astype(F32)
+    mid = (stamp - high).astype(BF16).astype(F32)
+    stamp_ref[...] = jnp.where(row == 0, high, jnp.where(row == 1, mid, jnp.where(row == 2, stamp - high - mid, 0.0)))
+
+
+def fourier_table(ids, shift_rows, shift_cols, frac_rows, frac_cols, period, tiles):
+    waves = ids.shape[1]
+    smem, vmem = pl.BlockSpec(memory_space=pltpu.SMEM), pl.BlockSpec(memory_space=pltpu.VMEM)
     return pl.pallas_call(
         functools.partial(table_kernel, period),
-        out_shape=jax.ShapeDtypeStruct((tiles * LANES, waves), BF16),
-        in_specs=[pl.BlockSpec(memory_space=pltpu.VMEM)],
-        out_specs=pl.BlockSpec(memory_space=pltpu.VMEM),
+        out_shape=[
+            jax.ShapeDtypeStruct((tiles * LANES, waves), BF16),
+            jax.ShapeDtypeStruct((1, waves), F32),
+            jax.ShapeDtypeStruct((8, LANES), F32),
+            jax.ShapeDtypeStruct((shift_rows.size * PER_BLOCK,), F32),
+        ],
+        in_specs=[vmem] + [smem] * 4,
+        out_specs=[vmem, vmem, vmem, smem],
         compiler_params=pltpu.CompilerParams(vmem_limit_bytes=8 << 20),
         cost_estimate=pl.CostEstimate(flops=20000000, bytes_accessed=2500000, transcendentals=0),
         name="fourier_table",
-    )(m)
+    )(ids, shift_rows, shift_cols, frac_rows, frac_cols)
 
 
 def fourier_kernel(scale, z_ref, m_ref, stamp_ref, e_ref, out_ref, l_ref, d_ref, g_ref):
@@ -218,9 +277,8 @@
         inside = (dst >= half) if upper else (dst < half)
         return jnp.where(inside & (src == want), 1.0, 0.0).astype(BF16)
 
-    lane = lax.broadcasted_iota(jnp.int32, (16, LANES), 1)
-    unused = (lane >= STAMP_LANE) & (lane < LANES - STAMP_LANE)
-    stamp = jnp.broadcast_to(stamp_ref[...], (16, LANES))
+    lane = lax.broadcasted_iota(jnp.int32, (8, LANES), 1)
+    stamp = stamp_ref[...]
     tiles = 2 * halves
     for t in range(tiles):
         first, second = t, (t + 1) % tiles
@@ -228,10 +286,14 @@
             g_ref[second], pick(second < halves, 1), preferred_element_type=F32
         )
         for a in range(16):
-            got = value[a * 16 : (a + 1) * 16]
-            if t == tiles - 1:
-                got = jnp.where(unused, stamp, got)
-            out_ref[a, pl.ds(t * 16, 16), :] = got.astype(BF16)
+            one, two = value[a * 16 : a * 16 + 8], value[a * 16 + 8 : a * 16 + 16]
+            if t < tiles - 1:
+                out_ref[a, pl.ds(t * 8, 8), :] = one.astype(BF16)
+                out_ref[a, pl.ds((tiles - 1 + t) * 8, 8), :] = two.astype(BF16)
+            else:
+                one, two = pltpu.roll(one, HALO, 1), pltpu.roll(two, 3 * HALO, 1)
+                halo = jnp.where(lane < 2 * HALO, one, jnp.where(lane < STAMP_LANE, two, stamp))
+                out_ref[a, pl.ds((tiles - 1) * 16, 8), :] = halo.astype(BF16)
 
 
 def fourier(z, m, stamp, table, scale):
@@ -239,7 +301,7 @@
     vmem = pl.BlockSpec(memory_space=pltpu.VMEM)
     return pl.pallas_call(
         functools.partial(fourier_kernel, scale),
-        out_shape=jax.ShapeDtypeStruct((16, tiles * 16, LANES), BF16),
+        out_shape=jax.ShapeDtypeStruct((16, tiles * 16 - 8, LANES), BF16),
         in_specs=[vmem] * 4,
         out_specs=vmem,
         scratch_shapes=[
@@ -264,46 +326,65 @@
     return [jax.ShapeDtypeStruct((n, tiles, fields, LANES), BF16) for n in (rows, ABOVE, BELOW)]
 
 
-def regroup_kernel(x_ref, out_ref, last_ref, first_ref, wide_ref):
-    rows, tiles = out_ref.shape[:2]
+def regroup_kernel(owner_ref, x_ref, out_ref, last_ref, first_ref, edge_ref, wide_ref):
+    rows, tiles, fields = out_ref.shape[:3]
     sources = x_ref.shape[0]
-    span = x_ref.shape[1]
+    main, span = (tiles - 1) * rows, tiles * rows
     for v in range(sources):
-        wide_ref[pl.ds(v * span, span), :] = x_ref[v].astype(F32)
+        halo = x_ref[v, pl.ds(2 * main, rows), :].astype(F32)
+        for f in range(2):
+            at = (2 * v + f) * span
+            wide_ref[pl.ds(at, main), :] = x_ref[v, pl.ds(f * main, main), :].astype(F32)
+            wide_ref[pl.ds(at + main, rows), :] = pltpu.roll(halo, LANES - HALO - 2 * HALO * f, 1)
     for j in range(rows):
         for t in range(tiles):
-            for f in range(2):
-                got = wide_ref[pl.ds(t * 16 + f * 8 + j, sources, stride=span), :]
-                put_row(j, rows, (t, pl.ds(f * sources, sources)), got.astype(BF16), out_ref, last_ref, first_ref)
-
-
-def regroup(x):
+            got = wide_ref[pl.ds(t * rows + j, fields, stride=span), :]
+            put_row(j, rows, (t,), got.astype(BF16), out_ref, last_ref, first_ref)
+    owner = owner_ref[0]
+    edges = []
+    for source in ((owner + sources - 1) % sources, (owner + 1) % sources):
+        parts = x_ref[source, pl.ds(2 * main, rows), :].astype(F32)
+        edges.append(parts[0:1] + parts[1:2] + parts[2:3])
+    edge_ref[...] = jnp.concatenate(edges, axis=0)
+
+
+def regroup(x, owner):
+    smem, vmem = pl.BlockSpec(memory_space=pltpu.SMEM), pl.BlockSpec(memory_space=pltpu.VMEM)
+    tiles = (x.shape[1] + 8) // 16
     return pl.pallas_call(
         regroup_kernel,
-        out_shape=state_shapes(8, x.shape[1] // 16, 32),
-        scratch_shapes=[pltpu.VMEM((x.shape[0] * x.shape[1], LANES), F32)],
+        out_shape=state_shapes(8, tiles, 32) + [jax.ShapeDtypeStruct((2, LANES), F32)],
+        in_specs=[smem, vmem],
+        out_specs=[vmem] * 4,
+        scratch_shapes=[pltpu.VMEM((32 * tiles * 8, LANES), F32)],
         compiler_params=pltpu.CompilerParams(vmem_limit_bytes=8 << 20),
         name="regroup",
-    )(x)
-
-
-def advance_kernel(last, move_ref, weight_ref, before_ref, now_ref, after_ref, phys_ref, bias_ref, *refs):
+    )(owner, x)
+
+
+def advance_kernel(last, param_ref, edge_ref, before_ref, now_ref, after_ref, phys_ref, bias_ref, *refs):
     rows, tiles, fields = now_ref.shape[:3]
     s_ref = refs[-1]
     s_ref[pl.ds(0, ABOVE)] = before_ref[...]
     s_ref[pl.ds(ABOVE, rows)] = now_ref[...]
     s_ref[pl.ds(ABOVE + rows, BELOW)] = after_ref[...]
+    bands = rows // BLOCK_ROWS
     lane = lax.broadcasted_iota(jnp.int32, (fields, LANES), 1)
     left_half = lane < LANES // 2
     phys = phys_ref[...]
-    bias = jnp.broadcast_to(bias_ref[...], (fields, LANES))
+    bias = jnp.broadcast_to(bias_ref[...], (LANES, fields)).T
 
     def departed(band, block, tile):
-        where = band * 7 + block
-        base = ABOVE - 2 + band * BLOCK_ROWS - move_ref[2 * where]
-        first = -move_ref[2 * where + 1] - 2
-        wr = [weight_ref[8 * where + a] for a in range(4)]
-        wc = [weight_ref[8 * where + 4 + a] for a in range(4)]
+        if 0 <= block < 5:
+            start = ((last * bands + band) * 5 + block) * PER_BLOCK
+            value = [param_ref[start + k] for k in range(PER_BLOCK)]
+        else:
+            west = block < 0
+            start = STAMP_LANE + (west * bands + band) * PER_BLOCK
+            value = [edge_ref[0 if west else 1, start + k] for k in range(PER_BLOCK)]
+        base = ABOVE - 2 + band * BLOCK_ROWS - value[0].astype(jnp.int32)
+        first = -value[1].astype(jnp.int32) - 2
+        wr, wc = value[2:6], value[6:10]
         centre, edge = [], []
         for k in range(BLOCK_ROWS + 3):
             before = s_ref[base + k, (tile + tiles - 1) % tiles].astype(F32)
@@ -327,13 +408,13 @@
             result.append(total)
         return result
 
-    for band in range(rows // BLOCK_ROWS):
+    for band in range(bands):
         for tile in range(5 if last else 6):
             if tile < 5:
-                dep = departed(band, tile + 1, tile)
+                dep = departed(band, tile, tile)
             else:
-                right = departed(band, 6, tile)
-                left = departed(band, 0, tile)
+                right = departed(band, 5, tile)
+                left = departed(band, -1, tile)
                 dep = [jnp.where(left_half, r, l) for r, l in zip(right, left)]
             low = jnp.concatenate(dep, axis=1).astype(BF16)
             forcing = jnp.dot(phys, low, preferred_element_type=F32)
@@ -347,13 +428,12 @@
                     put_row(row, rows, (tile,), value.astype(BF16), *refs[:3])
     if last:
         for f in range(fields):
-            kept = (f % 2) * (fields // 2) + f // 2
             for t in range(5):
-                got = refs[1][pl.ds(t * fields + kept, rows, stride=5 * fields), :]
+                got = refs[1][pl.ds(t * fields + f, rows, stride=5 * fields), :]
                 refs[0][f, :, pl.ds(t * LANES, LANES)] = got.astype(BF16)
 
 
-def advance(last, moves, weights, before, now, after, phys, bias):
+def advance(last, params, edges, before, now, after, phys, bias):
     rows, tiles, fields = now.shape[:3]
     smem, vmem = pl.BlockSpec(memory_space=pltpu.SMEM), pl.BlockSpec(memory_space=pltpu.VMEM)
     scratch = [pltpu.VMEM((ABOVE + rows + BELOW, tiles, fields, LANES), BF16)]
@@ -369,42 +449,7 @@
         scratch_shapes=scratch,
         compiler_params=pltpu.CompilerParams(vmem_limit_bytes=16 << 20),
         name="advance_last" if last else "advance_first",
-    )(moves, weights, before, now, after, phys, bias)
-
-
-def cubic_weights(fraction):
-    coord = 1.0 - fraction
-    return (
-        -coord * (coord - 1.0) * (coord - 2.0) / 6.0,
-        (coord + 1.0) * (coord - 1.0) * (coord - 2.0) / 2.0,
-        -(coord + 1.0) * coord * (coord - 2.0) / 2.0,
-        (coord + 1.0) * coord * (coord - 1.0) / 6.0,
-    )
-
-
-def three_parts(value):
-    high = lax.reduce_precision(value, 8, 7)
-    mid = lax.reduce_precision(value - high, 8, 7)
-    return high, mid, value - high - mid
-
-
-def edge_stamp(shift_rows, shift_cols, frac_rows, frac_cols):
-    pieces = [shift_rows.astype(F32), shift_cols.astype(F32), *three_parts(frac_rows), *three_parts(frac_cols)]
-    table = jnp.stack(pieces, axis=0)
-    edges = jnp.concatenate([table[:, :, :1], table[:, :, -1:]], axis=2)
-    flat = edges.reshape(1, -1)
-    return jnp.pad(flat, ((0, 0), (STAMP_LANE, LANES - STAMP_LANE - flat.shape[1])))
-
-
-def read_stamp(lanes, side):
-    table = lanes.astype(F32).reshape(8, 2, 2)[:, :, side : side + 1]
-    return table[0], table[1], table[2] + table[3] + table[4], table[5] + table[6] + table[7]
-
-
-def block_tables(shift_rows, shift_cols, frac_rows, frac_cols):
-    moves = jnp.stack([shift_rows, shift_cols], axis=-1).astype(jnp.int32).reshape(-1)
-    weights = jnp.stack(cubic_weights(frac_rows) + cubic_weights(frac_cols), axis=-1).reshape(-1)
-    return moves, weights
+    )(params, edges, before, now, after, phys, bias)
 
 
 def row_halos(last, first):
@@ -420,34 +465,25 @@
     bands, owners = lax.axis_size("wave"), lax.axis_size("lev")
     nlon = shift_rows.shape[2] * BLOCK_COLS * owners
     scale = 1.0 / math.sqrt(waves)
-    own_ids = lax.dynamic_slice_in_dim(wave_ids, lax.axis_index("wave") * slots, slots)
-    outgoing = legendre(spectral.reshape(slots * parts * fields, waves), own_ids, lat_rows, 8 * lats, nlon // owners - 1, 2 * nlon, scale)
+    band = lax.axis_index("wave").astype(jnp.int32).reshape(1)
+    owner = lax.axis_index("lev").astype(jnp.int32).reshape(1)
+    outgoing = legendre(
+        spectral.reshape(slots * parts * fields, waves), wave_ids, band, lat_rows, 8 * lats, nlon // owners - 1, 2 * nlon, scale
+    )
     outgoing = outgoing.reshape(bands, lats // bands, slots * parts * fields)
     arrived = lax.all_to_all(outgoing, "wave", split_axis=0, concat_axis=0, tiled=True)
-    m = wave_ids.astype(F32)[None, :]
-    table = fourier_table(m, 2 * nlon, 6)
-    stamp = edge_stamp(shift_rows[0], shift_cols[0], frac_rows[0], frac_cols[0])
-    own = (shift_rows.astype(F32), shift_cols.astype(F32), frac_rows, frac_cols)
-    second = block_tables(*[jnp.pad(o[1], ((0, 0), (1, 1))) for o in own])
-    split = (owners, fields)
-    phys = phys_weight.reshape(split + split).transpose(1, 0, 3, 2).reshape(phys_weight.shape)
-    bias = phys_bias.reshape(split).T.reshape(-1, 1)
-    arrived, second, phys, bias = lax.optimization_barrier((arrived, second, phys, bias))
+    table, m, stamp, params = fourier_table(
+        wave_ids[None, :], shift_rows, shift_cols, frac_rows, frac_cols, 2 * nlon, 6
+    )
+    bias = phys_bias[None, :]
+    arrived, params, bias = lax.optimization_barrier((arrived, params, bias))
     columns = fourier(arrived, m, stamp, table, scale)
     columns = lax.all_to_all(columns, "lev", split_axis=0, concat_axis=0, tiled=True)
-    state, *edges = regroup(columns)
-    before, after = row_halos(*edges)
-
-    me = lax.axis_index("lev")
-    stamp_row = columns.shape[1] - 16
-    size = (1, 1, 32)
-    west = lax.dynamic_slice(columns, ((me + owners - 1) % owners, stamp_row, STAMP_LANE), size)
-    east = lax.dynamic_slice(columns, ((me + 1) % owners, stamp_row, STAMP_LANE), size)
-    west, east = read_stamp(west, 1), read_stamp(east, 0)
-    first = [jnp.concatenate([w, o[0], e], axis=1) for w, o, e in zip(west, own, east)]
-    state, *edges = advance(False, *block_tables(*first), before, state, after, phys, bias)
-    before, after = row_halos(*edges)
-    return advance(True, *second, before, state, after, phys, bias)
+    state, last, first, edges = regroup(columns, owner)
+    before, after = row_halos(last, first)
+    state, last, first = advance(False, params, edges, before, state, after, phys_weight, bias)
+    before, after = row_halos(last, first)
+    return advance(True, params, edges, before, state, after, phys_weight, bias)
 
 
 def solution(mesh):

time: 92.4 us -> 88.6 us (0.959)
  other arithmetic: 9.72 us -> 0 us
  waiting for transfers between devices: 24.9 us -> 29.1 us
  local copies, waits for them, and re-layouts: 4.45 us -> 5.95 us
  Pallas kernels: 13.9 us -> 15.2 us
    all_to_all x1, waiting for transfers between devices: 1.22 us -> 6.15 us  [shards(): lax.all_to_all(outgoing, 'wave', split_axis=0, concat_axis=0, tiled=True)]
    unnamed x19 -> x0, other arithmetic: 4.25 us -> none
    convert_element_type x7 -> x0, other arithmetic: 3.54 us -> none  [the longest x2 1.37 us: shards(): own = (shift_rows.astype(F32), shift_cols.astype(F32), frac_rows, frac_cols)]
    unnamed x4 -> x14, local copies, waits for them, and re-layouts: 0.01 us -> 3.42 us
    concatenate x5 -> x0, other arithmetic: 1.57 us -> none  [the longest x4 1.49 us: shards(): jnp.concatenate([w, o[0], e], axis=1)]
    pallas_call x2, Pallas kernels: 1.39 us -> 2.76 us  [the longest x1 2.46 us: fourier_table(): pl.pallas_call(functools.partial(table_kernel, period), out_shape=[jax.Sh...]
    reshape x9 -> x1, local copies, waits for them, and re-layouts: 1.61 us -> 0.68 us  [legendre(): lat_rows.reshape(1, -1)]
  transfers between devices with their start and end apart: 6 -> 6, of which waited for: 4 -> 4; matrix products, arithmetic and copies ran while one was open for 12% -> 1% of each run, Pallas kernels for 1% -> 3%
where the time goes in v3:
time: 88.6 us; the launch traced here: 87.6 us
  starting transfers between devices  37.3 us (42%)
  waiting for transfers between devices  29.1 us (33%)
  Pallas kernels  15.2 us (17%)
  local copies, waits for them, and re-layouts  5.95 us (7%)
    all_to_all x1, starting transfers between devices, shards(): lax.all_to_all(outgoing, 'wave', split_axis=0, concat_axis=0, tiled=True)  17.9 us
    all_to_all x1, waiting for transfers between devices, shards(): lax.all_to_all(columns, 'lev', split_axis=0, concat_axis=0, tiled=True)  11.9 us
    ppermute x2, waiting for transfers between devices, row_halos(): after = lax.ppermute(first, 'wave', [(i + 1, i) for i in range(size - 1)])  10.9 us
    all_to_all x1, starting transfers between devices, shards(): lax.all_to_all(columns, 'lev', split_axis=0, concat_axis=0, tiled=True)  9.09 us
    all_to_all x1, waiting for transfers between devices, shards(): lax.all_to_all(outgoing, 'wave', split_axis=0, concat_axis=0, tiled=True)  6.15 us
    ppermute x2, starting transfers between devices, row_halos(): before = lax.ppermute(last, 'wave', [(i, i + 1) for i in range(size - 1)])  5.91 us
    pallas_call x2, Pallas kernels, advance(): pl.pallas_call(functools.partial(advance_kernel, last), out_shape=shape,...  4.54 us
    ppermute x2, starting transfers between devices, row_halos(): after = lax.ppermute(first, 'wave', [(i + 1, i) for i in range(size - 1)])  4.34 us
  transfers between devices with their start and end apart: 6, of which 4 were waited for; matrix products, arithmetic and copies ran while one was open for 1% of the time, Pallas kernels for 3%

profile of v3, /device:TPU:1, one launch (start us, length us, event | category | flops | bytes accessed | tf_op | source)
XLA Modules:
  0.0 87.6 jit_solution(14769280459686920390)
XLA Ops:
  0.0 0.7 reshape.15.lat_in_ref
  0.7 1.1 %reshape.17.x_ref = bf16[128,1536]{1,0:T(8,128)(2,1)S(1)} reshape(bf16[32,2,2,1536]{3,2,1,0:T(2,128)(2,1)} %param.9) | data formatting | bytes 786432 | tf_op jit(solution)/shard_map/reshape | solution.py:471
  1.8 0.7 copy-done.1
  2.5 3.8 %legendre.1 = bf16[384,128]{1,0:T(8,128)(2,1)} custom-call(s32[1536]{0:T(1024)S(1)} %copy-done.1, s32[1,384]{1,0:T(1,128)S(1)} %reshape.15.lat_in_ref, s32[1]{0:T(128)} %bitcast.band_ref, bf16[128,1536]{1,0:T(8,128)(2,1)S(1)} %reshape.17.x_ref), custom_call_target="tpu_custom_call" | custom-call | tf_op jit(solution)/shard_map/legendre/pallas_call | solution.py:106
  6.3 17.9 %all-to-all-start = ((bf16[48,8,128]{2,1,0:T(8,128)(2,1)}), bf16[48,8,128]{2,1,0:T(8,128)(2,1)S(1)}, u32[]{:S(2)}, u32[]{:S(2)}) async-start(bf16[48,8,128]{2,1,0:T(8,128)(2,1)} %bitcast.1), calls=%async_computation | async-start | bytes 196608 | tf_op jit(solution)/shard_map/all_to_all | solution.py:474
  24.2 0.7 broadcast_in_dim.6.ids_ref
  25.0 0.7 copy-done.3
  25.6 0.7 copy-done.4
  26.3 0.7 copy-done.5
  27.0 0.7 copy-done.6
  27.7 2.5 %fourier_table.1 = (bf16[768,1536]{1,0:T(8,128)(2,1)S(1)}, f32[1,1536]{1,0:T(1,128)S(1)}, f32[8,128]{1,0:T(8,128)S(1)}, f32[200]{0:T(256)S(1)}) custom-call(s32[1,1536]{1,0:T(1,128)S(1)} %broadcast_in_dim.6.ids_ref, s32[2,2,5]{2,1,0:T(2,128)S(1)} %copy-done.3, s32[2,2,5]{2,1,0:T(2,128)S(1)} %copy-done.4, f32[2,2,5]{2,1,0:T(2,128)S(1)} %copy-done.5, ...), custom_call_target="tpu_custom_call" | custom-call | flops 20000000 | bytes 2500000 | tf_op jit(solution)/shard_map/fourier_table/pallas_call | solution.py:218
  30.2 6.1 %all-to-all-done.z_ref = bf16[48,8,128]{2,1,0:T(8,128)(2,1)S(1)} async-done(((bf16[48,8,128]{2,1,0:T(8,128)(2,1)}), bf16[48,8,128]{2,1,0:T(8,128)(2,1)S(1)}, u32[]{:S(2)}, u32[]{:S(2)}) %all-to-all-start) | async-done | bytes 98336 | tf_op jit(solution)/shard_map/all_to_all | solution.py:474
  36.3 4.2 %fourier.1 = bf16[16,88,128]{2,1,0:T(8,128)(2,1)} custom-call(bf16[48,8,128]{2,1,0:T(8,128)(2,1)S(1)} %all-to-all-done.z_ref, f32[1,1536]{1,0:T(1,128)S(1)} %get-tuple-element.22.m_ref, f32[8,128]{1,0:T(8,128)S(1)} %get-tuple-element.23.stamp_ref, bf16[768,1536]{1,0:T(8,128)(2,1)S(1)} %get-tuple-element.24.e_ref), custom_call_target="tpu_custom_call" | custom-call | tf_op jit(solution)/shard_map/fourier/pallas_call | solution.py:302
  40.5 9.1 %all-to-all-start.1 = ((bf16[16,88,128]{2,1,0:T(8,128)(2,1)}), bf16[16,88,128]{2,1,0:T(8,128)(2,1)S(1)}, u32[]{:S(2)}, u32[]{:S(2)}) async-start(bf16[16,88,128]{2,1,0:T(8,128)(2,1)} %fourier.1), calls=%async_computation.1 | async-start | bytes 720896 | tf_op jit(solution)/shard_map/all_to_all | solution.py:481
  49.6 11.9 %all-to-all-done.1.x_ref = bf16[16,88,128]{2,1,0:T(8,128)(2,1)S(1)} async-done(((bf16[16,88,128]{2,1,0:T(8,128)(2,1)}), bf16[16,88,128]{2,1,0:T(8,128)(2,1)S(1)}, u32[]{:S(2)}, u32[]{:S(2)}) %all-to-all-start.1) | async-done | bytes 360480 | tf_op jit(solution)/shard_map/all_to_all | solution.py:481
  61.5 0.3 regroup.1
  61.8 4.0 %collective-permute-start = (bf16[6,6,32,128]{3,2,1,0:T(8,128)(2,1)S(1)}, bf16[6,6,32,128]{3,2,1,0:T(8,128)(2,1)S(1)}, u32[]{:S(2)}, u32[]{:S(2)}) collective-permute-start(bf16[6,6,32,128]{3,2,1,0:T(8,128)(2,1)S(1)} %get-tuple-element.26), channel_id=1, source_target_pairs={{0,16},{16,32},{32,48},{48,64},{64,80},{80,96},{96,112},{112,128},... | collective-permute-start | bytes 884744 | tf_op jit(solution)/shard_map/ppermute | solution.py:457
  65.8 1.9 %collective-permute-start.1 = (bf16[5,6,32,128]{3,2,1,0:T(8,128)(2,1)S(1)}, bf16[5,6,32,128]{3,2,1,0:T(8,128)(2,1)S(1)}, u32[]{:S(2)}, u32[]{:S(2)}) collective-permute-start(bf16[5,6,32,128]{3,2,1,0:T(8,128)(2,1)S(1)} %get-tuple-element.28), channel_id=1, source_target_pairs={{16,0},{32,16},{48,32},{64,48},{80,64},{96,80},{112,96},{128,112},... | collective-permute-start | bytes 737288 | tf_op jit(solution)/shard_map/ppermute | solution.py:458
  67.7 5.6 %collective-permute-done.1.after_ref = bf16[5,6,32,128]{3,2,1,0:T(8,128)(2,1)S(1)} collective-permute-done((bf16[5,6,32,128]{3,2,1,0:T(8,128)(2,1)S(1)}, bf16[5,6,32,128]{3,2,1,0:T(8,128)(2,1)S(1)}, u32[]{:S(2)}, u32[]{:S(2)}) %collective-permute-start.1) | collective-permute-done | bytes 245792 | tf_op jit(solution)/shard_map/ppermute | solution.py:458
  73.3 2.0 %advance_first.1 = (bf16[8,6,32,128]{3,2,1,0:T(8,128)(2,1)S(1)}, bf16[6,6,32,128]{3,2,1,0:T(8,128)(2,1)S(1)}, bf16[5,6,32,128]{3,2,1,0:T(8,128)(2,1)S(1)}) custom-call(f32[200]{0:T(256)S(1)} %get-tuple-element.20.param_ref, f32[2,128]{1,0:T(2,128)S(1)} %get-tuple-element.25.edge_ref, bf16[6,6,32,128]{3,2,1,0:T(8,128)(2,1)S(1)} %collective-permute-done.before_ref, ...), custom_call_target="tpu_custom_call" | custom-call | tf_op jit(solution)/shard_map/advance_first/pallas_call | solution.py:445
  75.3 1.9 %collective-permute-start.2 = (bf16[6,6,32,128]{3,2,1,0:T(8,128)(2,1)S(1)}, bf16[6,6,32,128]{3,2,1,0:T(8,128)(2,1)S(1)}, u32[]{:S(2)}, u32[]{:S(2)}) collective-permute-start(bf16[6,6,32,128]{3,2,1,0:T(8,128)(2,1)S(1)} %get-tuple-element.30), channel_id=1, source_target_pairs={{0,16},{16,32},{32,48},{48,64},{64,80},{80,96},{96,112},{112,128},... | collective-permute-start | bytes 884744 | tf_op jit(solution)/shard_map/ppermute | solution.py:457
  77.2 2.4 %collective-permute-start.3 = (bf16[5,6,32,128]{3,2,1,0:T(8,128)(2,1)S(1)}, bf16[5,6,32,128]{3,2,1,0:T(8,128)(2,1)S(1)}, u32[]{:S(2)}, u32[]{:S(2)}) collective-permute-start(bf16[5,6,32,128]{3,2,1,0:T(8,128)(2,1)S(1)} %get-tuple-element.32), channel_id=1, source_target_pairs={{16,0},{32,16},{48,32},{64,48},{80,64},{96,80},{112,96},{128,112},... | collective-permute-start | bytes 737288 | tf_op jit(solution)/shard_map/ppermute | solution.py:458
  79.7 5.4 %collective-permute-done.3.after_ref = bf16[5,6,32,128]{3,2,1,0:T(8,128)(2,1)S(1)} collective-permute-done((bf16[5,6,32,128]{3,2,1,0:T(8,128)(2,1)S(1)}, bf16[5,6,32,128]{3,2,1,0:T(8,128)(2,1)S(1)}, u32[]{:S(2)}, u32[]{:S(2)}) %collective-permute-start.3) | collective-permute-done | bytes 245792 | tf_op jit(solution)/shard_map/ppermute | solution.py:458
  85.0 2.6 %advance_last.1 = bf16[32,8,640]{2,1,0:T(8,128)(2,1)} custom-call(f32[200]{0:T(256)S(1)} %get-tuple-element.20.param_ref, f32[2,128]{1,0:T(2,128)S(1)} %get-tuple-element.25.edge_ref, bf16[6,6,32,128]{3,2,1,0:T(8,128)(2,1)S(1)} %collective-permute-done.2.before_ref, bf16[8,6,32,128]{3,2,1,0:T(8,128)(2,1)S(1)} %get-tuple-element.31.now_ref, ...), custom_call_target="tpu_custom_call" | custom-call | tf_op jit(solution)/shard_map/advance_last/pallas_call | solution.py:445
  (11 shorter events, 0.0 us)
Async XLA Ops:
  1.8 0.7 copy-start.1
  2.5 70.8 %copy-start = (bf16[32,32]{1,0:T(8,128)(2,1)S(1)}, bf16[32,32]{1,0:T(8,128)(2,1)}, u32[]{:S(2)}) copy-start(bf16[32,32]{1,0:T(8,128)(2,1)} %phys_ref.3) | copy-start | bytes 6148
  2.5 70.8 %copy-start.2 = (f32[32]{0:T(128)S(1)}, f32[32]{0:T(128)}, u32[]{:S(2)}) copy-start(f32[32]{0:T(128)} %param.17) | copy-start | bytes 388
  6.3 30.0 %all-to-all-start = ((bf16[48,8,128]{2,1,0:T(8,128)(2,1)}), bf16[48,8,128]{2,1,0:T(8,128)(2,1)S(1)}, u32[]{:S(2)}, u32[]{:S(2)}) async-start(bf16[48,8,128]{2,1,0:T(8,128)(2,1)} %bitcast.1), calls=%async_computation | async-start | bytes 196608 | tf_op jit(solution)/shard_map/all_to_all | solution.py:474
  25.0 0.7 copy-start.3
  25.6 0.7 copy-start.4
  26.3 0.7 copy-start.5
  27.0 0.7 copy-start.6
  40.5 21.1 %all-to-all-start.1 = ((bf16[16,88,128]{2,1,0:T(8,128)(2,1)}), bf16[16,88,128]{2,1,0:T(8,128)(2,1)S(1)}, u32[]{:S(2)}, u32[]{:S(2)}) async-start(bf16[16,88,128]{2,1,0:T(8,128)(2,1)} %fourier.1), calls=%async_computation.1 | async-start | bytes 720896 | tf_op jit(solution)/shard_map/all_to_all | solution.py:481
  61.8 11.5 %collective-permute-start = (bf16[6,6,32,128]{3,2,1,0:T(8,128)(2,1)S(1)}, bf16[6,6,32,128]{3,2,1,0:T(8,128)(2,1)S(1)}, u32[]{:S(2)}, u32[]{:S(2)}) collective-permute-start(bf16[6,6,32,128]{3,2,1,0:T(8,128)(2,1)S(1)} %get-tuple-element.26), channel_id=1, source_target_pairs={{0,16},{16,32},{32,48},{48,64},{64,80},{80,96},{96,112},{112,128},... | collective-permute-start | bytes 884744 | tf_op jit(solution)/shard_map/ppermute | solution.py:457
  65.8 7.5 %collective-permute-start.1 = (bf16[5,6,32,128]{3,2,1,0:T(8,128)(2,1)S(1)}, bf16[5,6,32,128]{3,2,1,0:T(8,128)(2,1)S(1)}, u32[]{:S(2)}, u32[]{:S(2)}) collective-permute-start(bf16[5,6,32,128]{3,2,1,0:T(8,128)(2,1)S(1)} %get-tuple-element.28), channel_id=1, source_target_pairs={{16,0},{32,16},{48,32},{64,48},{80,64},{96,80},{112,96},{128,112},... | collective-permute-start | bytes 737288 | tf_op jit(solution)/shard_map/ppermute | solution.py:458
  75.3 9.7 %collective-permute-start.2 = (bf16[6,6,32,128]{3,2,1,0:T(8,128)(2,1)S(1)}, bf16[6,6,32,128]{3,2,1,0:T(8,128)(2,1)S(1)}, u32[]{:S(2)}, u32[]{:S(2)}) collective-permute-start(bf16[6,6,32,128]{3,2,1,0:T(8,128)(2,1)S(1)} %get-tuple-element.30), channel_id=1, source_target_pairs={{0,16},{16,32},{32,48},{48,64},{64,80},{80,96},{96,112},{112,128},... | collective-permute-start | bytes 884744 | tf_op jit(solution)/shard_map/ppermute | solution.py:457
  77.2 7.8 %collective-permute-start.3 = (bf16[5,6,32,128]{3,2,1,0:T(8,128)(2,1)S(1)}, bf16[5,6,32,128]{3,2,1,0:T(8,128)(2,1)S(1)}, u32[]{:S(2)}, u32[]{:S(2)}) collective-permute-start(bf16[5,6,32,128]{3,2,1,0:T(8,128)(2,1)S(1)} %get-tuple-element.32), channel_id=1, source_target_pairs={{16,0},{32,16},{48,32},{64,48},{80,64},{96,80},{112,96},{128,112},... | collective-permute-start | bytes 737288 | tf_op jit(solution)/shard_map/ppermute | solution.py:458

commit v4 on v3

--- a/solution.py
+++ b/solution.py
@@ -11,8 +11,7 @@
 BLOCK_ROWS = 4
 BLOCK_COLS = 128
 LANES = 128
-ABOVE = 6
-BELOW = 5
+REACH = 6
 HALO = 16
 STAMP_LANE = 4 * HALO
 PER_BLOCK = 10
@@ -45,79 +44,104 @@
 
 
 def legendre_kernel(
-    period, middle, turn, scale, ids_ref, lat_in_ref, band_ref, x_ref, out_ref, cos_ref, sin_ref, cw_ref, sw_ref, lat_ref
+    period, middle, turn, scale, ids_hbm, lat_hbm, band_ref, x_hbm, out_ref, cos_ref, sin_ref, cw_ref, sw_ref, lat_ref,
+    ids_ref, lat_in_ref, x_ref, sems,
 ):
-    rows, waves = x_ref.shape
+    loads = [
+        pltpu.make_async_copy(src, dst, sems.at[i])
+        for i, (src, dst) in enumerate(((ids_hbm, ids_ref), (lat_hbm, lat_in_ref), (x_hbm, x_ref)))
+    ]
+    for load in loads:
+        load.start()
+    rows, waves = 4 * x_ref.shape[0], x_ref.shape[3]
+    half = waves // 2
     lats = out_ref.shape[0]
     slots = rows // 4
     step = 32
     lane = lax.broadcasted_iota(jnp.int32, (1, LANES), 1)
     first = band_ref[0] * slots
+    loads[0].wait()
     m_row = jnp.zeros((1, LANES), jnp.int32)
     for s in range(slots):
         m_row = jnp.where(lane // 4 == s, ids_ref[first + s], m_row)
-    m_col = down(m_row.astype(F32))
     m_row = m_row.astype(F32)
+    loads[1].wait()
     for i in range(lats // LANES):
-        lat_ref[pl.ds(i * LANES, LANES), :] = down(lat_in_ref[:, pl.ds(i * LANES, LANES)].astype(F32))
-    wide_lane = lax.broadcasted_iota(jnp.int32, (step, LANES), 1).astype(F32)
-    wide_m = jnp.broadcast_to(m_row, (step, LANES))
+        row = lat_in_ref[pl.ds(i * LANES, LANES)].astype(F32).reshape(1, LANES)
+        lat_ref[pl.ds(i * LANES, LANES), :] = down(row)
+    odd = 2.0 * lax.broadcasted_iota(jnp.int32, (step, LANES), 1).astype(F32) + 1.0
+    centre = jnp.broadcast_to(2.0 * m_row + float(waves - 1), (step, LANES))
 
     def fill(i, carry):
         at = pl.ds(pl.multiple_of(i * step, step), step)
         lat = lat_ref[at, :]
-        cw, sw = sincos(lat * wide_m, period)
+        cw, sw = sincos(lat * centre, 2 * period)
         cw_ref[at, :] = cw
         sw_ref[at, :] = sw
-        c, s = sincos(lat * wide_lane, period)
+        c, s = sincos(lat * odd, 2 * period)
         rc, rs = sincos(lat * float(LANES), period)
-        for a in range(waves // LANES):
+        for a in range(half // LANES):
             cols = pl.ds(a * LANES, LANES)
             cos_ref[at, cols] = c.astype(BF16)
             sin_ref[at, cols] = s.astype(BF16)
-            if a + 1 < waves // LANES:
+            if a + 1 < half // LANES:
                 c, s = rotate(c, s, rc, rs)
         return carry
 
     lax.fori_loop(0, lats // step, fill, 0)
+    loads[2].wait()
+    m_col = down(m_row)
+    k = lax.broadcasted_iota(jnp.int32, (rows, LANES), 1).astype(F32)
     kept = []
-    k = lax.broadcasted_iota(jnp.int32, (rows, LANES), 1).astype(F32)
     for a in range(waves // LANES):
-        part = x_ref[:, pl.ds(a * LANES, LANES)].astype(F32)
+        part = x_ref[:, :, :, pl.ds(a * LANES, LANES)].astype(F32).reshape(rows, LANES)
         kept.append(jnp.where(k < (waves - a * LANES) - m_col, part, 0.0).astype(BF16))
-    x = jnp.concatenate(kept, axis=1)
-    p0 = lax.dot_general(cos_ref[...], x, NT, preferred_element_type=F32)
-    p1 = lax.dot_general(sin_ref[...], x, NT, preferred_element_type=F32)
-    leg = (cw_ref[...] * p0 - sw_ref[...] * p1) * scale
+    src = lax.broadcasted_iota(jnp.int32, (rows, rows), 0)
+    dst = lax.broadcasted_iota(jnp.int32, (rows, rows), 1)
+    flip = jnp.where(src + dst == LANES - 1, 1.0, 0.0).astype(BF16)
+    count = half // LANES
+    upper = jnp.concatenate(kept[count:], axis=1)
+    lower = jnp.concatenate(
+        [jnp.dot(part, flip, preferred_element_type=F32).astype(BF16) for part in kept[count - 1 :: -1]], axis=1
+    )
+    both = jnp.concatenate([upper, lower], axis=0)
+    even = lax.dot_general(cos_ref[...], both, NT, preferred_element_type=F32)
+    odds = lax.dot_general(sin_ref[...], both, NT, preferred_element_type=F32)
+    even = even[:, :rows] + even[:, rows:]
+    odds = odds[:, :rows] - odds[:, rows:]
+    leg = (cw_ref[...] * even - sw_ref[...] * odds) * scale
     cos, sin = sincos(m_row * float(middle), turn)
     real = lane % 4 < 2
     other = jnp.where(real, pltpu.roll(leg, LANES - 2, 1), pltpu.roll(leg, 2, 1))
     leg = (leg * cos + other * jnp.where(real, -sin, sin)).astype(BF16)
-    src = lax.broadcasted_iota(jnp.int32, (rows, rows), 0)
-    dst = lax.broadcasted_iota(jnp.int32, (rows, rows), 1)
     order = jnp.where((src % 4) * slots + src // 4 == dst, 1.0, 0.0).astype(BF16)
     out_ref[...] = jnp.dot(leg, order, preferred_element_type=F32).astype(BF16)
 
 
 def legendre(x, wave_ids, band, lat_rows, period, middle, turn, scale):
-    rows, waves = x.shape
+    rows, waves = 4 * x.shape[0], x.shape[3]
     lats = lat_rows.shape[0]
-    smem, vmem = pl.BlockSpec(memory_space=pltpu.SMEM), pl.BlockSpec(memory_space=pltpu.VMEM)
+    hbm, smem = pl.BlockSpec(memory_space=pltpu.HBM), pl.BlockSpec(memory_space=pltpu.SMEM)
+    vmem = pl.BlockSpec(memory_space=pltpu.VMEM)
     return pl.pallas_call(
         functools.partial(legendre_kernel, period, middle, turn, scale),
         out_shape=jax.ShapeDtypeStruct((lats, rows), BF16),
-        in_specs=[smem, vmem, smem, vmem],
+        in_specs=[hbm, hbm, smem, hbm],
         out_specs=vmem,
         scratch_shapes=[
-            pltpu.VMEM((lats, waves), BF16),
-            pltpu.VMEM((lats, waves), BF16),
+            pltpu.VMEM((lats, waves // 2), BF16),
+            pltpu.VMEM((lats, waves // 2), BF16),
             pltpu.VMEM((lats, LANES), F32),
             pltpu.VMEM((lats, LANES), F32),
             pltpu.VMEM((lats, LANES), F32),
+            pltpu.SMEM(wave_ids.shape, jnp.int32),
+            pltpu.VMEM(lat_rows.shape, jnp.int32),
+            pltpu.VMEM(x.shape, BF16),
+            pltpu.SemaphoreType.DMA((3,)),
         ],
-        compiler_params=pltpu.CompilerParams(vmem_limit_bytes=24 << 20),
+        compiler_params=pltpu.CompilerParams(vmem_limit_bytes=67043328),
         name="legendre",
-    )(wave_ids, lat_rows.reshape(1, -1), band, x)
+    )(wave_ids, lat_rows, band, x)
 
 
 def times_i(z, power):
@@ -314,19 +338,19 @@
     )(z, m, stamp, table)
 
 
-def put_row(row, rows, at, value, out_ref, last_ref, first_ref):
-    out_ref[(row, *at)] = value
-    if row >= rows - ABOVE:
-        last_ref[(row - rows + ABOVE, *at)] = value
-    if row < BELOW:
-        first_ref[(row, *at)] = value
+def sent_start(rows, odd, side):
+    return odd * (rows - REACH) if side else (1 - odd) * (rows - REACH)
+
+
+def got_start(rows, odd, side):
+    return odd * (rows + REACH) if side else (1 - odd) * (rows + REACH)
 
 
 def state_shapes(rows, tiles, fields):
-    return [jax.ShapeDtypeStruct((n, tiles, fields, LANES), BF16) for n in (rows, ABOVE, BELOW)]
-
-
-def regroup_kernel(owner_ref, x_ref, out_ref, last_ref, first_ref, edge_ref, wide_ref):
+    return [jax.ShapeDtypeStruct((n, tiles, fields, LANES), BF16) for n in (rows, REACH, REACH)]
+
+
+def regroup_kernel(owner_ref, odd_ref, x_ref, out_ref, near_ref, far_ref, edge_ref, wide_ref):
     rows, tiles, fields = out_ref.shape[:3]
     sources = x_ref.shape[0]
     main, span = (tiles - 1) * rows, tiles * rows
@@ -339,7 +363,9 @@
     for j in range(rows):
         for t in range(tiles):
             got = wide_ref[pl.ds(t * rows + j, fields, stride=span), :]
-            put_row(j, rows, (t,), got.astype(BF16), out_ref, last_ref, first_ref)
+            out_ref[j, t] = got.astype(BF16)
+    for side, ref in enumerate((near_ref, far_ref)):
+        ref[...] = out_ref[pl.ds(sent_start(rows, odd_ref[0], side), REACH)]
     owner = owner_ref[0]
     edges = []
     for source in ((owner + sources - 1) % sources, (owner + 1) % sources):
@@ -348,26 +374,27 @@
     edge_ref[...] = jnp.concatenate(edges, axis=0)
 
 
-def regroup(x, owner):
+def regroup(x, owner, odd):
     smem, vmem = pl.BlockSpec(memory_space=pltpu.SMEM), pl.BlockSpec(memory_space=pltpu.VMEM)
     tiles = (x.shape[1] + 8) // 16
     return pl.pallas_call(
         regroup_kernel,
         out_shape=state_shapes(8, tiles, 32) + [jax.ShapeDtypeStruct((2, LANES), F32)],
-        in_specs=[smem, vmem],
+        in_specs=[smem, smem, vmem],
         out_specs=[vmem] * 4,
         scratch_shapes=[pltpu.VMEM((32 * tiles * 8, LANES), F32)],
         compiler_params=pltpu.CompilerParams(vmem_limit_bytes=8 << 20),
         name="regroup",
-    )(owner, x)
-
-
-def advance_kernel(last, param_ref, edge_ref, before_ref, now_ref, after_ref, phys_ref, bias_ref, *refs):
+    )(owner, odd, x)
+
+
+def advance_kernel(last, param_ref, edge_ref, odd_ref, near_ref, now_ref, far_ref, phys_ref, bias_ref, *refs):
     rows, tiles, fields = now_ref.shape[:3]
     s_ref = refs[-1]
-    s_ref[pl.ds(0, ABOVE)] = before_ref[...]
-    s_ref[pl.ds(ABOVE, rows)] = now_ref[...]
-    s_ref[pl.ds(ABOVE + rows, BELOW)] = after_ref[...]
+    odd = odd_ref[0]
+    s_ref[pl.ds(REACH, rows)] = now_ref[...]
+    for side, ref in enumerate((near_ref, far_ref)):
+        s_ref[pl.ds(got_start(rows, odd, side), REACH)] = ref[...]
     bands = rows // BLOCK_ROWS
     lane = lax.broadcasted_iota(jnp.int32, (fields, LANES), 1)
     left_half = lane < LANES // 2
@@ -382,7 +409,7 @@
             west = block < 0
             start = STAMP_LANE + (west * bands + band) * PER_BLOCK
             value = [edge_ref[0 if west else 1, start + k] for k in range(PER_BLOCK)]
-        base = ABOVE - 2 + band * BLOCK_ROWS - value[0].astype(jnp.int32)
+        base = REACH - 2 + band * BLOCK_ROWS - value[0].astype(jnp.int32)
         first = -value[1].astype(jnp.int32) - 2
         wr, wc = value[2:6], value[6:10]
         centre, edge = [], []
@@ -425,7 +452,10 @@
                 if last:
                     refs[1][pl.ds((row * 5 + tile) * fields, fields), :] = value
                 else:
-                    put_row(row, rows, (tile,), value.astype(BF16), *refs[:3])
+                    refs[0][row, tile] = value.astype(BF16)
+    if not last:
+        for side in range(2):
+            refs[1 + side][...] = refs[0][pl.ds(sent_start(rows, odd, side), REACH)]
     if last:
         for f in range(fields):
             for t in range(5):
@@ -433,10 +463,10 @@
                 refs[0][f, :, pl.ds(t * LANES, LANES)] = got.astype(BF16)
 
 
-def advance(last, params, edges, before, now, after, phys, bias):
+def advance(last, params, edges, odd, near, now, far, phys, bias):
     rows, tiles, fields = now.shape[:3]
     smem, vmem = pl.BlockSpec(memory_space=pltpu.SMEM), pl.BlockSpec(memory_space=pltpu.VMEM)
-    scratch = [pltpu.VMEM((ABOVE + rows + BELOW, tiles, fields, LANES), BF16)]
+    scratch = [pltpu.VMEM((rows + 2 * REACH, tiles, fields, LANES), BF16)]
     if last:
         shape = jax.ShapeDtypeStruct((fields, rows, 5 * LANES), BF16)
         scratch.insert(0, pltpu.VMEM((rows * 5 * fields, LANES), F32))
@@ -445,18 +475,19 @@
     return pl.pallas_call(
         functools.partial(advance_kernel, last),
         out_shape=shape,
-        in_specs=[smem, smem] + [vmem] * 5,
+        in_specs=[smem] * 3 + [vmem] * 5,
         scratch_shapes=scratch,
         compiler_params=pltpu.CompilerParams(vmem_limit_bytes=16 << 20),
         name="advance_last" if last else "advance_first",
-    )(params, edges, before, now, after, phys, bias)
-
-
-def row_halos(last, first):
+    )(params, edges, odd, near, now, far, phys, bias)
+
+
+def row_halos(near, far):
     size = lax.axis_size("wave")
-    before = lax.ppermute(last, "wave", [(i, i + 1) for i in range(size - 1)])
-    after = lax.ppermute(first, "wave", [(i + 1, i) for i in range(size - 1)])
-    return before, after
+    pairs = [(i + d, i + 1 - d) for i in range(size - 1) for d in (0, 1)]
+    far = lax.ppermute(far, "wave", [p for p in pairs if min(p) % 2])
+    near = lax.ppermute(near, "wave", [p for p in pairs if not min(p) % 2])
+    return near, far
 
 
 def shards(spectral, wave_ids, lat_rows, shift_rows, shift_cols, frac_rows, frac_cols, phys_weight, phys_bias):
@@ -468,7 +499,7 @@
     band = lax.axis_index("wave").astype(jnp.int32).reshape(1)
     owner = lax.axis_index("lev").astype(jnp.int32).reshape(1)
     outgoing = legendre(
-        spectral.reshape(slots * parts * fields, waves), wave_ids, band, lat_rows, 8 * lats, nlon // owners - 1, 2 * nlon, scale
+        spectral, wave_ids, band, lat_rows, 8 * lats, nlon // owners - 1, 2 * nlon, scale
     )
     outgoing = outgoing.reshape(bands, lats // bands, slots * parts * fields)
     arrived = lax.all_to_all(outgoing, "wave", split_axis=0, concat_axis=0, tiled=True)
@@ -479,11 +510,12 @@
     arrived, params, bias = lax.optimization_barrier((arrived, params, bias))
     columns = fourier(arrived, m, stamp, table, scale)
     columns = lax.all_to_all(columns, "lev", split_axis=0, concat_axis=0, tiled=True)
-    state, last, first, edges = regroup(columns, owner)
-    before, after = row_halos(last, first)
-    state, last, first = advance(False, params, edges, before, state, after, phys_weight, bias)
-    before, after = row_halos(last, first)
-    return advance(True, params, edges, before, state, after, phys_weight, bias)
+    odd = band % 2
+    state, near, far, edges = regroup(columns, owner, odd)
+    near, far = row_halos(near, far)
+    state, near, far = advance(False, params, edges, odd, near, state, far, phys_weight, bias)
+    near, far = row_halos(near, far)
+    return advance(True, params, edges, odd, near, state, far, phys_weight, bias)
 
 
 def solution(mesh):

time: 88.6 us -> 90.6 us (1.023)
  waiting for transfers between devices: 29.1 us -> 31.7 us
  local copies, waits for them, and re-layouts: 5.95 us -> 3.44 us
  starting transfers between devices: 37.3 us -> 39.5 us
    ppermute x4, waiting for transfers between devices: 11 us -> 13.6 us  [the longest x2 13.6 us: row_halos(): far = lax.ppermute(far, 'wave', [p for p in pairs if min(p) % 2])]
    ppermute x4, starting transfers between devices: 10.3 us -> 12.5 us  [the longest x2 6.31 us: row_halos(): far = lax.ppermute(far, 'wave', [p for p in pairs if min(p) % 2])]
    reshape x2 -> x0, local copies, waits for them, and re-layouts: 1.83 us -> none  [the longest x1 1.14 us: shards(): spectral.reshape(slots * parts * fields, waves)]
    unnamed x14 -> x12, local copies, waits for them, and re-layouts: 3.42 us -> 2.74 us
where the time goes in v4:
time: 90.6 us; the launch traced here: 89.9 us
  starting transfers between devices  39.5 us (44%)
  waiting for transfers between devices  31.7 us (35%)
  Pallas kernels  15.1 us (17%)
  local copies, waits for them, and re-layouts  3.44 us (4%)
    all_to_all x1, starting transfers between devices, shards(): lax.all_to_all(outgoing, 'wave', split_axis=0, concat_axis=0, tiled=True)  17.9 us
    ppermute x2, waiting for transfers between devices, row_halos(): far = lax.ppermute(far, 'wave', [p for p in pairs if min(p) % 2])  13.6 us
    all_to_all x1, waiting for transfers between devices, shards(): lax.all_to_all(columns, 'lev', split_axis=0, concat_axis=0, tiled=True)  12 us
    all_to_all x1, starting transfers between devices, shards(): lax.all_to_all(columns, 'lev', split_axis=0, concat_axis=0, tiled=True)  9.09 us
    ppermute x2, starting transfers between devices, row_halos(): far = lax.ppermute(far, 'wave', [p for p in pairs if min(p) % 2])  6.31 us
    ppermute x2, starting transfers between devices, row_halos(): near = lax.ppermute(near, 'wave', [p for p in pairs if not min(p) % 2])  6.23 us
    all_to_all x1, waiting for transfers between devices, shards(): lax.all_to_all(outgoing, 'wave', split_axis=0, concat_axis=0, tiled=True)  6.15 us
    pallas_call x2, Pallas kernels, advance(): pl.pallas_call(functools.partial(advance_kernel, last), out_shape=shape,...  4.58 us
  transfers between devices with their start and end apart: 6, of which 4 were waited for; matrix products, arithmetic and copies ran while one was open for 1% of the time, Pallas kernels for 3%

profile of v4, /device:TPU:1, one launch (start us, length us, event | category | flops | bytes accessed | tf_op | source)
XLA Modules:
  0.0 89.9 jit_solution(13948935109495474643)
XLA Ops:
  0.0 3.6 %legendre.1 = bf16[384,128]{1,0:T(8,128)(2,1)} custom-call(s32[1536]{0:T(1024)} %ids_hbm.1, s32[384]{0:T(512)} %lat_hbm.1, s32[1]{0:T(128)} %bitcast.band_ref, bf16[32,2,2,1536]{3,2,1,0:T(2,128)(2,1)} %x_hbm.1), custom_call_target="tpu_custom_call" | custom-call | tf_op jit(solution)/shard_map/legendre/pallas_call | solution.py:126
  3.6 0.0 copy-start
  3.6 0.0 copy-start.1
  3.6 17.9 %all-to-all-start = ((bf16[48,8,128]{2,1,0:T(8,128)(2,1)}), bf16[48,8,128]{2,1,0:T(8,128)(2,1)S(1)}, u32[]{:S(2)}, u32[]{:S(2)}) async-start(bf16[48,8,128]{2,1,0:T(8,128)(2,1)} %bitcast.6), calls=%async_computation | async-start | bytes 196608 | tf_op jit(solution)/shard_map/all_to_all | solution.py:505
  21.5 0.7 broadcast_in_dim.6.ids_ref
  22.2 0.7 copy-done.2
  22.9 0.7 copy-done.3
  23.6 0.7 copy-done.4
  24.3 0.7 copy-done.5
  25.0 2.5 %fourier_table.1 = (bf16[768,1536]{1,0:T(8,128)(2,1)S(1)}, f32[1,1536]{1,0:T(1,128)S(1)}, f32[8,128]{1,0:T(8,128)S(1)}, f32[200]{0:T(256)S(1)}) custom-call(s32[1,1536]{1,0:T(1,128)S(1)} %broadcast_in_dim.6.ids_ref, s32[2,2,5]{2,1,0:T(2,128)S(1)} %copy-done.2, s32[2,2,5]{2,1,0:T(2,128)S(1)} %copy-done.3, f32[2,2,5]{2,1,0:T(2,128)S(1)} %copy-done.4, ...), custom_call_target="tpu_custom_call" | custom-call | flops 20000000 | bytes 2500000 | tf_op jit(solution)/shard_map/fourier_table/pallas_call | solution.py:242
  27.4 6.1 %all-to-all-done.z_ref = bf16[48,8,128]{2,1,0:T(8,128)(2,1)S(1)} async-done(((bf16[48,8,128]{2,1,0:T(8,128)(2,1)}), bf16[48,8,128]{2,1,0:T(8,128)(2,1)S(1)}, u32[]{:S(2)}, u32[]{:S(2)}) %all-to-all-start) | async-done | bytes 98336 | tf_op jit(solution)/shard_map/all_to_all | solution.py:505
  33.6 4.2 %fourier.1 = bf16[16,88,128]{2,1,0:T(8,128)(2,1)} custom-call(bf16[48,8,128]{2,1,0:T(8,128)(2,1)S(1)} %all-to-all-done.z_ref, f32[1,1536]{1,0:T(1,128)S(1)} %get-tuple-element.22.m_ref, f32[8,128]{1,0:T(8,128)S(1)} %get-tuple-element.23.stamp_ref, bf16[768,1536]{1,0:T(8,128)(2,1)S(1)} %get-tuple-element.24.e_ref), custom_call_target="tpu_custom_call" | custom-call | tf_op jit(solution)/shard_map/fourier/pallas_call | solution.py:326
  37.8 9.1 %all-to-all-start.1 = ((bf16[16,88,128]{2,1,0:T(8,128)(2,1)}), bf16[16,88,128]{2,1,0:T(8,128)(2,1)S(1)}, u32[]{:S(2)}, u32[]{:S(2)}) async-start(bf16[16,88,128]{2,1,0:T(8,128)(2,1)} %fourier.1), calls=%async_computation.1 | async-start | bytes 720896 | tf_op jit(solution)/shard_map/all_to_all | solution.py:512
  46.9 12.0 %all-to-all-done.1.x_ref = bf16[16,88,128]{2,1,0:T(8,128)(2,1)S(1)} async-done(((bf16[16,88,128]{2,1,0:T(8,128)(2,1)}), bf16[16,88,128]{2,1,0:T(8,128)(2,1)S(1)}, u32[]{:S(2)}, u32[]{:S(2)}) %all-to-all-start.1) | async-done | bytes 360480 | tf_op jit(solution)/shard_map/all_to_all | solution.py:512
  58.8 0.3 regroup.1
  59.1 4.3 %collective-permute-start = (bf16[6,6,32,128]{3,2,1,0:T(8,128)(2,1)S(1)}, bf16[6,6,32,128]{3,2,1,0:T(8,128)(2,1)S(1)}, u32[]{:S(2)}, u32[]{:S(2)}) collective-permute-start(bf16[6,6,32,128]{3,2,1,0:T(8,128)(2,1)S(1)} %get-tuple-element.26), channel_id=1, source_target_pairs={{0,16},{16,0},{32,48},{48,32},{64,80},{80,64},{96,112},{112,96},{1... | collective-permute-start | bytes 884744 | tf_op jit(solution)/shard_map/ppermute | solution.py:489
  63.5 1.9 %collective-permute-start.1 = (bf16[6,6,32,128]{3,2,1,0:T(8,128)(2,1)S(1)}, bf16[6,6,32,128]{3,2,1,0:T(8,128)(2,1)S(1)}, u32[]{:S(2)}, u32[]{:S(2)}) collective-permute-start(bf16[6,6,32,128]{3,2,1,0:T(8,128)(2,1)S(1)} %get-tuple-element.28), channel_id=1, source_target_pairs={{16,32},{32,16},{48,64},{64,48},{80,96},{96,80},{112,128},{128,112... | collective-permute-start | bytes 884744 | tf_op jit(solution)/shard_map/ppermute | solution.py:488
  65.4 6.8 %collective-permute-done.1.far_ref = bf16[6,6,32,128]{3,2,1,0:T(8,128)(2,1)S(1)} collective-permute-done((bf16[6,6,32,128]{3,2,1,0:T(8,128)(2,1)S(1)}, bf16[6,6,32,128]{3,2,1,0:T(8,128)(2,1)S(1)}, u32[]{:S(2)}, u32[]{:S(2)}) %collective-permute-start.1) | collective-permute-done | bytes 294944 | tf_op jit(solution)/shard_map/ppermute | solution.py:488
  72.2 2.0 %advance_first.1 = (bf16[8,6,32,128]{3,2,1,0:T(8,128)(2,1)S(1)}, bf16[6,6,32,128]{3,2,1,0:T(8,128)(2,1)S(1)}, bf16[6,6,32,128]{3,2,1,0:T(8,128)(2,1)S(1)}) custom-call(f32[200]{0:T(256)S(1)} %get-tuple-element.20.param_ref, f32[2,128]{1,0:T(2,128)S(1)} %get-tuple-element.25.edge_ref, s32[1]{0:T(128)S(6)} %select_n.7.odd_ref, ...), custom_call_target="tpu_custom_call" | custom-call | tf_op jit(solution)/shard_map/advance_first/pallas_call | solution.py:475
  74.2 1.9 %collective-permute-start.2 = (bf16[6,6,32,128]{3,2,1,0:T(8,128)(2,1)S(1)}, bf16[6,6,32,128]{3,2,1,0:T(8,128)(2,1)S(1)}, u32[]{:S(2)}, u32[]{:S(2)}) collective-permute-start(bf16[6,6,32,128]{3,2,1,0:T(8,128)(2,1)S(1)} %get-tuple-element.30), channel_id=1, source_target_pairs={{0,16},{16,0},{32,48},{48,32},{64,80},{80,64},{96,112},{112,96},{1... | collective-permute-start | bytes 884744 | tf_op jit(solution)/shard_map/ppermute | solution.py:489
  76.1 4.4 %collective-permute-start.3 = (bf16[6,6,32,128]{3,2,1,0:T(8,128)(2,1)S(1)}, bf16[6,6,32,128]{3,2,1,0:T(8,128)(2,1)S(1)}, u32[]{:S(2)}, u32[]{:S(2)}) collective-permute-start(bf16[6,6,32,128]{3,2,1,0:T(8,128)(2,1)S(1)} %get-tuple-element.32), channel_id=1, source_target_pairs={{16,32},{32,16},{48,64},{64,48},{80,96},{96,80},{112,128},{128,112... | collective-permute-start | bytes 884744 | tf_op jit(solution)/shard_map/ppermute | solution.py:488
  80.5 0.0 collective-permute-done.2.near_ref
  80.6 6.8 %collective-permute-done.3.far_ref = bf16[6,6,32,128]{3,2,1,0:T(8,128)(2,1)S(1)} collective-permute-done((bf16[6,6,32,128]{3,2,1,0:T(8,128)(2,1)S(1)}, bf16[6,6,32,128]{3,2,1,0:T(8,128)(2,1)S(1)}, u32[]{:S(2)}, u32[]{:S(2)}) %collective-permute-start.3) | collective-permute-done | bytes 294944 | tf_op jit(solution)/shard_map/ppermute | solution.py:488
  87.4 2.6 %advance_last.1 = bf16[32,8,640]{2,1,0:T(8,128)(2,1)} custom-call(f32[200]{0:T(256)S(1)} %get-tuple-element.20.param_ref, f32[2,128]{1,0:T(2,128)S(1)} %get-tuple-element.25.edge_ref, s32[1]{0:T(128)S(6)} %select_n.7.odd_ref, bf16[6,6,32,128]{3,2,1,0:T(8,128)(2,1)S(1)} %collective-permute-done.2.near_ref, ...), custom_call_target="tpu_custom_call" | custom-call | tf_op jit(solution)/shard_map/advance_last/pallas_call | solution.py:475
  (7 shorter events, 0.0 us)
Async XLA Ops:
  3.6 68.6 %copy-start = (bf16[32,32]{1,0:T(8,128)(2,1)S(1)}, bf16[32,32]{1,0:T(8,128)(2,1)}, u32[]{:S(2)}) copy-start(bf16[32,32]{1,0:T(8,128)(2,1)} %phys_ref.3) | copy-start | bytes 6148
  3.6 68.6 %copy-start.1 = (f32[32]{0:T(128)S(1)}, f32[32]{0:T(128)}, u32[]{:S(2)}) copy-start(f32[32]{0:T(128)} %param.17) | copy-start | bytes 388
  3.6 30.0 %all-to-all-start = ((bf16[48,8,128]{2,1,0:T(8,128)(2,1)}), bf16[48,8,128]{2,1,0:T(8,128)(2,1)S(1)}, u32[]{:S(2)}, u32[]{:S(2)}) async-start(bf16[48,8,128]{2,1,0:T(8,128)(2,1)} %bitcast.6), calls=%async_computation | async-start | bytes 196608 | tf_op jit(solution)/shard_map/all_to_all | solution.py:505
  22.2 0.7 copy-start.2
  22.9 0.7 copy-start.3
  23.6 0.7 copy-start.4
  24.3 0.7 copy-start.5
  37.8 21.1 %all-to-all-start.1 = ((bf16[16,88,128]{2,1,0:T(8,128)(2,1)}), bf16[16,88,128]{2,1,0:T(8,128)(2,1)S(1)}, u32[]{:S(2)}, u32[]{:S(2)}) async-start(bf16[16,88,128]{2,1,0:T(8,128)(2,1)} %fourier.1), calls=%async_computation.1 | async-start | bytes 720896 | tf_op jit(solution)/shard_map/all_to_all | solution.py:512
  59.1 6.2 %collective-permute-start = (bf16[6,6,32,128]{3,2,1,0:T(8,128)(2,1)S(1)}, bf16[6,6,32,128]{3,2,1,0:T(8,128)(2,1)S(1)}, u32[]{:S(2)}, u32[]{:S(2)}) collective-permute-start(bf16[6,6,32,128]{3,2,1,0:T(8,128)(2,1)S(1)} %get-tuple-element.26), channel_id=1, source_target_pairs={{0,16},{16,0},{32,48},{48,32},{64,80},{80,64},{96,112},{112,96},{1... | collective-permute-start | bytes 884744 | tf_op jit(solution)/shard_map/ppermute | solution.py:489
  63.5 8.7 %collective-permute-start.1 = (bf16[6,6,32,128]{3,2,1,0:T(8,128)(2,1)S(1)}, bf16[6,6,32,128]{3,2,1,0:T(8,128)(2,1)S(1)}, u32[]{:S(2)}, u32[]{:S(2)}) collective-permute-start(bf16[6,6,32,128]{3,2,1,0:T(8,128)(2,1)S(1)} %get-tuple-element.28), channel_id=1, source_target_pairs={{16,32},{32,16},{48,64},{64,48},{80,96},{96,80},{112,128},{128,112... | collective-permute-start | bytes 884744 | tf_op jit(solution)/shard_map/ppermute | solution.py:488
  74.2 6.3 %collective-permute-start.2 = (bf16[6,6,32,128]{3,2,1,0:T(8,128)(2,1)S(1)}, bf16[6,6,32,128]{3,2,1,0:T(8,128)(2,1)S(1)}, u32[]{:S(2)}, u32[]{:S(2)}) collective-permute-start(bf16[6,6,32,128]{3,2,1,0:T(8,128)(2,1)S(1)} %get-tuple-element.30), channel_id=1, source_target_pairs={{0,16},{16,0},{32,48},{48,32},{64,80},{80,64},{96,112},{112,96},{1... | collective-permute-start | bytes 884744 | tf_op jit(solution)/shard_map/ppermute | solution.py:489
  76.1 11.2 %collective-permute-start.3 = (bf16[6,6,32,128]{3,2,1,0:T(8,128)(2,1)S(1)}, bf16[6,6,32,128]{3,2,1,0:T(8,128)(2,1)S(1)}, u32[]{:S(2)}, u32[]{:S(2)}) collective-permute-start(bf16[6,6,32,128]{3,2,1,0:T(8,128)(2,1)S(1)} %get-tuple-element.32), channel_id=1, source_target_pairs={{16,32},{32,16},{48,64},{64,48},{80,96},{96,80},{112,128},{128,112... | collective-permute-start | bytes 884744 | tf_op jit(solution)/shard_map/ppermute | solution.py:488

commit v5 on v4

--- a/solution.py
+++ b/solution.py
@@ -11,7 +11,8 @@
 BLOCK_ROWS = 4
 BLOCK_COLS = 128
 LANES = 128
-REACH = 6
+ABOVE = 6
+BELOW = 5
 HALO = 16
 STAMP_LANE = 4 * HALO
 PER_BLOCK = 10
@@ -338,19 +339,35 @@
     )(z, m, stamp, table)
 
 
-def sent_start(rows, odd, side):
-    return odd * (rows - REACH) if side else (1 - odd) * (rows - REACH)
-
-
-def got_start(rows, odd, side):
-    return odd * (rows + REACH) if side else (1 - odd) * (rows + REACH)
+def send_rows(state_ref, first, sent_ref):
+    fields = state_ref.shape[2]
+    lane = lax.broadcasted_iota(jnp.int32, (8, LANES), 1)
+    for r in range(sent_ref.shape[0]):
+        for t in range(5):
+            sent_ref[r, pl.ds(t * fields, fields)] = state_ref[first + r, t]
+        halo = state_ref[first + r, 5].astype(F32)
+        packed = pltpu.roll(halo[0:8], HALO, 1)
+        for g in range(1, fields // 8):
+            packed = jnp.where(lane < 2 * HALO * g, packed, pltpu.roll(halo[8 * g : 8 * g + 8], HALO * (2 * g + 1), 1))
+        sent_ref[r, pl.ds(5 * fields, 8)] = packed.astype(BF16)
+
+
+def take_rows(got_ref, first, state_ref):
+    fields = state_ref.shape[2]
+    for r in range(got_ref.shape[0]):
+        for t in range(5):
+            state_ref[first + r, t] = got_ref[r, pl.ds(t * fields, fields)]
+        packed = got_ref[r, pl.ds(5 * fields, 8)].astype(F32)
+        halo = [pltpu.roll(packed, (LANES - HALO * (2 * g + 1)) % LANES, 1) for g in range(fields // 8)]
+        state_ref[first + r, 5] = jnp.concatenate(halo, axis=0).astype(BF16)
 
 
 def state_shapes(rows, tiles, fields):
-    return [jax.ShapeDtypeStruct((n, tiles, fields, LANES), BF16) for n in (rows, REACH, REACH)]
-
-
-def regroup_kernel(owner_ref, odd_ref, x_ref, out_ref, near_ref, far_ref, edge_ref, wide_ref):
+    shapes = [(rows, tiles, fields, LANES)] + [(n, 5 * fields + 8, LANES) for n in (ABOVE, BELOW)]
+    return [jax.ShapeDtypeStruct(shape, BF16) for shape in shapes]
+
+
+def regroup_kernel(owner_ref, x_ref, out_ref, last_ref, first_ref, edge_ref, wide_ref):
     rows, tiles, fields = out_ref.shape[:3]
     sources = x_ref.shape[0]
     main, span = (tiles - 1) * rows, tiles * rows
@@ -364,8 +381,8 @@
         for t in range(tiles):
             got = wide_ref[pl.ds(t * rows + j, fields, stride=span), :]
             out_ref[j, t] = got.astype(BF16)
-    for side, ref in enumerate((near_ref, far_ref)):
-        ref[...] = out_ref[pl.ds(sent_start(rows, odd_ref[0], side), REACH)]
+    send_rows(out_ref, rows - ABOVE, last_ref)
+    send_rows(out_ref, 0, first_ref)
     owner = owner_ref[0]
     edges = []
     for source in ((owner + sources - 1) % sources, (owner + 1) % sources):
@@ -374,27 +391,26 @@
     edge_ref[...] = jnp.concatenate(edges, axis=0)
 
 
-def regroup(x, owner, odd):
+def regroup(x, owner):
     smem, vmem = pl.BlockSpec(memory_space=pltpu.SMEM), pl.BlockSpec(memory_space=pltpu.VMEM)
     tiles = (x.shape[1] + 8) // 16
     return pl.pallas_call(
         regroup_kernel,
         out_shape=state_shapes(8, tiles, 32) + [jax.ShapeDtypeStruct((2, LANES), F32)],
-        in_specs=[smem, smem, vmem],
+        in_specs=[smem, vmem],
         out_specs=[vmem] * 4,
         scratch_shapes=[pltpu.VMEM((32 * tiles * 8, LANES), F32)],
         compiler_params=pltpu.CompilerParams(vmem_limit_bytes=8 << 20),
         name="regroup",
-    )(owner, odd, x)
-
-
-def advance_kernel(last, param_ref, edge_ref, odd_ref, near_ref, now_ref, far_ref, phys_ref, bias_ref, *refs):
+    )(owner, x)
+
+
+def advance_kernel(last, param_ref, edge_ref, before_ref, now_ref, after_ref, phys_ref, bias_ref, *refs):
     rows, tiles, fields = now_ref.shape[:3]
     s_ref = refs[-1]
-    odd = odd_ref[0]
-    s_ref[pl.ds(REACH, rows)] = now_ref[...]
-    for side, ref in enumerate((near_ref, far_ref)):
-        s_ref[pl.ds(got_start(rows, odd, side), REACH)] = ref[...]
+    take_rows(before_ref, 0, s_ref)
+    s_ref[pl.ds(ABOVE, rows)] = now_ref[...]
+    take_rows(after_ref, ABOVE + rows, s_ref)
     bands = rows // BLOCK_ROWS
     lane = lax.broadcasted_iota(jnp.int32, (fields, LANES), 1)
     left_half = lane < LANES // 2
@@ -409,7 +425,7 @@
             west = block < 0
             start = STAMP_LANE + (west * bands + band) * PER_BLOCK
             value = [edge_ref[0 if west else 1, start + k] for k in range(PER_BLOCK)]
-        base = REACH - 2 + band * BLOCK_ROWS - value[0].astype(jnp.int32)
+        base = ABOVE - 2 + band * BLOCK_ROWS - value[0].astype(jnp.int32)
         first = -value[1].astype(jnp.int32) - 2
         wr, wc = value[2:6], value[6:10]
         centre, edge = [], []
@@ -454,8 +470,8 @@
                 else:
                     refs[0][row, tile] = value.astype(BF16)
     if not last:
-        for side in range(2):
-            refs[1 + side][...] = refs[0][pl.ds(sent_start(rows, odd, side), REACH)]
+        send_rows(refs[0], rows - ABOVE, refs[1])
+        send_rows(refs[0], 0, refs[2])
     if last:
         for f in range(fields):
             for t in range(5):
@@ -463,10 +479,10 @@
                 refs[0][f, :, pl.ds(t * LANES, LANES)] = got.astype(BF16)
 
 
-def advance(last, params, edges, odd, near, now, far, phys, bias):
+def advance(last, params, edges, before, now, after, phys, bias):
     rows, tiles, fields = now.shape[:3]
     smem, vmem = pl.BlockSpec(memory_space=pltpu.SMEM), pl.BlockSpec(memory_space=pltpu.VMEM)
-    scratch = [pltpu.VMEM((rows + 2 * REACH, tiles, fields, LANES), BF16)]
+    scratch = [pltpu.VMEM((ABOVE + rows + BELOW, tiles, fields, LANES), BF16)]
     if last:
         shape = jax.ShapeDtypeStruct((fields, rows, 5 * LANES), BF16)
         scratch.insert(0, pltpu.VMEM((rows * 5 * fields, LANES), F32))
@@ -475,19 +491,18 @@
     return pl.pallas_call(
         functools.partial(advance_kernel, last),
         out_shape=shape,
-        in_specs=[smem] * 3 + [vmem] * 5,
+        in_specs=[smem] * 2 + [vmem] * 5,
         scratch_shapes=scratch,
         compiler_params=pltpu.CompilerParams(vmem_limit_bytes=16 << 20),
         name="advance_last" if last else "advance_first",
-    )(params, edges, odd, near, now, far, phys, bias)
-
-
-def row_halos(near, far):
+    )(params, edges, before, now, after, phys, bias)
+
+
+def row_halos(last, first):
     size = lax.axis_size("wave")
-    pairs = [(i + d, i + 1 - d) for i in range(size - 1) for d in (0, 1)]
-    far = lax.ppermute(far, "wave", [p for p in pairs if min(p) % 2])
-    near = lax.ppermute(near, "wave", [p for p in pairs if not min(p) % 2])
-    return near, far
+    before = lax.ppermute(last, "wave", [(i, i + 1) for i in range(size - 1)])
+    after = lax.ppermute(first, "wave", [(i + 1, i) for i in range(size - 1)])
+    return before, after
 
 
 def shards(spectral, wave_ids, lat_rows, shift_rows, shift_cols, frac_rows, frac_cols, phys_weight, phys_bias):
@@ -510,12 +525,11 @@
     arrived, params, bias = lax.optimization_barrier((arrived, params, bias))
     columns = fourier(arrived, m, stamp, table, scale)
     columns = lax.all_to_all(columns, "lev", split_axis=0, concat_axis=0, tiled=True)
-    odd = band % 2
-    state, near, far, edges = regroup(columns, owner, odd)
-    near, far = row_halos(near, far)
-    state, near, far = advance(False, params, edges, odd, near, state, far, phys_weight, bias)
-    near, far = row_halos(near, far)
-    return advance(True, params, edges, odd, near, state, far, phys_weight, bias)
+    state, last, first, edges = regroup(columns, owner)
+    before, after = row_halos(last, first)
+    state, last, first = advance(False, params, edges, before, state, after, phys_weight, bias)
+    before, after = row_halos(last, first)
+    return advance(True, params, edges, before, state, after, phys_weight, bias)
 
 
 def solution(mesh):

time: 90.6 us -> 85.7 us (0.946)
  waiting for transfers between devices: 31.7 us -> 28.4 us
  starting transfers between devices: 39.5 us -> 37.2 us
    ppermute x4, waiting for transfers between devices: 13.6 us -> 10.3 us  [the longest x2 10.3 us: row_halos(): after = lax.ppermute(first, 'wave', [(i + 1, i) for i in range(size - 1)])]
    ppermute x4, starting transfers between devices: 12.5 us -> 10.2 us  [the longest x2 5.87 us: row_halos(): before = lax.ppermute(last, 'wave', [(i, i + 1) for i in range(size - 1)])]
where the time goes in v5:
time: 85.7 us; the launch traced here: 84.7 us
  starting transfers between devices  37.2 us (43%)
  waiting for transfers between devices  28.4 us (33%)
  Pallas kernels  15.5 us (18%)
  local copies, waits for them, and re-layouts  3.44 us (4%)
    all_to_all x1, starting transfers between devices, shards(): lax.all_to_all(outgoing, 'wave', split_axis=0, concat_axis=0, tiled=True)  17.9 us
    all_to_all x1, waiting for transfers between devices, shards(): lax.all_to_all(columns, 'lev', split_axis=0, concat_axis=0, tiled=True)  12 us
    ppermute x2, waiting for transfers between devices, row_halos(): after = lax.ppermute(first, 'wave', [(i + 1, i) for i in range(size - 1)])  10.3 us
    all_to_all x1, starting transfers between devices, shards(): lax.all_to_all(columns, 'lev', split_axis=0, concat_axis=0, tiled=True)  9.09 us
    all_to_all x1, waiting for transfers between devices, shards(): lax.all_to_all(outgoing, 'wave', split_axis=0, concat_axis=0, tiled=True)  6.15 us
    ppermute x2, starting transfers between devices, row_halos(): before = lax.ppermute(last, 'wave', [(i, i + 1) for i in range(size - 1)])  5.87 us
    pallas_call x2, Pallas kernels, advance(): pl.pallas_call(functools.partial(advance_kernel, last), out_shape=shape,...  4.88 us
    ppermute x2, starting transfers between devices, row_halos(): after = lax.ppermute(first, 'wave', [(i + 1, i) for i in range(size - 1)])  4.34 us
  transfers between devices with their start and end apart: 6, of which 4 were waited for; matrix products, arithmetic and copies ran while one was open for 1% of the time, Pallas kernels for 3%

profile of v5, /device:TPU:1, one launch (start us, length us, event | category | flops | bytes accessed | tf_op | source)
XLA Modules:
  0.0 84.7 jit_solution(14640044264812591507)
XLA Ops:
  0.0 3.6 %legendre.1 = bf16[384,128]{1,0:T(8,128)(2,1)} custom-call(s32[1536]{0:T(1024)} %ids_hbm.1, s32[384]{0:T(512)} %lat_hbm.1, s32[1]{0:T(128)} %bitcast.band_ref, bf16[32,2,2,1536]{3,2,1,0:T(2,128)(2,1)} %x_hbm.1), custom_call_target="tpu_custom_call" | custom-call | tf_op jit(solution)/shard_map/legendre/pallas_call | solution.py:127
  3.6 0.0 copy-start
  3.6 0.0 copy-start.1
  3.6 17.9 %all-to-all-start = ((bf16[48,8,128]{2,1,0:T(8,128)(2,1)}), bf16[48,8,128]{2,1,0:T(8,128)(2,1)S(1)}, u32[]{:S(2)}, u32[]{:S(2)}) async-start(bf16[48,8,128]{2,1,0:T(8,128)(2,1)} %bitcast.6), calls=%async_computation | async-start | bytes 196608 | tf_op jit(solution)/shard_map/all_to_all | solution.py:520
  21.5 0.7 broadcast_in_dim.6.ids_ref
  22.2 0.7 copy-done.2
  22.9 0.7 copy-done.3
  23.6 0.7 copy-done.4
  24.3 0.7 copy-done.5
  25.0 2.5 %fourier_table.1 = (bf16[768,1536]{1,0:T(8,128)(2,1)S(1)}, f32[1,1536]{1,0:T(1,128)S(1)}, f32[8,128]{1,0:T(8,128)S(1)}, f32[200]{0:T(256)S(1)}) custom-call(s32[1,1536]{1,0:T(1,128)S(1)} %broadcast_in_dim.6.ids_ref, s32[2,2,5]{2,1,0:T(2,128)S(1)} %copy-done.2, s32[2,2,5]{2,1,0:T(2,128)S(1)} %copy-done.3, f32[2,2,5]{2,1,0:T(2,128)S(1)} %copy-done.4, ...), custom_call_target="tpu_custom_call" | custom-call | flops 20000000 | bytes 2500000 | tf_op jit(solution)/shard_map/fourier_table/pallas_call | solution.py:243
  27.4 6.1 %all-to-all-done.z_ref = bf16[48,8,128]{2,1,0:T(8,128)(2,1)S(1)} async-done(((bf16[48,8,128]{2,1,0:T(8,128)(2,1)}), bf16[48,8,128]{2,1,0:T(8,128)(2,1)S(1)}, u32[]{:S(2)}, u32[]{:S(2)}) %all-to-all-start) | async-done | bytes 98336 | tf_op jit(solution)/shard_map/all_to_all | solution.py:520
  33.6 4.2 %fourier.1 = bf16[16,88,128]{2,1,0:T(8,128)(2,1)} custom-call(bf16[48,8,128]{2,1,0:T(8,128)(2,1)S(1)} %all-to-all-done.z_ref, f32[1,1536]{1,0:T(1,128)S(1)} %get-tuple-element.22.m_ref, f32[8,128]{1,0:T(8,128)S(1)} %get-tuple-element.23.stamp_ref, bf16[768,1536]{1,0:T(8,128)(2,1)S(1)} %get-tuple-element.24.e_ref), custom_call_target="tpu_custom_call" | custom-call | tf_op jit(solution)/shard_map/fourier/pallas_call | solution.py:327
  37.8 9.1 %all-to-all-start.1 = ((bf16[16,88,128]{2,1,0:T(8,128)(2,1)}), bf16[16,88,128]{2,1,0:T(8,128)(2,1)S(1)}, u32[]{:S(2)}, u32[]{:S(2)}) async-start(bf16[16,88,128]{2,1,0:T(8,128)(2,1)} %fourier.1), calls=%async_computation.1 | async-start | bytes 720896 | tf_op jit(solution)/shard_map/all_to_all | solution.py:527
  46.9 12.0 %all-to-all-done.1.x_ref = bf16[16,88,128]{2,1,0:T(8,128)(2,1)S(1)} async-done(((bf16[16,88,128]{2,1,0:T(8,128)(2,1)}), bf16[16,88,128]{2,1,0:T(8,128)(2,1)S(1)}, u32[]{:S(2)}, u32[]{:S(2)}) %all-to-all-start.1) | async-done | bytes 360480 | tf_op jit(solution)/shard_map/all_to_all | solution.py:527
  58.8 0.4 regroup.1
  59.2 4.0 %collective-permute-start = (bf16[6,168,128]{2,1,0:T(8,128)(2,1)S(1)}, bf16[6,168,128]{2,1,0:T(8,128)(2,1)S(1)}, u32[]{:S(2)}, u32[]{:S(2)}) collective-permute-start(bf16[6,168,128]{2,1,0:T(8,128)(2,1)S(1)} %get-tuple-element.26), channel_id=1, source_target_pairs={{0,16},{16,32},{32,48},{48,64},{64,80},{80,96},{96,112},{112,128},... | collective-permute-start | bytes 774152 | tf_op jit(solution)/shard_map/ppermute | solution.py:503
  63.2 1.9 %collective-permute-start.1 = (bf16[5,168,128]{2,1,0:T(8,128)(2,1)S(1)}, bf16[5,168,128]{2,1,0:T(8,128)(2,1)S(1)}, u32[]{:S(2)}, u32[]{:S(2)}) collective-permute-start(bf16[5,168,128]{2,1,0:T(8,128)(2,1)S(1)} %get-tuple-element.28), channel_id=1, source_target_pairs={{16,0},{32,16},{48,32},{64,48},{80,64},{96,80},{112,96},{128,112},... | collective-permute-start | bytes 645128 | tf_op jit(solution)/shard_map/ppermute | solution.py:504
  65.1 5.3 %collective-permute-done.1.after_ref = bf16[5,168,128]{2,1,0:T(8,128)(2,1)S(1)} collective-permute-done((bf16[5,168,128]{2,1,0:T(8,128)(2,1)S(1)}, bf16[5,168,128]{2,1,0:T(8,128)(2,1)S(1)}, u32[]{:S(2)}, u32[]{:S(2)}) %collective-permute-start.1) | collective-permute-done | bytes 215072 | tf_op jit(solution)/shard_map/ppermute | solution.py:504
  70.4 0.0 collective-permute-done.before_ref
  70.4 2.2 %advance_first.1 = (bf16[8,6,32,128]{3,2,1,0:T(8,128)(2,1)S(1)}, bf16[6,168,128]{2,1,0:T(8,128)(2,1)S(1)}, bf16[5,168,128]{2,1,0:T(8,128)(2,1)S(1)}) custom-call(f32[200]{0:T(256)S(1)} %get-tuple-element.20.param_ref, f32[2,128]{1,0:T(2,128)S(1)} %get-tuple-element.25.edge_ref, bf16[6,168,128]{2,1,0:T(8,128)(2,1)S(1)} %collective-permute-done.before_ref, ...), custom_call_target="tpu_custom_call" | custom-call | tf_op jit(solution)/shard_map/advance_first/pallas_call | solution.py:491
  72.6 1.9 %collective-permute-start.2 = (bf16[6,168,128]{2,1,0:T(8,128)(2,1)S(1)}, bf16[6,168,128]{2,1,0:T(8,128)(2,1)S(1)}, u32[]{:S(2)}, u32[]{:S(2)}) collective-permute-start(bf16[6,168,128]{2,1,0:T(8,128)(2,1)S(1)} %get-tuple-element.30), channel_id=1, source_target_pairs={{0,16},{16,32},{32,48},{48,64},{64,80},{80,96},{96,112},{112,128},... | collective-permute-start | bytes 774152 | tf_op jit(solution)/shard_map/ppermute | solution.py:503
  74.5 2.4 %collective-permute-start.3 = (bf16[5,168,128]{2,1,0:T(8,128)(2,1)S(1)}, bf16[5,168,128]{2,1,0:T(8,128)(2,1)S(1)}, u32[]{:S(2)}, u32[]{:S(2)}) collective-permute-start(bf16[5,168,128]{2,1,0:T(8,128)(2,1)S(1)} %get-tuple-element.32), channel_id=1, source_target_pairs={{16,0},{32,16},{48,32},{64,48},{80,64},{96,80},{112,96},{128,112},... | collective-permute-start | bytes 645128 | tf_op jit(solution)/shard_map/ppermute | solution.py:504
  77.0 5.0 %collective-permute-done.3.after_ref = bf16[5,168,128]{2,1,0:T(8,128)(2,1)S(1)} collective-permute-done((bf16[5,168,128]{2,1,0:T(8,128)(2,1)S(1)}, bf16[5,168,128]{2,1,0:T(8,128)(2,1)S(1)}, u32[]{:S(2)}, u32[]{:S(2)}) %collective-permute-start.3) | collective-permute-done | bytes 215072 | tf_op jit(solution)/shard_map/ppermute | solution.py:504
  82.0 2.6 %advance_last.1 = bf16[32,8,640]{2,1,0:T(8,128)(2,1)} custom-call(f32[200]{0:T(256)S(1)} %get-tuple-element.20.param_ref, f32[2,128]{1,0:T(2,128)S(1)} %get-tuple-element.25.edge_ref, bf16[6,168,128]{2,1,0:T(8,128)(2,1)S(1)} %collective-permute-done.2.before_ref, bf16[8,6,32,128]{3,2,1,0:T(8,128)(2,1)S(1)} %get-tuple-element.31.now_ref, ...), custom_call_target="tpu_custom_call" | custom-call | tf_op jit(solution)/shard_map/advance_last/pallas_call | solution.py:491
  (7 shorter events, 0.0 us)
Async XLA Ops:
  3.6 66.8 %copy-start = (bf16[32,32]{1,0:T(8,128)(2,1)S(1)}, bf16[32,32]{1,0:T(8,128)(2,1)}, u32[]{:S(2)}) copy-start(bf16[32,32]{1,0:T(8,128)(2,1)} %phys_ref.3) | copy-start | bytes 6148
  3.6 66.8 %copy-start.1 = (f32[32]{0:T(128)S(1)}, f32[32]{0:T(128)}, u32[]{:S(2)}) copy-start(f32[32]{0:T(128)} %param.17) | copy-start | bytes 388
  3.6 30.0 %all-to-all-start = ((bf16[48,8,128]{2,1,0:T(8,128)(2,1)}), bf16[48,8,128]{2,1,0:T(8,128)(2,1)S(1)}, u32[]{:S(2)}, u32[]{:S(2)}) async-start(bf16[48,8,128]{2,1,0:T(8,128)(2,1)} %bitcast.6), calls=%async_computation | async-start | bytes 196608 | tf_op jit(solution)/shard_map/all_to_all | solution.py:520
  22.2 0.7 copy-start.2
  22.9 0.7 copy-start.3
  23.6 0.7 copy-start.4
  24.3 0.7 copy-start.5
  37.8 21.1 %all-to-all-start.1 = ((bf16[16,88,128]{2,1,0:T(8,128)(2,1)}), bf16[16,88,128]{2,1,0:T(8,128)(2,1)S(1)}, u32[]{:S(2)}, u32[]{:S(2)}) async-start(bf16[16,88,128]{2,1,0:T(8,128)(2,1)} %fourier.1), calls=%async_computation.1 | async-start | bytes 720896 | tf_op jit(solution)/shard_map/all_to_all | solution.py:527
  59.2 11.1 %collective-permute-start = (bf16[6,168,128]{2,1,0:T(8,128)(2,1)S(1)}, bf16[6,168,128]{2,1,0:T(8,128)(2,1)S(1)}, u32[]{:S(2)}, u32[]{:S(2)}) collective-permute-start(bf16[6,168,128]{2,1,0:T(8,128)(2,1)S(1)} %get-tuple-element.26), channel_id=1, source_target_pairs={{0,16},{16,32},{32,48},{48,64},{64,80},{80,96},{96,112},{112,128},... | collective-permute-start | bytes 774152 | tf_op jit(solution)/shard_map/ppermute | solution.py:503
  63.2 7.2 %collective-permute-start.1 = (bf16[5,168,128]{2,1,0:T(8,128)(2,1)S(1)}, bf16[5,168,128]{2,1,0:T(8,128)(2,1)S(1)}, u32[]{:S(2)}, u32[]{:S(2)}) collective-permute-start(bf16[5,168,128]{2,1,0:T(8,128)(2,1)S(1)} %get-tuple-element.28), channel_id=1, source_target_pairs={{16,0},{32,16},{48,32},{64,48},{80,64},{96,80},{112,96},{128,112},... | collective-permute-start | bytes 645128 | tf_op jit(solution)/shard_map/ppermute | solution.py:504
  72.6 9.4 %collective-permute-start.2 = (bf16[6,168,128]{2,1,0:T(8,128)(2,1)S(1)}, bf16[6,168,128]{2,1,0:T(8,128)(2,1)S(1)}, u32[]{:S(2)}, u32[]{:S(2)}) collective-permute-start(bf16[6,168,128]{2,1,0:T(8,128)(2,1)S(1)} %get-tuple-element.30), channel_id=1, source_target_pairs={{0,16},{16,32},{32,48},{48,64},{64,80},{80,96},{96,112},{112,128},... | collective-permute-start | bytes 774152 | tf_op jit(solution)/shard_map/ppermute | solution.py:503
  74.5 7.5 %collective-permute-start.3 = (bf16[5,168,128]{2,1,0:T(8,128)(2,1)S(1)}, bf16[5,168,128]{2,1,0:T(8,128)(2,1)S(1)}, u32[]{:S(2)}, u32[]{:S(2)}) collective-permute-start(bf16[5,168,128]{2,1,0:T(8,128)(2,1)S(1)} %get-tuple-element.32), channel_id=1, source_target_pairs={{16,0},{32,16},{48,32},{64,48},{80,64},{96,80},{112,96},{128,112},... | collective-permute-start | bytes 645128 | tf_op jit(solution)/shard_map/ppermute | solution.py:504

commit v6 on v5

--- a/solution.py
+++ b/solution.py
@@ -522,7 +522,7 @@
         wave_ids[None, :], shift_rows, shift_cols, frac_rows, frac_cols, 2 * nlon, 6
     )
     bias = phys_bias[None, :]
-    arrived, params, bias = lax.optimization_barrier((arrived, params, bias))
+    arrived, params, bias, owner = lax.optimization_barrier((arrived, params, bias, owner))
     columns = fourier(arrived, m, stamp, table, scale)
     columns = lax.all_to_all(columns, "lev", split_axis=0, concat_axis=0, tiled=True)
     state, last, first, edges = regroup(columns, owner)

time: 85.7 us -> 84.7 us (0.988)
  blocking collectives: 0 us -> 20.9 us
  waiting for transfers between devices: 28.4 us -> 16.5 us
  starting transfers between devices: 37.2 us -> 28.1 us
    all_to_all x0 -> x1, blocking collectives: none -> 20.9 us  [shards(): lax.all_to_all(columns, 'lev', split_axis=0, concat_axis=0, tiled=True)]
    all_to_all x1 -> x0, waiting for transfers between devices: 12 us -> none  [shards(): lax.all_to_all(columns, 'lev', split_axis=0, concat_axis=0, tiled=True)]
    all_to_all x1 -> x0, starting transfers between devices: 9.09 us -> none  [shards(): lax.all_to_all(columns, 'lev', split_axis=0, concat_axis=0, tiled=True)]
  transfers between devices with their start and end apart: 6 -> 5, of which waited for: 4 -> 3; matrix products, arithmetic and copies ran while one was open for 1% -> 1% of each run, Pallas kernels for 3% -> 3%
where the time goes in v6:
time: 84.7 us; the launch traced here: 83.7 us
  starting transfers between devices  28.1 us (33%)
  blocking collectives  20.9 us (25%)
  waiting for transfers between devices  16.5 us (19%)
  Pallas kernels  14.8 us (17%)
  local copies, waits for them, and re-layouts  3.44 us (4%)
    all_to_all x1, blocking collectives, shards(): lax.all_to_all(columns, 'lev', split_axis=0, concat_axis=0, tiled=True)  20.9 us
    all_to_all x1, starting transfers between devices, shards(): lax.all_to_all(outgoing, 'wave', split_axis=0, concat_axis=0, tiled=True)  17.9 us
    ppermute x2, waiting for transfers between devices, row_halos(): after = lax.ppermute(first, 'wave', [(i + 1, i) for i in range(size - 1)])  10.3 us
    all_to_all x1, waiting for transfers between devices, shards(): lax.all_to_all(outgoing, 'wave', split_axis=0, concat_axis=0, tiled=True)  6.15 us
    ppermute x2, starting transfers between devices, row_halos(): before = lax.ppermute(last, 'wave', [(i, i + 1) for i in range(size - 1)])  5.87 us
    pallas_call x2, Pallas kernels, advance(): pl.pallas_call(functools.partial(advance_kernel, last), out_shape=shape,...  4.88 us
    ppermute x2, starting transfers between devices, row_halos(): after = lax.ppermute(first, 'wave', [(i + 1, i) for i in range(size - 1)])  4.34 us
    pallas_call x1, Pallas kernels, legendre(): pl.pallas_call(functools.partial(legendre_kernel, period, middle, turn, s...  3.6 us
  transfers between devices with their start and end apart: 5, of which 3 were waited for; matrix products, arithmetic and copies ran while one was open for 1% of the time, Pallas kernels for 3%

profile of v6, /device:TPU:1, one launch (start us, length us, event | category | flops | bytes accessed | tf_op | source)
XLA Modules:
  0.0 83.7 jit_solution(9797652685717135831)
XLA Ops:
  0.0 3.6 %legendre.1 = bf16[384,128]{1,0:T(8,128)(2,1)} custom-call(s32[1536]{0:T(1024)} %ids_hbm.1, s32[384]{0:T(512)} %lat_hbm.1, s32[1]{0:T(128)} %bitcast.band_ref, bf16[32,2,2,1536]{3,2,1,0:T(2,128)(2,1)} %x_hbm.1), custom_call_target="tpu_custom_call" | custom-call | tf_op jit(solution)/shard_map/legendre/pallas_call | solution.py:127
  3.6 0.0 copy-start
  3.6 0.0 copy-start.1
  3.6 17.9 %all-to-all-start = ((bf16[48,8,128]{2,1,0:T(8,128)(2,1)}), bf16[48,8,128]{2,1,0:T(8,128)(2,1)S(1)}, u32[]{:S(2)}, u32[]{:S(2)}) async-start(bf16[48,8,128]{2,1,0:T(8,128)(2,1)} %bitcast.6), calls=%async_computation | async-start | bytes 196608 | tf_op jit(solution)/shard_map/all_to_all | solution.py:520
  21.5 0.7 broadcast_in_dim.6.ids_ref
  22.2 0.7 copy-done.2
  22.9 0.7 copy-done.3
  23.6 0.7 copy-done.4
  24.3 0.7 copy-done.5
  25.0 2.5 %fourier_table.1 = (bf16[768,1536]{1,0:T(8,128)(2,1)S(1)}, f32[1,1536]{1,0:T(1,128)S(1)}, f32[8,128]{1,0:T(8,128)S(1)}, f32[200]{0:T(256)S(1)}) custom-call(s32[1,1536]{1,0:T(1,128)S(1)} %broadcast_in_dim.6.ids_ref, s32[2,2,5]{2,1,0:T(2,128)S(1)} %copy-done.2, s32[2,2,5]{2,1,0:T(2,128)S(1)} %copy-done.3, f32[2,2,5]{2,1,0:T(2,128)S(1)} %copy-done.4, ...), custom_call_target="tpu_custom_call" | custom-call | flops 20000000 | bytes 2500000 | tf_op jit(solution)/shard_map/fourier_table/pallas_call | solution.py:243
  27.4 6.1 %all-to-all-done.z_ref = bf16[48,8,128]{2,1,0:T(8,128)(2,1)S(1)} async-done(((bf16[48,8,128]{2,1,0:T(8,128)(2,1)}), bf16[48,8,128]{2,1,0:T(8,128)(2,1)S(1)}, u32[]{:S(2)}, u32[]{:S(2)}) %all-to-all-start) | async-done | bytes 98336 | tf_op jit(solution)/shard_map/all_to_all | solution.py:520
  33.6 3.4 %fourier.1 = bf16[16,88,128]{2,1,0:T(8,128)(2,1)S(1)} custom-call(bf16[48,8,128]{2,1,0:T(8,128)(2,1)S(1)} %all-to-all-done.z_ref, f32[1,1536]{1,0:T(1,128)S(1)} %get-tuple-element.24.m_ref, f32[8,128]{1,0:T(8,128)S(1)} %get-tuple-element.25.stamp_ref, bf16[768,1536]{1,0:T(8,128)(2,1)S(1)} %get-tuple-element.26.e_ref), custom_call_target="tpu_custom_call" | custom-call | tf_op jit(solution)/shard_map/fourier/pallas_call | solution.py:327
  37.0 20.9 %all_to_all.10.x_ref = bf16[16,88,128]{2,1,0:T(8,128)(2,1)S(1)} all-to-all(bf16[16,88,128]{2,1,0:T(8,128)(2,1)S(1)} %fourier.1), channel_id=1, replica_groups=mesh['wave'=48,'lev'=16] {'lev'}, dimensions={0} | all-to-all | bytes 720896 | tf_op jit(solution)/shard_map/all_to_all | solution.py:527
  57.9 0.4 regroup.1
  58.3 4.0 %collective-permute-start = (bf16[6,168,128]{2,1,0:T(8,128)(2,1)S(1)}, bf16[6,168,128]{2,1,0:T(8,128)(2,1)S(1)}, u32[]{:S(2)}, u32[]{:S(2)}) collective-permute-start(bf16[6,168,128]{2,1,0:T(8,128)(2,1)S(1)} %get-tuple-element.28), channel_id=1, source_target_pairs={{0,16},{16,32},{32,48},{48,64},{64,80},{80,96},{96,112},{112,128},... | collective-permute-start | bytes 774152 | tf_op jit(solution)/shard_map/ppermute | solution.py:503
  62.2 1.9 %collective-permute-start.1 = (bf16[5,168,128]{2,1,0:T(8,128)(2,1)S(1)}, bf16[5,168,128]{2,1,0:T(8,128)(2,1)S(1)}, u32[]{:S(2)}, u32[]{:S(2)}) collective-permute-start(bf16[5,168,128]{2,1,0:T(8,128)(2,1)S(1)} %get-tuple-element.30), channel_id=1, source_target_pairs={{16,0},{32,16},{48,32},{64,48},{80,64},{96,80},{112,96},{128,112},... | collective-permute-start | bytes 645128 | tf_op jit(solution)/shard_map/ppermute | solution.py:504
  64.2 5.3 %collective-permute-done.1.after_ref = bf16[5,168,128]{2,1,0:T(8,128)(2,1)S(1)} collective-permute-done((bf16[5,168,128]{2,1,0:T(8,128)(2,1)S(1)}, bf16[5,168,128]{2,1,0:T(8,128)(2,1)S(1)}, u32[]{:S(2)}, u32[]{:S(2)}) %collective-permute-start.1) | collective-permute-done | bytes 215072 | tf_op jit(solution)/shard_map/ppermute | solution.py:504
  69.4 0.0 collective-permute-done.before_ref
  69.4 2.2 %advance_first.1 = (bf16[8,6,32,128]{3,2,1,0:T(8,128)(2,1)S(1)}, bf16[6,168,128]{2,1,0:T(8,128)(2,1)S(1)}, bf16[5,168,128]{2,1,0:T(8,128)(2,1)S(1)}) custom-call(f32[200]{0:T(256)S(1)} %get-tuple-element.21.param_ref, f32[2,128]{1,0:T(2,128)S(1)} %get-tuple-element.27.edge_ref, bf16[6,168,128]{2,1,0:T(8,128)(2,1)S(1)} %collective-permute-done.before_ref, ...), custom_call_target="tpu_custom_call" | custom-call | tf_op jit(solution)/shard_map/advance_first/pallas_call | solution.py:491
  71.7 1.9 %collective-permute-start.2 = (bf16[6,168,128]{2,1,0:T(8,128)(2,1)S(1)}, bf16[6,168,128]{2,1,0:T(8,128)(2,1)S(1)}, u32[]{:S(2)}, u32[]{:S(2)}) collective-permute-start(bf16[6,168,128]{2,1,0:T(8,128)(2,1)S(1)} %get-tuple-element.32), channel_id=1, source_target_pairs={{0,16},{16,32},{32,48},{48,64},{64,80},{80,96},{96,112},{112,128},... | collective-permute-start | bytes 774152 | tf_op jit(solution)/shard_map/ppermute | solution.py:503
  73.6 2.4 %collective-permute-start.3 = (bf16[5,168,128]{2,1,0:T(8,128)(2,1)S(1)}, bf16[5,168,128]{2,1,0:T(8,128)(2,1)S(1)}, u32[]{:S(2)}, u32[]{:S(2)}) collective-permute-start(bf16[5,168,128]{2,1,0:T(8,128)(2,1)S(1)} %get-tuple-element.34), channel_id=1, source_target_pairs={{16,0},{32,16},{48,32},{64,48},{80,64},{96,80},{112,96},{128,112},... | collective-permute-start | bytes 645128 | tf_op jit(solution)/shard_map/ppermute | solution.py:504
  76.0 5.0 %collective-permute-done.3.after_ref = bf16[5,168,128]{2,1,0:T(8,128)(2,1)S(1)} collective-permute-done((bf16[5,168,128]{2,1,0:T(8,128)(2,1)S(1)}, bf16[5,168,128]{2,1,0:T(8,128)(2,1)S(1)}, u32[]{:S(2)}, u32[]{:S(2)}) %collective-permute-start.3) | collective-permute-done | bytes 215072 | tf_op jit(solution)/shard_map/ppermute | solution.py:504
  81.1 0.0 collective-permute-done.2.before_ref
  81.1 2.6 %advance_last.1 = bf16[32,8,640]{2,1,0:T(8,128)(2,1)} custom-call(f32[200]{0:T(256)S(1)} %get-tuple-element.21.param_ref, f32[2,128]{1,0:T(2,128)S(1)} %get-tuple-element.27.edge_ref, bf16[6,168,128]{2,1,0:T(8,128)(2,1)S(1)} %collective-permute-done.2.before_ref, bf16[8,6,32,128]{3,2,1,0:T(8,128)(2,1)S(1)} %get-tuple-element.33.now_ref, ...), custom_call_target="tpu_custom_call" | custom-call | tf_op jit(solution)/shard_map/advance_last/pallas_call | solution.py:491
  (6 shorter events, 0.0 us)
Async XLA Ops:
  3.6 65.8 %copy-start = (bf16[32,32]{1,0:T(8,128)(2,1)S(1)}, bf16[32,32]{1,0:T(8,128)(2,1)}, u32[]{:S(2)}) copy-start(bf16[32,32]{1,0:T(8,128)(2,1)} %phys_ref.3) | copy-start | bytes 6148
  3.6 65.8 %copy-start.1 = (f32[32]{0:T(128)S(1)}, f32[32]{0:T(128)}, u32[]{:S(2)}) copy-start(f32[32]{0:T(128)} %param.17) | copy-start | bytes 388
  3.6 30.0 %all-to-all-start = ((bf16[48,8,128]{2,1,0:T(8,128)(2,1)}), bf16[48,8,128]{2,1,0:T(8,128)(2,1)S(1)}, u32[]{:S(2)}, u32[]{:S(2)}) async-start(bf16[48,8,128]{2,1,0:T(8,128)(2,1)} %bitcast.6), calls=%async_computation | async-start | bytes 196608 | tf_op jit(solution)/shard_map/all_to_all | solution.py:520
  22.2 0.7 copy-start.2
  22.9 0.7 copy-start.3
  23.6 0.7 copy-start.4
  24.3 0.7 copy-start.5
  58.3 11.1 %collective-permute-start = (bf16[6,168,128]{2,1,0:T(8,128)(2,1)S(1)}, bf16[6,168,128]{2,1,0:T(8,128)(2,1)S(1)}, u32[]{:S(2)}, u32[]{:S(2)}) collective-permute-start(bf16[6,168,128]{2,1,0:T(8,128)(2,1)S(1)} %get-tuple-element.28), channel_id=1, source_target_pairs={{0,16},{16,32},{32,48},{48,64},{64,80},{80,96},{96,112},{112,128},... | collective-permute-start | bytes 774152 | tf_op jit(solution)/shard_map/ppermute | solution.py:503
  62.2 7.2 %collective-permute-start.1 = (bf16[5,168,128]{2,1,0:T(8,128)(2,1)S(1)}, bf16[5,168,128]{2,1,0:T(8,128)(2,1)S(1)}, u32[]{:S(2)}, u32[]{:S(2)}) collective-permute-start(bf16[5,168,128]{2,1,0:T(8,128)(2,1)S(1)} %get-tuple-element.30), channel_id=1, source_target_pairs={{16,0},{32,16},{48,32},{64,48},{80,64},{96,80},{112,96},{128,112},... | collective-permute-start | bytes 645128 | tf_op jit(solution)/shard_map/ppermute | solution.py:504
  71.7 9.4 %collective-permute-start.2 = (bf16[6,168,128]{2,1,0:T(8,128)(2,1)S(1)}, bf16[6,168,128]{2,1,0:T(8,128)(2,1)S(1)}, u32[]{:S(2)}, u32[]{:S(2)}) collective-permute-start(bf16[6,168,128]{2,1,0:T(8,128)(2,1)S(1)} %get-tuple-element.32), channel_id=1, source_target_pairs={{0,16},{16,32},{32,48},{48,64},{64,80},{80,96},{96,112},{112,128},... | collective-permute-start | bytes 774152 | tf_op jit(solution)/shard_map/ppermute | solution.py:503
  73.6 7.5 %collective-permute-start.3 = (bf16[5,168,128]{2,1,0:T(8,128)(2,1)S(1)}, bf16[5,168,128]{2,1,0:T(8,128)(2,1)S(1)}, u32[]{:S(2)}, u32[]{:S(2)}) collective-permute-start(bf16[5,168,128]{2,1,0:T(8,128)(2,1)S(1)} %get-tuple-element.34), channel_id=1, source_target_pairs={{16,0},{32,16},{48,32},{64,48},{80,64},{96,80},{112,96},{128,112},... | collective-permute-start | bytes 645128 | tf_op jit(solution)/shard_map/ppermute | solution.py:504

commit v7 on v5

--- a/solution.py
+++ b/solution.py
@@ -40,12 +40,16 @@
     return c * rc - s * rs, s * rc + c * rs
 
 
+def position(axis):
+    return lax.axis_index(axis)
+
+
 def down(row):
     return jnp.broadcast_to(row, (LANES, LANES)).T
 
 
 def legendre_kernel(
-    period, middle, turn, scale, ids_hbm, lat_hbm, band_ref, x_hbm, out_ref, cos_ref, sin_ref, cw_ref, sw_ref, lat_ref,
+    period, middle, turn, scale, ids_hbm, lat_hbm, x_hbm, out_ref, cos_ref, sin_ref, cw_ref, sw_ref, lat_ref,
     ids_ref, lat_in_ref, x_ref, sems,
 ):
     loads = [
@@ -60,7 +64,7 @@
     slots = rows // 4
     step = 32
     lane = lax.broadcasted_iota(jnp.int32, (1, LANES), 1)
-    first = band_ref[0] * slots
+    first = position("wave") * slots
     loads[0].wait()
     m_row = jnp.zeros((1, LANES), jnp.int32)
     for s in range(slots):
@@ -119,15 +123,15 @@
     out_ref[...] = jnp.dot(leg, order, preferred_element_type=F32).astype(BF16)
 
 
-def legendre(x, wave_ids, band, lat_rows, period, middle, turn, scale):
+def legendre(x, wave_ids, lat_rows, period, middle, turn, scale):
     rows, waves = 4 * x.shape[0], x.shape[3]
     lats = lat_rows.shape[0]
-    hbm, smem = pl.BlockSpec(memory_space=pltpu.HBM), pl.BlockSpec(memory_space=pltpu.SMEM)
+    hbm = pl.BlockSpec(memory_space=pltpu.HBM)
     vmem = pl.BlockSpec(memory_space=pltpu.VMEM)
     return pl.pallas_call(
         functools.partial(legendre_kernel, period, middle, turn, scale),
         out_shape=jax.ShapeDtypeStruct((lats, rows), BF16),
-        in_specs=[hbm, hbm, smem, hbm],
+        in_specs=[hbm, hbm, hbm],
         out_specs=vmem,
         scratch_shapes=[
             pltpu.VMEM((lats, waves // 2), BF16),
@@ -142,7 +146,7 @@
         ],
         compiler_params=pltpu.CompilerParams(vmem_limit_bytes=67043328),
         name="legendre",
-    )(wave_ids, lat_rows, band, x)
+    )(wave_ids, lat_rows, x)
 
 
 def times_i(z, power):
@@ -367,7 +371,7 @@
     return [jax.ShapeDtypeStruct(shape, BF16) for shape in shapes]
 
 
-def regroup_kernel(owner_ref, x_ref, out_ref, last_ref, first_ref, edge_ref, wide_ref):
+def regroup_kernel(x_ref, out_ref, last_ref, first_ref, edge_ref, wide_ref):
     rows, tiles, fields = out_ref.shape[:3]
     sources = x_ref.shape[0]
     main, span = (tiles - 1) * rows, tiles * rows
@@ -383,7 +387,7 @@
             out_ref[j, t] = got.astype(BF16)
     send_rows(out_ref, rows - ABOVE, last_ref)
     send_rows(out_ref, 0, first_ref)
-    owner = owner_ref[0]
+    owner = position("lev")
     edges = []
     for source in ((owner + sources - 1) % sources, (owner + 1) % sources):
         parts = x_ref[source, pl.ds(2 * main, rows), :].astype(F32)
@@ -391,29 +395,38 @@
     edge_ref[...] = jnp.concatenate(edges, axis=0)
 
 
-def regroup(x, owner):
-    smem, vmem = pl.BlockSpec(memory_space=pltpu.SMEM), pl.BlockSpec(memory_space=pltpu.VMEM)
+def regroup(x):
+    vmem = pl.BlockSpec(memory_space=pltpu.VMEM)
     tiles = (x.shape[1] + 8) // 16
     return pl.pallas_call(
         regroup_kernel,
         out_shape=state_shapes(8, tiles, 32) + [jax.ShapeDtypeStruct((2, LANES), F32)],
-        in_specs=[smem, vmem],
+        in_specs=[vmem],
         out_specs=[vmem] * 4,
         scratch_shapes=[pltpu.VMEM((32 * tiles * 8, LANES), F32)],
         compiler_params=pltpu.CompilerParams(vmem_limit_bytes=8 << 20),
         name="regroup",
-    )(owner, x)
-
-
-def advance_kernel(last, param_ref, edge_ref, before_ref, now_ref, after_ref, phys_ref, bias_ref, *refs):
+    )(x)
+
+
+def advance_kernel(last, param_hbm, before_ref, now_ref, after_ref, phys_ref, bias_ref, *refs):
     rows, tiles, fields = now_ref.shape[:3]
-    s_ref = refs[-1]
+    if not last:
+        edge_hbm, *refs = refs
+    *refs, s_ref, param_ref, edge_ref, sems = refs
+    loads = [pltpu.make_async_copy(param_hbm, param_ref, sems.at[0])]
+    if not last:
+        loads.append(pltpu.make_async_copy(edge_hbm, edge_ref, sems.at[1]))
+    for load in loads:
+        load.start()
     take_rows(before_ref, 0, s_ref)
     s_ref[pl.ds(ABOVE, rows)] = now_ref[...]
     take_rows(after_ref, ABOVE + rows, s_ref)
     bands = rows // BLOCK_ROWS
     lane = lax.broadcasted_iota(jnp.int32, (fields, LANES), 1)
     left_half = lane < LANES // 2
+    for load in loads:
+        load.wait()
     phys = phys_ref[...]
     bias = jnp.broadcast_to(bias_ref[...], (LANES, fields)).T
 
@@ -430,10 +443,10 @@
         wr, wc = value[2:6], value[6:10]
         centre, edge = [], []
         for k in range(BLOCK_ROWS + 3):
-            before = s_ref[base + k, (tile + tiles - 1) % tiles].astype(F32)
-            after = s_ref[base + k, (tile + 1) % tiles].astype(F32)
+            before = s_ref[base + k, (tile + tiles - 1) % tiles]
+            after = s_ref[base + k, (tile + 1) % tiles]
             centre.append(s_ref[base + k, tile].astype(F32))
-            edge.append(jnp.where(left_half, after, before))
+            edge.append(jnp.where(left_half, after, before).astype(F32))
         taps = []
         for b in range(4):
             shift = first + b
@@ -466,36 +479,37 @@
                 value = dep[i] + jnp.tanh(push)
                 row = band * BLOCK_ROWS + i
                 if last:
-                    refs[1][pl.ds((row * 5 + tile) * fields, fields), :] = value
+                    refs[1][row, tile] = value
                 else:
                     refs[0][row, tile] = value.astype(BF16)
     if not last:
         send_rows(refs[0], rows - ABOVE, refs[1])
         send_rows(refs[0], 0, refs[2])
     if last:
-        for f in range(fields):
-            for t in range(5):
-                got = refs[1][pl.ds(t * fields + f, rows, stride=5 * fields), :]
-                refs[0][f, :, pl.ds(t * LANES, LANES)] = got.astype(BF16)
-
-
-def advance(last, params, edges, before, now, after, phys, bias):
+        for t in range(5):
+            for g in range(0, fields, 8):
+                got = jnp.swapaxes(refs[1][:, t, pl.ds(g, 8), :], 0, 1)
+                refs[0][pl.ds(g, 8), :, pl.ds(t * LANES, LANES)] = got.astype(BF16)
+
+
+def advance(last, params, before, now, after, phys, bias, *edges):
     rows, tiles, fields = now.shape[:3]
-    smem, vmem = pl.BlockSpec(memory_space=pltpu.SMEM), pl.BlockSpec(memory_space=pltpu.VMEM)
+    anywhere, vmem = pl.BlockSpec(memory_space=pl.ANY), pl.BlockSpec(memory_space=pltpu.VMEM)
     scratch = [pltpu.VMEM((ABOVE + rows + BELOW, tiles, fields, LANES), BF16)]
+    scratch += [pltpu.SMEM(params.shape, F32), pltpu.SMEM((2, LANES), F32), pltpu.SemaphoreType.DMA((2,))]
     if last:
         shape = jax.ShapeDtypeStruct((fields, rows, 5 * LANES), BF16)
-        scratch.insert(0, pltpu.VMEM((rows * 5 * fields, LANES), F32))
+        scratch.insert(0, pltpu.VMEM((rows, 5, fields, LANES), F32))
     else:
         shape = state_shapes(rows, tiles, fields)
     return pl.pallas_call(
         functools.partial(advance_kernel, last),
         out_shape=shape,
-        in_specs=[smem] * 2 + [vmem] * 5,
+        in_specs=[anywhere] + [vmem] * 5 + [anywhere] * len(edges),
         scratch_shapes=scratch,
         compiler_params=pltpu.CompilerParams(vmem_limit_bytes=16 << 20),
         name="advance_last" if last else "advance_first",
-    )(params, edges, before, now, after, phys, bias)
+    )(params, before, now, after, phys, bias, *edges)
 
 
 def row_halos(last, first):
@@ -511,10 +525,8 @@
     bands, owners = lax.axis_size("wave"), lax.axis_size("lev")
     nlon = shift_rows.shape[2] * BLOCK_COLS * owners
     scale = 1.0 / math.sqrt(waves)
-    band = lax.axis_index("wave").astype(jnp.int32).reshape(1)
-    owner = lax.axis_index("lev").astype(jnp.int32).reshape(1)
     outgoing = legendre(
-        spectral, wave_ids, band, lat_rows, 8 * lats, nlon // owners - 1, 2 * nlon, scale
+        spectral, wave_ids, lat_rows, 8 * lats, nlon // owners - 1, 2 * nlon, scale
     )
     outgoing = outgoing.reshape(bands, lats // bands, slots * parts * fields)
     arrived = lax.all_to_all(outgoing, "wave", split_axis=0, concat_axis=0, tiled=True)
@@ -525,11 +537,11 @@
     arrived, params, bias = lax.optimization_barrier((arrived, params, bias))
     columns = fourier(arrived, m, stamp, table, scale)
     columns = lax.all_to_all(columns, "lev", split_axis=0, concat_axis=0, tiled=True)
-    state, last, first, edges = regroup(columns, owner)
+    state, last, first, edges = regroup(columns)
     before, after = row_halos(last, first)
-    state, last, first = advance(False, params, edges, before, state, after, phys_weight, bias)
+    state, last, first = advance(False, params, before, state, after, phys_weight, bias, edges)
     before, after = row_halos(last, first)
-    return advance(True, params, edges, before, state, after, phys_weight, bias)
+    return advance(True, params, before, state, after, phys_weight, bias)
 
 
 def solution(mesh):

time: 85.7 us -> 84.3 us (0.984)
  blocking collectives: 0 us -> 20.8 us
  waiting for transfers between devices: 28.4 us -> 16.4 us
  starting transfers between devices: 37.2 us -> 28.1 us
  Pallas kernels: 15.5 us -> 14.3 us
    all_to_all x0 -> x1, blocking collectives: none -> 20.8 us  [shards(): lax.all_to_all(columns, 'lev', split_axis=0, concat_axis=0, tiled=True)]
    all_to_all x1 -> x0, waiting for transfers between devices: 12 us -> none  [shards(): lax.all_to_all(columns, 'lev', split_axis=0, concat_axis=0, tiled=True)]
    all_to_all x1 -> x0, starting transfers between devices: 9.09 us -> none  [shards(): lax.all_to_all(columns, 'lev', split_axis=0, concat_axis=0, tiled=True)]
  transfers between devices with their start and end apart: 6 -> 5, of which waited for: 4 -> 3; matrix products, arithmetic and copies ran while one was open for 1% -> 1% of each run, Pallas kernels for 3% -> 3%
where the time goes in v7:
time: 84.3 us; the launch traced here: 83.3 us
  starting transfers between devices  28.1 us (33%)
  blocking collectives  20.8 us (25%)
  waiting for transfers between devices  16.4 us (19%)
  Pallas kernels  14.3 us (17%)
  local copies, waits for them, and re-layouts  3.44 us (4%)
    all_to_all x1, blocking collectives, shards(): lax.all_to_all(columns, 'lev', split_axis=0, concat_axis=0, tiled=True)  20.8 us
    all_to_all x1, starting transfers between devices, shards(): lax.all_to_all(outgoing, 'wave', split_axis=0, concat_axis=0, tiled=True)  17.9 us
    ppermute x2, waiting for transfers between devices, row_halos(): after = lax.ppermute(first, 'wave', [(i + 1, i) for i in range(size - 1)])  10.3 us
    all_to_all x1, waiting for transfers between devices, shards(): lax.all_to_all(outgoing, 'wave', split_axis=0, concat_axis=0, tiled=True)  6.15 us
    ppermute x2, starting transfers between devices, row_halos(): before = lax.ppermute(last, 'wave', [(i, i + 1) for i in range(size - 1)])  5.9 us
    pallas_call x2, Pallas kernels, advance(): pl.pallas_call(functools.partial(advance_kernel, last), out_shape=shape,...  4.47 us
    ppermute x2, starting transfers between devices, row_halos(): after = lax.ppermute(first, 'wave', [(i + 1, i) for i in range(size - 1)])  4.34 us
    pallas_call x1, Pallas kernels, legendre(): pl.pallas_call(functools.partial(legendre_kernel, period, middle, turn, s...  3.6 us
  transfers between devices with their start and end apart: 5, of which 3 were waited for; matrix products, arithmetic and copies ran while one was open for 1% of the time, Pallas kernels for 3%

profile of v7, /device:TPU:1, one launch (start us, length us, event | category | flops | bytes accessed | tf_op | source)
XLA Modules:
  0.0 83.3 jit_solution(4390674969322991911)
XLA Ops:
  0.0 3.6 %legendre.1 = bf16[384,128]{1,0:T(8,128)(2,1)} custom-call(s32[1536]{0:T(1024)} %ids_hbm.1, s32[384]{0:T(512)} %lat_hbm.1, bf16[32,2,2,1536]{3,2,1,0:T(2,128)(2,1)} %x_hbm.1), custom_call_target="tpu_custom_call" | custom-call | tf_op jit(solution)/shard_map/legendre/pallas_call | solution.py:131
  3.6 0.0 copy-start
  3.6 0.0 copy-start.1
  3.6 17.9 %all-to-all-start = ((bf16[48,8,128]{2,1,0:T(8,128)(2,1)}), bf16[48,8,128]{2,1,0:T(8,128)(2,1)S(1)}, u32[]{:S(2)}, u32[]{:S(2)}) async-start(bf16[48,8,128]{2,1,0:T(8,128)(2,1)} %bitcast.4), calls=%async_computation | async-start | bytes 196608 | tf_op jit(solution)/shard_map/all_to_all | solution.py:532
  21.5 0.7 broadcast_in_dim.6.ids_ref
  22.2 0.7 copy-done.2
  22.9 0.7 copy-done.3
  23.6 0.7 copy-done.4
  24.3 0.7 copy-done.5
  25.0 2.5 %fourier_table.1 = (bf16[768,1536]{1,0:T(8,128)(2,1)S(1)}, f32[1,1536]{1,0:T(1,128)S(1)}, f32[8,128]{1,0:T(8,128)S(1)}, f32[200]{0:T(256)S(1)}) custom-call(s32[1,1536]{1,0:T(1,128)S(1)} %broadcast_in_dim.6.ids_ref, s32[2,2,5]{2,1,0:T(2,128)S(1)} %copy-done.2, s32[2,2,5]{2,1,0:T(2,128)S(1)} %copy-done.3, f32[2,2,5]{2,1,0:T(2,128)S(1)} %copy-done.4, ...), custom_call_target="tpu_custom_call" | custom-call | flops 20000000 | bytes 2500000 | tf_op jit(solution)/shard_map/fourier_table/pallas_call | solution.py:247
  27.4 6.1 %all-to-all-done.z_ref = bf16[48,8,128]{2,1,0:T(8,128)(2,1)S(1)} async-done(((bf16[48,8,128]{2,1,0:T(8,128)(2,1)}), bf16[48,8,128]{2,1,0:T(8,128)(2,1)S(1)}, u32[]{:S(2)}, u32[]{:S(2)}) %all-to-all-start) | async-done | bytes 98336 | tf_op jit(solution)/shard_map/all_to_all | solution.py:532
  33.6 3.4 %fourier.1 = bf16[16,88,128]{2,1,0:T(8,128)(2,1)S(1)} custom-call(bf16[48,8,128]{2,1,0:T(8,128)(2,1)S(1)} %all-to-all-done.z_ref, f32[1,1536]{1,0:T(1,128)S(1)} %get-tuple-element.22.m_ref, f32[8,128]{1,0:T(8,128)S(1)} %get-tuple-element.23.stamp_ref, bf16[768,1536]{1,0:T(8,128)(2,1)S(1)} %get-tuple-element.24.e_ref), custom_call_target="tpu_custom_call" | custom-call | tf_op jit(solution)/shard_map/fourier/pallas_call | solution.py:331
  37.0 20.8 %all_to_all.10.x_ref = bf16[16,88,128]{2,1,0:T(8,128)(2,1)S(1)} all-to-all(bf16[16,88,128]{2,1,0:T(8,128)(2,1)S(1)} %fourier.1), channel_id=1, replica_groups=mesh['wave'=48,'lev'=16] {'lev'}, dimensions={0} | all-to-all | bytes 720896 | tf_op jit(solution)/shard_map/all_to_all | solution.py:539
  57.9 0.4 regroup.1
  58.3 4.0 %collective-permute-start = (bf16[6,168,128]{2,1,0:T(8,128)(2,1)S(1)}, bf16[6,168,128]{2,1,0:T(8,128)(2,1)S(1)}, u32[]{:S(2)}, u32[]{:S(2)}) collective-permute-start(bf16[6,168,128]{2,1,0:T(8,128)(2,1)S(1)} %get-tuple-element.25), channel_id=1, source_target_pairs={{0,16},{16,32},{32,48},{48,64},{64,80},{80,96},{96,112},{112,128},... | collective-permute-start | bytes 774152 | tf_op jit(solution)/shard_map/ppermute | solution.py:517
  62.2 1.9 %collective-permute-start.1 = (bf16[5,168,128]{2,1,0:T(8,128)(2,1)S(1)}, bf16[5,168,128]{2,1,0:T(8,128)(2,1)S(1)}, u32[]{:S(2)}, u32[]{:S(2)}) collective-permute-start(bf16[5,168,128]{2,1,0:T(8,128)(2,1)S(1)} %get-tuple-element.27), channel_id=1, source_target_pairs={{16,0},{32,16},{48,32},{64,48},{80,64},{96,80},{112,96},{128,112},... | collective-permute-start | bytes 645128 | tf_op jit(solution)/shard_map/ppermute | solution.py:518
  64.2 5.3 %collective-permute-done.1.after_ref = bf16[5,168,128]{2,1,0:T(8,128)(2,1)S(1)} collective-permute-done((bf16[5,168,128]{2,1,0:T(8,128)(2,1)S(1)}, bf16[5,168,128]{2,1,0:T(8,128)(2,1)S(1)}, u32[]{:S(2)}, u32[]{:S(2)}) %collective-permute-start.1) | collective-permute-done | bytes 215072 | tf_op jit(solution)/shard_map/ppermute | solution.py:518
  69.4 0.0 collective-permute-done.before_ref
  69.4 2.1 %advance_first.1 = (bf16[8,6,32,128]{3,2,1,0:T(8,128)(2,1)S(1)}, bf16[6,168,128]{2,1,0:T(8,128)(2,1)S(1)}, bf16[5,168,128]{2,1,0:T(8,128)(2,1)S(1)}) custom-call(f32[200]{0:T(256)S(1)} %get-tuple-element.20.param_hbm, bf16[6,168,128]{2,1,0:T(8,128)(2,1)S(1)} %collective-permute-done.before_ref, bf16[8,6,32,128]{3,2,1,0:T(8,128)(2,1)S(1)} %get-tuple-element.26.now_ref, ...), custom_call_target="tpu_custom_call" | custom-call | tf_op jit(solution)/shard_map/advance_first/pallas_call | solution.py:505
  71.5 1.9 %collective-permute-start.2 = (bf16[6,168,128]{2,1,0:T(8,128)(2,1)S(1)}, bf16[6,168,128]{2,1,0:T(8,128)(2,1)S(1)}, u32[]{:S(2)}, u32[]{:S(2)}) collective-permute-start(bf16[6,168,128]{2,1,0:T(8,128)(2,1)S(1)} %get-tuple-element.30), channel_id=1, source_target_pairs={{0,16},{16,32},{32,48},{48,64},{64,80},{80,96},{96,112},{112,128},... | collective-permute-start | bytes 774152 | tf_op jit(solution)/shard_map/ppermute | solution.py:517
  73.5 2.4 %collective-permute-start.3 = (bf16[5,168,128]{2,1,0:T(8,128)(2,1)S(1)}, bf16[5,168,128]{2,1,0:T(8,128)(2,1)S(1)}, u32[]{:S(2)}, u32[]{:S(2)}) collective-permute-start(bf16[5,168,128]{2,1,0:T(8,128)(2,1)S(1)} %get-tuple-element.32), channel_id=1, source_target_pairs={{16,0},{32,16},{48,32},{64,48},{80,64},{96,80},{112,96},{128,112},... | collective-permute-start | bytes 645128 | tf_op jit(solution)/shard_map/ppermute | solution.py:518
  75.9 5.0 %collective-permute-done.3.after_ref = bf16[5,168,128]{2,1,0:T(8,128)(2,1)S(1)} collective-permute-done((bf16[5,168,128]{2,1,0:T(8,128)(2,1)S(1)}, bf16[5,168,128]{2,1,0:T(8,128)(2,1)S(1)}, u32[]{:S(2)}, u32[]{:S(2)}) %collective-permute-start.3) | collective-permute-done | bytes 215072 | tf_op jit(solution)/shard_map/ppermute | solution.py:518
  80.9 0.0 collective-permute-done.2.before_ref
  80.9 2.4 %advance_last.1 = bf16[32,8,640]{2,1,0:T(8,128)(2,1)} custom-call(f32[200]{0:T(256)S(1)} %get-tuple-element.20.param_hbm, bf16[6,168,128]{2,1,0:T(8,128)(2,1)S(1)} %collective-permute-done.2.before_ref, bf16[8,6,32,128]{3,2,1,0:T(8,128)(2,1)S(1)} %get-tuple-element.31.now_ref, bf16[5,168,128]{2,1,0:T(8,128)(2,1)S(1)} %collective-permute-done.3.after_ref, ...), custom_call_target="tpu_custom_call" | custom-call | tf_op jit(solution)/shard_map/advance_last/pallas_call | solution.py:505
  (6 shorter events, 0.0 us)
Async XLA Ops:
  3.6 65.8 %copy-start = (bf16[32,32]{1,0:T(8,128)(2,1)S(1)}, bf16[32,32]{1,0:T(8,128)(2,1)}, u32[]{:S(2)}) copy-start(bf16[32,32]{1,0:T(8,128)(2,1)} %phys_ref.3) | copy-start | bytes 6148
  3.6 65.8 %copy-start.1 = (f32[32]{0:T(128)S(1)}, f32[32]{0:T(128)}, u32[]{:S(2)}) copy-start(f32[32]{0:T(128)} %param.17) | copy-start | bytes 388
  3.6 30.0 %all-to-all-start = ((bf16[48,8,128]{2,1,0:T(8,128)(2,1)}), bf16[48,8,128]{2,1,0:T(8,128)(2,1)S(1)}, u32[]{:S(2)}, u32[]{:S(2)}) async-start(bf16[48,8,128]{2,1,0:T(8,128)(2,1)} %bitcast.4), calls=%async_computation | async-start | bytes 196608 | tf_op jit(solution)/shard_map/all_to_all | solution.py:532
  22.2 0.7 copy-start.2
  22.9 0.7 copy-start.3
  23.6 0.7 copy-start.4
  24.3 0.7 copy-start.5
  58.3 11.2 %collective-permute-start = (bf16[6,168,128]{2,1,0:T(8,128)(2,1)S(1)}, bf16[6,168,128]{2,1,0:T(8,128)(2,1)S(1)}, u32[]{:S(2)}, u32[]{:S(2)}) collective-permute-start(bf16[6,168,128]{2,1,0:T(8,128)(2,1)S(1)} %get-tuple-element.25), channel_id=1, source_target_pairs={{0,16},{16,32},{32,48},{48,64},{64,80},{80,96},{96,112},{112,128},... | collective-permute-start | bytes 774152 | tf_op jit(solution)/shard_map/ppermute | solution.py:517
  62.2 7.2 %collective-permute-start.1 = (bf16[5,168,128]{2,1,0:T(8,128)(2,1)S(1)}, bf16[5,168,128]{2,1,0:T(8,128)(2,1)S(1)}, u32[]{:S(2)}, u32[]{:S(2)}) collective-permute-start(bf16[5,168,128]{2,1,0:T(8,128)(2,1)S(1)} %get-tuple-element.27), channel_id=1, source_target_pairs={{16,0},{32,16},{48,32},{64,48},{80,64},{96,80},{112,96},{128,112},... | collective-permute-start | bytes 645128 | tf_op jit(solution)/shard_map/ppermute | solution.py:518
  71.5 9.4 %collective-permute-start.2 = (bf16[6,168,128]{2,1,0:T(8,128)(2,1)S(1)}, bf16[6,168,128]{2,1,0:T(8,128)(2,1)S(1)}, u32[]{:S(2)}, u32[]{:S(2)}) collective-permute-start(bf16[6,168,128]{2,1,0:T(8,128)(2,1)S(1)} %get-tuple-element.30), channel_id=1, source_target_pairs={{0,16},{16,32},{32,48},{48,64},{64,80},{80,96},{96,112},{112,128},... | collective-permute-start | bytes 774152 | tf_op jit(solution)/shard_map/ppermute | solution.py:517
  73.5 7.5 %collective-permute-start.3 = (bf16[5,168,128]{2,1,0:T(8,128)(2,1)S(1)}, bf16[5,168,128]{2,1,0:T(8,128)(2,1)S(1)}, u32[]{:S(2)}, u32[]{:S(2)}) collective-permute-start(bf16[5,168,128]{2,1,0:T(8,128)(2,1)S(1)} %get-tuple-element.32), channel_id=1, source_target_pairs={{16,0},{32,16},{48,32},{64,48},{80,64},{96,80},{112,96},{128,112},... | collective-permute-start | bytes 645128 | tf_op jit(solution)/shard_map/ppermute | solution.py:518
